TPU v7x, 256 devices: a whole 4x4x8 slice. The times are simulated.
256 devices in a mesh: macro: 4 (over x), micro: 64 (over y, z, core).
Axes of the slice: x: 4, y: 4, z: 8, core: 2. Of those that a mesh axis runs over, the one named last changes fastest.
Arguments:
- displacement: float32 [3, 8, 128, 256], P(None, 'macro', 'micro'), may hold values from -6 to 6
- load: float32 [3, 8, 128, 256], P(None, 'macro', 'micro'), may hold values from -6 to 6
- routes: int32 [4, 64, 1024, 1], P('macro', 'micro'), may hold values from 0 to 63; in each aligned block of 1024 rows (0 to 1023, 1024 to 2047, ..., all dimensions but the last counted through in order) at most 32 rows name the same one
- counts: int32 [4, 64, 1024], P('macro', 'micro'), may hold values from 1 to 4
- stiffness: bfloat16 [64, 512, 512], P('micro'), may hold values from -0.5 to 2.5, as said below
- precond: bfloat16 [64, 512, 512], P('micro'), may hold values from -0.5 to 2.5, as said below
- forcing: bfloat16 [64, 6, 512], P('micro'), may hold values from -2.5 to 2.5
- coupling: bfloat16 [64, 512, 6], P('micro'), may hold values from -0.25 to 0.25
- lame_first: float32 [64], P('micro'), may hold values from 0.5 to 2
- lame_shear: float32 [64], P('micro'), may hold values from 0.5 to 2
Outputs:
- increment: float32 [3, 8, 128, 256], P(None, 'macro', 'micro')
- residual: float32 [3, 8, 128, 256], P(None, 'macro', 'micro')
Inputs may be any that keep to these rules, and one draw needn't show every extreme that they name: `routes`: among the points of one block (one device's points), no owner is named by more than 32 points, a bound that some block reaches. `stiffness`: Symmetric. `precond`: Symmetric.
All inputs are finite; a program needn't handle non-finite values.
Results may differ from a plain program's by a relative error of at most 0.002.
Values sent between devices are 32-bit elements; how exact they have to be, the bound alone decides.
No kernel may reach another device: no remote copies, remote signals or barrier semaphores. Data moves between devices by JAX's collectives and lax.ppermute only.
A program may use at most 64 MiB of HBM per device.

v0:
```python
import functools

import jax
import jax.numpy as jnp
import numpy as np
from jax import lax
from jax.sharding import Mesh
from jax.sharding import PartitionSpec as P

ITMAX = 4
ITERS = 5
MACRO_MICRO = ("macro", "micro_0", "micro_1", "micro_2")
MICRO = ("micro_0", "micro_1", "micro_2")


BETA = 0.1
OMEGA = 0.8
MASS = 0.1
VOIGT = ((0, 5, 4), (5, 1, 3), (4, 3, 2))
UPPER_PAIRS = tuple(
    ((first_axis, second_axis) for first_axis in range(6) for second_axis in range(first_axis, 6))
)
UNPACK = np.array(
    [
        UPPER_PAIRS.index((min(first_axis, second_axis), max(first_axis, second_axis)))
        for first_axis in range(6)
        for second_axis in range(6)
    ],
    dtype=np.int32,
)


def with_halo(block, sides, width):
    for axis, dim in sides:
        count = lax.axis_size(axis)
        forward = [(i, i + 1) for i in range(count - 1)]
        backward = [(target, source) for source, target in forward]
        low = lax.ppermute(
            lax.slice_in_dim(block, block.shape[dim] - width, None, axis=dim), axis, forward
        )
        high = lax.ppermute(lax.slice_in_dim(block, 0, width, axis=dim), axis, backward)
        block = jnp.concatenate([low, block, high], axis=dim)
    return block


def by_axis(shard, axes):
    return functools.reduce(lax.psum, axes, shard)


def passed_along(value, axis, steps):
    count = lax.axis_size(axis)
    initial, last = (max(0, -steps), min(count, count - steps))
    return lax.ppermute(value, axis, [(source, source + steps) for source in range(initial, last)])


def element_strain(nodes):
    count_x = nodes.shape[1] - 1
    count_y = nodes.shape[2] - 1
    count_z = nodes.shape[3]
    padded = jnp.pad(nodes, ((0, 0), (0, 0), (0, 0), (0, 1)))
    zeros = jnp.zeros((3, count_x, count_y, count_z), jnp.float32)
    grad_x, grad_y, grad_z = (zeros, zeros, zeros)
    for corner_x in (0, 1):
        for corner_y in (0, 1):
            for corner_z in (0, 1):
                piece = padded[
                    :,
                    corner_x : corner_x + count_x,
                    corner_y : corner_y + count_y,
                    corner_z : corner_z + count_z,
                ]
                grad_x = grad_x + 0.25 * (2 * corner_x - 1) * piece
                grad_y = grad_y + 0.25 * (2 * corner_y - 1) * piece
                grad_z = grad_z + 0.25 * (2 * corner_z - 1) * piece
    return jnp.stack(
        [
            grad_x[0],
            grad_y[1],
            grad_z[2],
            grad_z[1] + grad_y[2],
            grad_z[0] + grad_x[2],
            grad_y[0] + grad_x[1],
        ]
    )


def node_force(stress):
    count_x, count_y, count_z = (stress.shape[1], stress.shape[2], stress.shape[3])
    forces = jnp.zeros((3, count_x + 1, count_y + 1, count_z + 1), jnp.float32)
    for corner_x in (0, 1):
        for corner_y in (0, 1):
            for corner_z in (0, 1):
                signs = (2 * corner_x - 1, 2 * corner_y - 1, 2 * corner_z - 1)
                parts = []
                for component in range(3):
                    table = VOIGT[component]
                    parts.append(
                        0.25
                        * (
                            signs[0] * stress[table[0]]
                            + signs[1] * stress[table[1]]
                            + signs[2] * stress[table[2]]
                        )
                    )
                contrib = jnp.stack(parts)
                forces = forces + jnp.pad(
                    contrib,
                    (
                        (0, 0),
                        (corner_x, 1 - corner_x),
                        (corner_y, 1 - corner_y),
                        (corner_z, 1 - corner_z),
                    ),
                )
    return forces


def micro_solve(
    strain, sweeps, stiffness, precond, forcing, coupling, lame_first, lame_shear, pairs
):
    strain_half = strain.astype(jnp.bfloat16)
    modal_load = lax.dot_general(
        strain_half, forcing, (((0,), (0,)), ((), ())), preferred_element_type=jnp.float32
    )
    modes = jnp.zeros_like(modal_load)
    for sweep in range(ITMAX):
        misfit = (
            jnp.dot(modes.astype(jnp.bfloat16), stiffness, preferred_element_type=jnp.float32)
            + BETA * jnp.tanh(modes)
            - modal_load
        )
        update = modes - OMEGA * jnp.dot(
            misfit.astype(jnp.bfloat16), precond, preferred_element_type=jnp.float32
        )
        modes = jnp.where((sweeps[0] > sweep)[:, None], update, modes)
    trace = strain[0] + strain[1] + strain[2]
    elastic = jnp.stack(
        [
            lame_first * trace + 2.0 * lame_shear * strain[0],
            lame_first * trace + 2.0 * lame_shear * strain[1],
            lame_first * trace + 2.0 * lame_shear * strain[2],
            lame_shear * strain[3],
            lame_shear * strain[4],
            lame_shear * strain[5],
        ]
    )
    stress = elastic + lax.dot_general(
        coupling,
        modes.astype(jnp.bfloat16),
        (((0,), (1,)), ((), ())),
        preferred_element_type=jnp.float32,
    )
    slope = 1.0 - jnp.tanh(modes) ** 2
    wide = coupling.astype(jnp.float32)
    products = jnp.stack([wide[:, pair[0]] * wide[:, pair[1]] for pair in pairs], axis=1)
    extra = lax.dot_general(
        products,
        slope,
        (((0,), (1,)), ((), ())),
        precision=lax.Precision.HIGHEST,
        preferred_element_type=jnp.float32,
    )
    base = jnp.stack(
        [
            lame_first * float(pair[0] < 3 and pair[1] < 3)
            + lame_shear
            * (
                2.0 * float(pair[0] == pair[1] and pair[0] < 3)
                + float(pair[0] == pair[1] and pair[0] >= 3)
            )
            for pair in pairs
        ]
    )
    return jnp.concatenate([stress, extra + base[:, None]], axis=0)


def extend(field):
    return with_halo(field, (("macro", 1), (MICRO, 2)), 1)


def operate(field, tangent_ext):
    strain = element_strain(extend(field))
    stress = jnp.sum(tangent_ext * strain[None], axis=1)
    return MASS * field + node_force(stress)[:, 1:-1, 1:-1, :-1]


def two_products(residual, image):
    return (
        by_axis(jnp.sum(residual * residual), MACRO_MICRO),
        by_axis(jnp.sum(residual * image), MACRO_MICRO),
    )


def shards(
    displacement,
    load,
    routes,
    counts,
    stiffness,
    precond,
    forcing,
    coupling,
    lame_first,
    lame_shear,
):
    count_x, count_y, count_z = (
        displacement.shape[1],
        displacement.shape[2],
        displacement.shape[3],
    )
    points = count_x * count_y * count_z
    owners = lax.axis_size(MICRO)
    capacity = max(2, 2 * points // owners)
    strain_ext = element_strain(extend(displacement))
    strain_points = strain_ext[:, 1:, 1:].reshape(6, points)
    owner_of = routes.reshape(points)
    sweeps_of = counts.reshape(points)
    onehot = (owner_of[:, None] == jnp.arange(owners, dtype=jnp.int32)[None, :]).astype(jnp.int32)
    ranks = jnp.sum((jnp.cumsum(onehot, axis=0) - 1) * onehot, axis=1)
    target = owner_of * capacity + ranks
    send_strain = jnp.zeros((6, owners * capacity), jnp.float32).at[:, target].set(strain_points)
    send_sweeps = jnp.zeros((1, owners * capacity), jnp.int32).at[0, target].set(sweeps_of)
    got_strain, got_sweeps = (
        lax.all_to_all(send_strain, MICRO, split_axis=1, concat_axis=1, tiled=True),
        lax.all_to_all(send_sweeps, MICRO, split_axis=1, concat_axis=1, tiled=True),
    )
    rows = micro_solve(
        got_strain,
        got_sweeps,
        stiffness[0],
        precond[0],
        forcing[0],
        coupling[0],
        lame_first[0],
        lame_shear[0],
        UPPER_PAIRS,
    )
    back = lax.all_to_all(rows, MICRO, split_axis=1, concat_axis=1, tiled=True)
    picked = jnp.take(back, target, axis=1)
    values = jnp.concatenate([picked[:6], picked[6:][UNPACK]], axis=0)
    values = values.reshape(42, count_x, count_y, count_z)
    left_x = passed_along(values[:, -1:], "macro", 1)
    values = jnp.concatenate([left_x, values], axis=1)
    left_y = passed_along(values[:, :, -1:], MICRO, 1)
    values = jnp.concatenate([left_y, values], axis=2)
    stress_ext = values[:6]
    tangent_ext = values[6:].reshape(6, 6, count_x + 1, count_y + 1, count_z)
    rhs = load - node_force(stress_ext)[:, 1:-1, 1:-1, :-1]

    def apply(field):
        return operate(field, tangent_ext)

    increment = jnp.zeros_like(rhs)
    residual = rhs
    image = apply(residual)
    norm_now, product = two_products(residual, image)
    alpha = norm_now / product
    direction, along = (residual, image)
    for step in range(ITERS):
        increment = increment + alpha * direction
        residual = residual - alpha * along
        if step + 1 < ITERS:
            image = apply(residual)
            norm_next, product = two_products(residual, image)
            ratio = norm_next / norm_now
            alpha = norm_next / (product - ratio * norm_next / alpha)
            direction = residual + ratio * direction
            along = image + ratio * along
            norm_now = norm_next
    return (increment, residual)


def solution(mesh):
    split = Mesh(
        mesh.devices.reshape(mesh.shape["macro"], 4, 8, 2),
        ("macro", "micro_0", "micro_1", "micro_2"),
    )
    placed = (
        P(None, "macro", MICRO, None),
        P(None, "macro", MICRO, None),
        P("macro", MICRO, None, None),
        P("macro", MICRO, None),
        P(MICRO, None, None),
        P(MICRO, None, None),
        P(MICRO, None, None),
        P(MICRO, None, None),
        P(MICRO),
        P(MICRO),
    )
    return jax.shard_map(
        shards,
        mesh=split,
        in_specs=placed,
        out_specs=(P(None, "macro", MICRO, None), P(None, "macro", MICRO, None)),
        check_vma=False,
    )
```

profile of v0, /device:TPU:1, one launch (start us, length us, event | category | flops | bytes accessed | tf_op | source)
XLA Modules:
  0.0 474.1 jit_solution(1995910594395095443)
XLA Ops:
  7.4 18.0 %reduce-window.6 = s32[64,8,128]{2,1,0:T(8,128)S(1)} reduce-window(s32[64,8,128]{2,1,0:T(8,128)S(1)} %fusion.38, s32[]{:T(128)} %constant.22.clone.1), window={size=1x1x128 pad=0_0x0_0x127_0}, to_apply=%region_0.1 | reduce-window | flops 8323072 | bytes 524292 | tf_op jit(solution)/shard_map/reduce-window
  34.0 12.6 %all-to-all-start.1 = ((s32[1,64,32]{2,0,1:T(1,128)}), s32[1,64,32]{2,0,1:T(1,128)S(1)}, u32[]{:S(2)}, u32[]{:S(2)}) async-start(s32[1,64,32]{2,0,1:T(1,128)} %bitcast.13), calls=%async_computation.1 | async-start | bytes 65536 | tf_op jit(solution)/shard_map/all_to_all | solution.py:225
  62.2 10.2 %all-to-all-start = ((f32[64,1,192]{2,1,0:T(1,128)}), f32[64,1,192]{2,1,0:T(1,128)S(1)}, u32[]{:S(2)}, u32[]{:S(2)}) async-start(f32[64,1,192]{2,1,0:T(1,128)} %reshape.332), calls=%async_computation | async-start | bytes 131072 | tf_op jit(solution)/shard_map/all_to_all | solution.py:224
  73.2 9.0 %all-to-all-done = f32[64,1,192]{2,1,0:T(1,128)S(1)} async-done(((f32[64,1,192]{2,1,0:T(1,128)}), f32[64,1,192]{2,1,0:T(1,128)S(1)}, u32[]{:S(2)}, u32[]{:S(2)}) %all-to-all-start) | async-done | bytes 49184 | tf_op jit(solution)/shard_map/all_to_all | solution.py:224
  87.9 6.6 %subtract_select_fusion.3 = f32[2048,512]{1,0:T(8,128)} fusion(pred[2048]{0:T(1024)(128)(4,1)S(1)} %gt.63, f32[2048,512]{1,0:T(8,128)} %fusion.209, bf16[1,512,512]{2,1,0:T(8,128)(2,1)S(1)} %copy-done, bf16[1,512,512]{2,1,0:T(8,128)(2,1)S(1)} %copy-done.7), kind=kOutput, calls=%fused_computation.14 | convolution fusion | flops 2152726528 | bytes 9439232 | tf_op jit(solution)/shard_map/dot_general | solution.py:132
  94.5 9.7 %subtract_select_fusion.2 = f32[2048,512]{1,0:T(8,128)} fusion(f32[2048,512]{1,0:T(8,128)} %subtract_select_fusion.3, pred[2048]{0:T(1024)(128)(4,1)S(1)} %gt.60, f32[2048,512]{1,0:T(8,128)} %fusion.209, bf16[1,512,512]{2,1,0:T(8,128)(2,1)S(1)} %copy-done, bf16[1,512,512]{2,1,0:T(8,128)(2,1)S(1)} %copy-done.7), kind=kOutput, calls=%fused_computation.6 | convolution fusion | flops 2155872256 | bytes 13633536 | tf_op jit(solution)/shard_map/dot_general | solution.py:132
  104.2 10.1 %subtract_select_fusion.1 = f32[2048,512]{1,0:T(8,128)} fusion(f32[2048,512]{1,0:T(8,128)} %subtract_select_fusion.2, pred[2048]{0:T(1024)(128)(4,1)S(1)} %gt.57, f32[2048,512]{1,0:T(8,128)} %fusion.209, bf16[1,512,512]{2,1,0:T(8,128)(2,1)S(1)} %copy-done, bf16[1,512,512]{2,1,0:T(8,128)(2,1)S(1)} %copy-done.7), kind=kOutput, calls=%fused_computation.5 | convolution fusion | flops 2155872256 | bytes 13633536 | tf_op jit(solution)/shard_map/dot_general | solution.py:132
  114.4 9.7 %subtract_select_fusion = f32[2048,512]{1,0:T(8,128)} fusion(f32[2048,512]{1,0:T(8,128)} %subtract_select_fusion.1, pred[2048]{0:T(1024)(128)(4,1)S(1)} %gt.54, f32[2048,512]{1,0:T(8,128)} %fusion.209, bf16[1,512,512]{2,1,0:T(8,128)(2,1)S(1)} %copy-done, bf16[1,512,512]{2,1,0:T(8,128)(2,1)S(1)} %copy-done.7), kind=kOutput, calls=%fused_computation.4 | convolution fusion | flops 2155872256 | bytes 13633536 | tf_op jit(solution)/shard_map/dot_general | solution.py:132
  137.9 11.2 %all-to-all-done.2 = f32[64,1,864]{2,1,0:T(1,128)S(1)} async-done(((f32[64,1,864]{2,1,0:T(1,128)}), f32[64,1,864]{2,1,0:T(1,128)S(1)}, u32[]{:S(2)}, u32[]{:S(2)}) %all-to-all-start.2) | async-done | bytes 221216 | tf_op jit(solution)/shard_map/all_to_all | solution.py:238
  177.7 5.8 %collective-permute-start.8 = (f32[3,4,1,256]{3,2,1,0:T(1,128)S(1)}, f32[3,4,1,256]{3,2,1,0:T(1,128)S(1)}, u32[]{:S(2)}, u32[]{:S(2)}) collective-permute-start(f32[3,4,1,256]{3,2,1,0:T(1,128)S(1)} %get-tuple-element.252), channel_id=1, source_target_pairs={{0,1},{1,2},{2,3},{3,4},{4,5},{5,6},{6,7},{7,8},{8,9},{9,10},{10,1... | collective-permute-start | bytes 36872 | tf_op jit(solution)/shard_map/ppermute | solution.py:38
  190.6 7.8 %all-reduce.69 = (f32[]{:T(128)}, f32[]{:T(128)}) all-reduce(f32[]{:T(128)} %get-tuple-element.21, f32[]{:T(128)} %get-tuple-element.20), channel_id=1, replica_groups=mesh['macro'=4,'micro_0'=4,'micro_1'=8,'micro_2'=2] {'macro'}, use_global_device_ids=true, to_apply=%region_6.7 | all-reduce | flops 2 | bytes 16 | tf_op jit(solution)/shard_map/psum | solution.py:47
  198.4 8.1 %all-reduce.64 = (f32[]{:T(128)}, f32[]{:T(128)}) all-reduce(f32[]{:T(128)} %get-tuple-element.50, f32[]{:T(128)} %get-tuple-element.51), channel_id=1, replica_groups=mesh['macro'=4,'micro_0'=4,'micro_1'=8,'micro_2'=2] {'micro_0'}, use_global_device_ids=true, to_apply=%region_7.8 | all-reduce | flops 2 | bytes 16 | tf_op jit(solution)/shard_map/psum | solution.py:47
  206.5 17.3 %all-reduce.59 = (f32[]{:T(128)}, f32[]{:T(128)}) all-reduce(f32[]{:T(128)} %get-tuple-element.40, f32[]{:T(128)} %get-tuple-element.41), channel_id=1, replica_groups=mesh['macro'=4,'micro_0'=4,'micro_1'=8,'micro_2'=2] {'micro_1'}, use_global_device_ids=true, to_apply=%region_8.9 | all-reduce | flops 2 | bytes 16 | tf_op jit(solution)/shard_map/psum | solution.py:47
  223.8 8.2 %all-reduce.74 = (f32[]{:T(128)}, f32[]{:T(128)}) all-reduce(f32[]{:T(128)} %get-tuple-element.30, f32[]{:T(128)} %get-tuple-element.31), channel_id=1, replica_groups=mesh['macro'=4,'micro_0'=4,'micro_1'=8,'micro_2'=2] {'micro_2'}, use_global_device_ids=true, to_apply=%region_9.10 | all-reduce | flops 2 | bytes 16 | tf_op jit(solution)/shard_map/psum | solution.py:47
  239.9 5.3 %collective-permute-start.12 = (f32[3,4,1,256]{3,2,1,0:T(1,128)S(1)}, f32[3,4,1,256]{3,2,1,0:T(1,128)S(1)}, u32[]{:S(2)}, u32[]{:S(2)}) collective-permute-start(f32[3,4,1,256]{3,2,1,0:T(1,128)S(1)} %get-tuple-element.248), channel_id=1, source_target_pairs={{0,1},{1,2},{2,3},{3,4},{4,5},{5,6},{6,7},{7,8},{8,9},{9,10},{10,1... | collective-permute-start | bytes 36872 | tf_op jit(solution)/shard_map/ppermute | solution.py:38
  252.5 6.7 %all-reduce.68 = (f32[]{:T(128)}, f32[]{:T(128)}) all-reduce(f32[]{:T(128)} %get-tuple-element.19, f32[]{:T(128)} %get-tuple-element.18), channel_id=1, replica_groups=mesh['macro'=4,'micro_0'=4,'micro_1'=8,'micro_2'=2] {'macro'}, use_global_device_ids=true, to_apply=%region_17.18 | all-reduce | flops 2 | bytes 16 | tf_op jit(solution)/shard_map/psum | solution.py:47
  259.2 6.7 %all-reduce.63 = (f32[]{:T(128)}, f32[]{:T(128)}) all-reduce(f32[]{:T(128)} %get-tuple-element.48, f32[]{:T(128)} %get-tuple-element.49), channel_id=1, replica_groups=mesh['macro'=4,'micro_0'=4,'micro_1'=8,'micro_2'=2] {'micro_0'}, use_global_device_ids=true, to_apply=%region_18.19 | all-reduce | flops 2 | bytes 16 | tf_op jit(solution)/shard_map/psum | solution.py:47
  265.8 14.4 %all-reduce.58 = (f32[]{:T(128)}, f32[]{:T(128)}) all-reduce(f32[]{:T(128)} %get-tuple-element.38, f32[]{:T(128)} %get-tuple-element.39), channel_id=1, replica_groups=mesh['macro'=4,'micro_0'=4,'micro_1'=8,'micro_2'=2] {'micro_1'}, use_global_device_ids=true, to_apply=%region_19.20 | all-reduce | flops 2 | bytes 16 | tf_op jit(solution)/shard_map/psum | solution.py:47
  280.2 7.4 %all-reduce.73 = (f32[]{:T(128)}, f32[]{:T(128)}) all-reduce(f32[]{:T(128)} %get-tuple-element.28, f32[]{:T(128)} %get-tuple-element.29), channel_id=1, replica_groups=mesh['macro'=4,'micro_0'=4,'micro_1'=8,'micro_2'=2] {'micro_2'}, use_global_device_ids=true, to_apply=%region_20.21 | all-reduce | flops 2 | bytes 16 | tf_op jit(solution)/shard_map/psum | solution.py:47
  312.4 6.6 %all-reduce.67 = (f32[]{:T(128)}, f32[]{:T(128)}) all-reduce(f32[]{:T(128)} %get-tuple-element.17, f32[]{:T(128)} %get-tuple-element.16), channel_id=1, replica_groups=mesh['macro'=4,'micro_0'=4,'micro_1'=8,'micro_2'=2] {'macro'}, use_global_device_ids=true, to_apply=%region_28.29 | all-reduce | flops 2 | bytes 16 | tf_op jit(solution)/shard_map/psum | solution.py:47
  319.0 6.8 %all-reduce.62 = (f32[]{:T(128)}, f32[]{:T(128)}) all-reduce(f32[]{:T(128)} %get-tuple-element.46, f32[]{:T(128)} %get-tuple-element.47), channel_id=1, replica_groups=mesh['macro'=4,'micro_0'=4,'micro_1'=8,'micro_2'=2] {'micro_0'}, use_global_device_ids=true, to_apply=%region_29.30 | all-reduce | flops 2 | bytes 16 | tf_op jit(solution)/shard_map/psum | solution.py:47
  325.8 15.8 %all-reduce.57 = (f32[]{:T(128)}, f32[]{:T(128)}) all-reduce(f32[]{:T(128)} %get-tuple-element.36, f32[]{:T(128)} %get-tuple-element.37), channel_id=1, replica_groups=mesh['macro'=4,'micro_0'=4,'micro_1'=8,'micro_2'=2] {'micro_1'}, use_global_device_ids=true, to_apply=%region_30.31 | all-reduce | flops 2 | bytes 16 | tf_op jit(solution)/shard_map/psum | solution.py:47
  341.6 7.7 %all-reduce.72 = (f32[]{:T(128)}, f32[]{:T(128)}) all-reduce(f32[]{:T(128)} %get-tuple-element.26, f32[]{:T(128)} %get-tuple-element.27), channel_id=1, replica_groups=mesh['macro'=4,'micro_0'=4,'micro_1'=8,'micro_2'=2] {'micro_2'}, use_global_device_ids=true, to_apply=%region_31.32 | all-reduce | flops 2 | bytes 16 | tf_op jit(solution)/shard_map/psum | solution.py:47
  361.3 5.3 %collective-permute-start.20 = (f32[3,4,1,256]{3,2,1,0:T(1,128)S(1)}, f32[3,4,1,256]{3,2,1,0:T(1,128)S(1)}, u32[]{:S(2)}, u32[]{:S(2)}) collective-permute-start(f32[3,4,1,256]{3,2,1,0:T(1,128)S(1)} %get-tuple-element.240), channel_id=1, source_target_pairs={{0,1},{1,2},{2,3},{3,4},{4,5},{5,6},{6,7},{7,8},{8,9},{9,10},{10,1... | collective-permute-start | bytes 36872 | tf_op jit(solution)/shard_map/ppermute | solution.py:38
  373.8 6.7 %all-reduce.66 = (f32[]{:T(128)}, f32[]{:T(128)}) all-reduce(f32[]{:T(128)} %get-tuple-element.15, f32[]{:T(128)} %get-tuple-element.14), channel_id=1, replica_groups=mesh['macro'=4,'micro_0'=4,'micro_1'=8,'micro_2'=2] {'macro'}, use_global_device_ids=true, to_apply=%region_39.40 | all-reduce | flops 2 | bytes 16 | tf_op jit(solution)/shard_map/psum | solution.py:47
  380.5 6.8 %all-reduce.61 = (f32[]{:T(128)}, f32[]{:T(128)}) all-reduce(f32[]{:T(128)} %get-tuple-element.44, f32[]{:T(128)} %get-tuple-element.45), channel_id=1, replica_groups=mesh['macro'=4,'micro_0'=4,'micro_1'=8,'micro_2'=2] {'micro_0'}, use_global_device_ids=true, to_apply=%region_40.41 | all-reduce | flops 2 | bytes 16 | tf_op jit(solution)/shard_map/psum | solution.py:47
  387.3 14.4 %all-reduce.56 = (f32[]{:T(128)}, f32[]{:T(128)}) all-reduce(f32[]{:T(128)} %get-tuple-element.34, f32[]{:T(128)} %get-tuple-element.35), channel_id=1, replica_groups=mesh['macro'=4,'micro_0'=4,'micro_1'=8,'micro_2'=2] {'micro_1'}, use_global_device_ids=true, to_apply=%region_41.42 | all-reduce | flops 2 | bytes 16 | tf_op jit(solution)/shard_map/psum | solution.py:47
  401.7 7.2 %all-reduce.71 = (f32[]{:T(128)}, f32[]{:T(128)}) all-reduce(f32[]{:T(128)} %get-tuple-element.24, f32[]{:T(128)} %get-tuple-element.25), channel_id=1, replica_groups=mesh['macro'=4,'micro_0'=4,'micro_1'=8,'micro_2'=2] {'micro_2'}, use_global_device_ids=true, to_apply=%region_42.43 | all-reduce | flops 2 | bytes 16 | tf_op jit(solution)/shard_map/psum | solution.py:47
  433.2 6.6 %all-reduce.65 = (f32[]{:T(128)}, f32[]{:T(128)}) all-reduce(f32[]{:T(128)} %get-tuple-element.13, f32[]{:T(128)} %get-tuple-element.12), channel_id=1, replica_groups=mesh['macro'=4,'micro_0'=4,'micro_1'=8,'micro_2'=2] {'macro'}, use_global_device_ids=true, to_apply=%region_50.51 | all-reduce | flops 2 | bytes 16 | tf_op jit(solution)/shard_map/psum | solution.py:47
  439.8 6.6 %all-reduce.60 = (f32[]{:T(128)}, f32[]{:T(128)}) all-reduce(f32[]{:T(128)} %get-tuple-element.42, f32[]{:T(128)} %get-tuple-element.43), channel_id=1, replica_groups=mesh['macro'=4,'micro_0'=4,'micro_1'=8,'micro_2'=2] {'micro_0'}, use_global_device_ids=true, to_apply=%region_51.52 | all-reduce | flops 2 | bytes 16 | tf_op jit(solution)/shard_map/psum | solution.py:47
  446.4 15.5 %all-reduce.55 = (f32[]{:T(128)}, f32[]{:T(128)}) all-reduce(f32[]{:T(128)} %get-tuple-element.32, f32[]{:T(128)} %get-tuple-element.33), channel_id=1, replica_groups=mesh['macro'=4,'micro_0'=4,'micro_1'=8,'micro_2'=2] {'micro_1'}, use_global_device_ids=true, to_apply=%region_52.53 | all-reduce | flops 2 | bytes 16 | tf_op jit(solution)/shard_map/psum | solution.py:47
  461.9 7.7 %all-reduce.70 = (f32[]{:T(128)}, f32[]{:T(128)}) all-reduce(f32[]{:T(128)} %get-tuple-element.22, f32[]{:T(128)} %get-tuple-element.23), channel_id=1, replica_groups=mesh['macro'=4,'micro_0'=4,'micro_1'=8,'micro_2'=2] {'micro_2'}, use_global_device_ids=true, to_apply=%region_53.54 | all-reduce | flops 2 | bytes 16 | tf_op jit(solution)/shard_map/psum | solution.py:47
  (332 shorter events, 154.6 us)
Async XLA Ops:
  0.6 87.3 %copy-start = (bf16[1,512,512]{2,1,0:T(8,128)(2,1)S(1)}, bf16[1,512,512]{2,1,0:T(8,128)(2,1)}, u32[]{:S(2)}) copy-start(bf16[1,512,512]{2,1,0:T(8,128)(2,1)} %param.17) | copy-start | bytes 1572868
  1.4 46.0 %collective-permute-start = (f32[3,1,2,256]{3,2,1,0:T(2,128)S(1)}, f32[3,1,2,256]{3,2,1,0:T(2,128)S(1)}, u32[]{:S(2)}, u32[]{:S(2)}) collective-permute-start(f32[3,1,2,256]{3,2,1,0:T(2,128)S(1)} %get-tuple-element.294), channel_id=1, source_target_pairs={{0,64},{64,128},{128,192},{1,65},{65,129},{129,193},{2,66},{66,130... | collective-permute-start | bytes 18440 | tf_op jit(solution)/shard_map/ppermute | solution.py:38
  5.4 42.8 %collective-permute-start.1 = (f32[3,1,2,256]{3,2,1,0:T(2,128)S(1)}, f32[3,1,2,256]{3,2,1,0:T(2,128)S(1)}, u32[]{:S(2)}, u32[]{:S(2)}) collective-permute-start(f32[3,1,2,256]{3,2,1,0:T(2,128)S(1)} %get-tuple-element.293), channel_id=1, source_target_pairs={{64,0},{128,64},{192,128},{65,1},{129,65},{193,129},{66,2},{130,66... | collective-permute-start | bytes 18440 | tf_op jit(solution)/shard_map/ppermute | solution.py:41
  25.4 59.8 %copy-start.5 = (bf16[1,6,512]{2,1,0:T(8,128)(2,1)S(1)}, bf16[1,6,512]{2,1,0:T(8,128)(2,1)}, u32[]{:S(2)}) copy-start(bf16[1,6,512]{2,1,0:T(8,128)(2,1)} %param.18) | copy-start | bytes 18436
  34.0 28.2 %all-to-all-start.1 = ((s32[1,64,32]{2,0,1:T(1,128)}), s32[1,64,32]{2,0,1:T(1,128)S(1)}, u32[]{:S(2)}, u32[]{:S(2)}) async-start(s32[1,64,32]{2,0,1:T(1,128)} %bitcast.13), calls=%async_computation.1 | async-start | bytes 65536 | tf_op jit(solution)/shard_map/all_to_all | solution.py:225
  48.2 7.0 %collective-permute-start.2 = (f32[3,4,1,256]{3,2,1,0:T(1,128)S(1)}, f32[3,4,1,256]{3,2,1,0:T(1,128)S(1)}, u32[]{:S(2)}, u32[]{:S(2)}) collective-permute-start(f32[3,4,1,256]{3,2,1,0:T(1,128)S(1)} %get-tuple-element.253), channel_id=1, source_target_pairs={{0,1},{1,2},{2,3},{3,4},{4,5},{5,6},{6,7},{7,8},{8,9},{9,10},{10,1... | collective-permute-start | bytes 36872 | tf_op jit(solution)/shard_map/ppermute | solution.py:38
  51.8 5.0 %collective-permute-start.3 = (f32[3,4,1,256]{3,2,1,0:T(1,128)S(1)}, f32[3,4,1,256]{3,2,1,0:T(1,128)S(1)}, u32[]{:S(2)}, u32[]{:S(2)}) collective-permute-start(f32[3,4,1,256]{3,2,1,0:T(1,128)S(1)} %get-tuple-element.254), channel_id=1, source_target_pairs={{1,0},{2,1},{3,2},{4,3},{5,4},{6,5},{7,6},{8,7},{9,8},{10,9},{11,1... | collective-permute-start | bytes 36872 | tf_op jit(solution)/shard_map/ppermute | solution.py:41
  61.0 27.0 %copy-start.7 = (bf16[1,512,512]{2,1,0:T(8,128)(2,1)S(1)}, bf16[1,512,512]{2,1,0:T(8,128)(2,1)}, u32[]{:S(2)}) copy-start(bf16[1,512,512]{2,1,0:T(8,128)(2,1)} %param.16) | copy-start | bytes 1572868
  62.2 20.0 %all-to-all-start = ((f32[64,1,192]{2,1,0:T(1,128)}), f32[64,1,192]{2,1,0:T(1,128)S(1)}, u32[]{:S(2)}, u32[]{:S(2)}) async-start(f32[64,1,192]{2,1,0:T(1,128)} %reshape.332), calls=%async_computation | async-start | bytes 131072 | tf_op jit(solution)/shard_map/all_to_all | solution.py:224
  133.4 15.7 %all-to-all-start.2 = ((f32[64,1,864]{2,1,0:T(1,128)}), f32[64,1,864]{2,1,0:T(1,128)S(1)}, u32[]{:S(2)}, u32[]{:S(2)}) async-start(f32[64,1,864]{2,1,0:T(1,128)} %reshape.334), calls=%async_computation.2 | async-start | bytes 458752 | tf_op jit(solution)/shard_map/all_to_all | solution.py:238
  155.6 5.8 %collective-permute-start.4 = (f32[42,1,2,256]{3,2,1,0:T(2,128)S(1)}, f32[42,1,2,256]{3,2,1,0:T(2,128)S(1)}, u32[]{:S(2)}, u32[]{:S(2)}) collective-permute-start(f32[42,1,2,256]{3,2,1,0:T(2,128)S(1)} %slice.1288), channel_id=1, source_target_pairs={{0,64},{64,128},{128,192},{1,65},{65,129},{129,193},{2,66},{66,130... | collective-permute-start | bytes 258056 | tf_op jit(solution)/shard_map/ppermute | solution.py:53
  161.6 6.5 %collective-permute-start.5 = (f32[42,3,1,256]{3,2,1,0:T(1,128)S(1)}, f32[42,3,1,256]{3,2,1,0:T(1,128)S(1)}, u32[]{:S(2)}, u32[]{:S(2)}) collective-permute-start(f32[42,3,1,256]{3,2,1,0:T(1,128)S(1)} %slice.1289), channel_id=1, source_target_pairs={{0,1},{1,2},{2,3},{3,4},{4,5},{5,6},{6,7},{7,8},{8,9},{9,10},{10,1... | collective-permute-start | bytes 387080 | tf_op jit(solution)/shard_map/ppermute | solution.py:53
  169.1 5.4 %collective-permute-start.6 = (f32[3,1,2,256]{3,2,1,0:T(2,128)S(1)}, f32[3,1,2,256]{3,2,1,0:T(2,128)S(1)}, u32[]{:S(2)}, u32[]{:S(2)}) collective-permute-start(f32[3,1,2,256]{3,2,1,0:T(2,128)S(1)} %get-tuple-element.286), channel_id=1, source_target_pairs={{0,64},{64,128},{128,192},{1,65},{65,129},{129,193},{2,66},{66,130... | collective-permute-start | bytes 18440 | tf_op jit(solution)/shard_map/ppermute | solution.py:38
  173.2 4.4 collective-permute-start.7
  177.7 7.9 %collective-permute-start.8 = (f32[3,4,1,256]{3,2,1,0:T(1,128)S(1)}, f32[3,4,1,256]{3,2,1,0:T(1,128)S(1)}, u32[]{:S(2)}, u32[]{:S(2)}) collective-permute-start(f32[3,4,1,256]{3,2,1,0:T(1,128)S(1)} %get-tuple-element.252), channel_id=1, source_target_pairs={{0,1},{1,2},{2,3},{3,4},{4,5},{5,6},{6,7},{7,8},{8,9},{9,10},{10,1... | collective-permute-start | bytes 36872 | tf_op jit(solution)/shard_map/ppermute | solution.py:38
  183.4 5.0 %collective-permute-start.9 = (f32[3,4,1,256]{3,2,1,0:T(1,128)S(1)}, f32[3,4,1,256]{3,2,1,0:T(1,128)S(1)}, u32[]{:S(2)}, u32[]{:S(2)}) collective-permute-start(f32[3,4,1,256]{3,2,1,0:T(1,128)S(1)} %get-tuple-element.251), channel_id=1, source_target_pairs={{1,0},{2,1},{3,2},{4,3},{5,4},{6,5},{7,6},{8,7},{9,8},{10,9},{11,1... | collective-permute-start | bytes 36872 | tf_op jit(solution)/shard_map/ppermute | solution.py:41
  233.3 3.5 collective-permute-start.10
  235.5 4.4 collective-permute-start.11
  239.9 7.5 %collective-permute-start.12 = (f32[3,4,1,256]{3,2,1,0:T(1,128)S(1)}, f32[3,4,1,256]{3,2,1,0:T(1,128)S(1)}, u32[]{:S(2)}, u32[]{:S(2)}) collective-permute-start(f32[3,4,1,256]{3,2,1,0:T(1,128)S(1)} %get-tuple-element.248), channel_id=1, source_target_pairs={{0,1},{1,2},{2,3},{3,4},{4,5},{5,6},{6,7},{7,8},{8,9},{9,10},{10,1... | collective-permute-start | bytes 36872 | tf_op jit(solution)/shard_map/ppermute | solution.py:38
  245.2 5.0 %collective-permute-start.13 = (f32[3,4,1,256]{3,2,1,0:T(1,128)S(1)}, f32[3,4,1,256]{3,2,1,0:T(1,128)S(1)}, u32[]{:S(2)}, u32[]{:S(2)}) collective-permute-start(f32[3,4,1,256]{3,2,1,0:T(1,128)S(1)} %get-tuple-element.247), channel_id=1, source_target_pairs={{1,0},{2,1},{3,2},{4,3},{5,4},{6,5},{7,6},{8,7},{9,8},{10,9},{11,1... | collective-permute-start | bytes 36872 | tf_op jit(solution)/shard_map/ppermute | solution.py:41
  292.2 4.7 collective-permute-start.14
  295.6 4.4 collective-permute-start.15
  300.0 7.1 %collective-permute-start.16 = (f32[3,4,1,256]{3,2,1,0:T(1,128)S(1)}, f32[3,4,1,256]{3,2,1,0:T(1,128)S(1)}, u32[]{:S(2)}, u32[]{:S(2)}) collective-permute-start(f32[3,4,1,256]{3,2,1,0:T(1,128)S(1)} %get-tuple-element.244), channel_id=1, source_target_pairs={{0,1},{1,2},{2,3},{3,4},{4,5},{5,6},{6,7},{7,8},{8,9},{9,10},{10,1... | collective-permute-start | bytes 36872 | tf_op jit(solution)/shard_map/ppermute | solution.py:38
  305.2 5.0 %collective-permute-start.17 = (f32[3,4,1,256]{3,2,1,0:T(1,128)S(1)}, f32[3,4,1,256]{3,2,1,0:T(1,128)S(1)}, u32[]{:S(2)}, u32[]{:S(2)}) collective-permute-start(f32[3,4,1,256]{3,2,1,0:T(1,128)S(1)} %get-tuple-element.243), channel_id=1, source_target_pairs={{1,0},{2,1},{3,2},{4,3},{5,4},{6,5},{7,6},{8,7},{9,8},{10,9},{11,1... | collective-permute-start | bytes 36872 | tf_op jit(solution)/shard_map/ppermute | solution.py:41
  353.3 4.9 %collective-permute-start.18 = (f32[3,1,2,256]{3,2,1,0:T(2,128)S(1)}, f32[3,1,2,256]{3,2,1,0:T(2,128)S(1)}, u32[]{:S(2)}, u32[]{:S(2)}) collective-permute-start(f32[3,1,2,256]{3,2,1,0:T(2,128)S(1)} %get-tuple-element.280), channel_id=1, source_target_pairs={{0,64},{64,128},{128,192},{1,65},{65,129},{129,193},{2,66},{66,130... | collective-permute-start | bytes 18440 | tf_op jit(solution)/shard_map/ppermute | solution.py:38
  356.9 4.4 collective-permute-start.19
  361.3 7.2 %collective-permute-start.20 = (f32[3,4,1,256]{3,2,1,0:T(1,128)S(1)}, f32[3,4,1,256]{3,2,1,0:T(1,128)S(1)}, u32[]{:S(2)}, u32[]{:S(2)}) collective-permute-start(f32[3,4,1,256]{3,2,1,0:T(1,128)S(1)} %get-tuple-element.240), channel_id=1, source_target_pairs={{0,1},{1,2},{2,3},{3,4},{4,5},{5,6},{6,7},{7,8},{8,9},{9,10},{10,1... | collective-permute-start | bytes 36872 | tf_op jit(solution)/shard_map/ppermute | solution.py:38
  366.6 5.0 %collective-permute-start.21 = (f32[3,4,1,256]{3,2,1,0:T(1,128)S(1)}, f32[3,4,1,256]{3,2,1,0:T(1,128)S(1)}, u32[]{:S(2)}, u32[]{:S(2)}) collective-permute-start(f32[3,4,1,256]{3,2,1,0:T(1,128)S(1)} %get-tuple-element.239), channel_id=1, source_target_pairs={{1,0},{2,1},{3,2},{4,3},{5,4},{6,5},{7,6},{8,7},{9,8},{10,9},{11,1... | collective-permute-start | bytes 36872 | tf_op jit(solution)/shard_map/ppermute | solution.py:41
  412.7 4.9 %collective-permute-start.22 = (f32[3,1,2,256]{3,2,1,0:T(2,128)S(1)}, f32[3,1,2,256]{3,2,1,0:T(2,128)S(1)}, u32[]{:S(2)}, u32[]{:S(2)}) collective-permute-start(f32[3,1,2,256]{3,2,1,0:T(2,128)S(1)} %get-tuple-element.278), channel_id=1, source_target_pairs={{0,64},{64,128},{128,192},{1,65},{65,129},{129,193},{2,66},{66,130... | collective-permute-start | bytes 18440 | tf_op jit(solution)/shard_map/ppermute | solution.py:38
  416.3 4.4 collective-permute-start.23
  420.7 7.2 %collective-permute-start.24 = (f32[3,4,1,256]{3,2,1,0:T(1,128)S(1)}, f32[3,4,1,256]{3,2,1,0:T(1,128)S(1)}, u32[]{:S(2)}, u32[]{:S(2)}) collective-permute-start(f32[3,4,1,256]{3,2,1,0:T(1,128)S(1)} %get-tuple-element.236), channel_id=1, source_target_pairs={{0,1},{1,2},{2,3},{3,4},{4,5},{5,6},{6,7},{7,8},{8,9},{9,10},{10,1... | collective-permute-start | bytes 36872 | tf_op jit(solution)/shard_map/ppermute | solution.py:38
  426.0 5.0 %collective-permute-start.25 = (f32[3,4,1,256]{3,2,1,0:T(1,128)S(1)}, f32[3,4,1,256]{3,2,1,0:T(1,128)S(1)}, u32[]{:S(2)}, u32[]{:S(2)}) collective-permute-start(f32[3,4,1,256]{3,2,1,0:T(1,128)S(1)} %get-tuple-element.235), channel_id=1, source_target_pairs={{1,0},{2,1},{3,2},{4,3},{5,4},{6,5},{7,6},{8,7},{9,8},{10,9},{11,1... | collective-permute-start | bytes 36872 | tf_op jit(solution)/shard_map/ppermute | solution.py:41
  (5 other events, 48.6 us)
where the time goes:
time: 476 us; the launch traced here: 474 us
  blocking collectives  185 us (39%)
  starting transfers between devices  107 us (22%)
  waiting for transfers between devices  55.4 us (12%)
  matrix products  45.6 us (10%)
  other arithmetic  38.4 us (8%)
  local copies, waits for them, and re-layouts  21.9 us (5%)
  between operations  21 us (4%)
    psum x20, blocking collectives, by_axis(): return functools.reduce(lax.psum, axes, shard)  185 us
    ppermute x12, starting transfers between devices, with_halo(): lax.ppermute(lax.slice_in_dim(block, block.shape[dim] - width, None, axis...  51.2 us
    dot_general x4, matrix products, micro_solve(): jnp.dot(misfit.astype(jnp.bfloat16), precond, preferred_element_type=jnp....  36.2 us
    ppermute x12, waiting for transfers between devices, with_halo(): lax.ppermute(lax.slice_in_dim(block, 0, width, axis=dim), axis, backward)  31.8 us
    ppermute x12, starting transfers between devices, with_halo(): lax.ppermute(lax.slice_in_dim(block, 0, width, axis=dim), axis, backward)  19.5 us
    another operation x2, other arithmetic  18 us
    all_to_all x1, starting transfers between devices, shards(): lax.all_to_all(send_sweeps, MICRO, split_axis=1, concat_axis=1, tiled=True)  12.6 us
    all_to_all x1, waiting for transfers between devices, shards(): back = lax.all_to_all(rows, MICRO, split_axis=1, concat_axis=1, tiled=True)  11.2 us
  transfers between devices with their start and end apart: 29, of which 15 were waited for; matrix products, arithmetic and copies ran while one was open for 7% of the time, Pallas kernels for 0%

commit v1 on v0

v1 whole, which is shorter than its diff:
```python
import jax
import jax.numpy as jnp
from jax import lax
from jax.experimental import pallas as pl
from jax.experimental.pallas import tpu as pltpu
from jax.sharding import Mesh
from jax.sharding import PartitionSpec as P

ITMAX = 4
MICRO = ("micro_0", "micro_1", "micro_2")

BETA = 0.1
OMEGA = 0.8
MASS = 0.1
VOIGT = ((0, 5, 4), (5, 1, 3), (4, 3, 2))
PAIRS = tuple((i, j) for i in range(6) for j in range(i, 6))
TANGENT = {}
for number, (i, j) in enumerate(PAIRS):
    TANGENT[i, j] = TANGENT[j, i] = 6 + number
ROWS = 27
LOAD = 27
FIELDS = 30
DOTS = 128
F32 = jnp.float32
BF16 = jnp.bfloat16


def micro_kernel(strain_ref, stiff_ref, pre_ref, force_ref, maps_ref, cols_ref, out_ref):
    stiff = stiff_ref[...]
    pre = pre_ref[...]
    halves = 2
    width = strain_ref.shape[1] // halves
    loads, modes, sweeps = [], [], []
    for h in range(halves):
        part = strain_ref[:, h * width : (h + 1) * width]
        load = jnp.dot(force_ref[...], part.astype(BF16), preferred_element_type=F32)
        loads.append(load)
        sweeps.append(part[6:7])
    for h in range(halves):
        modes.append(OMEGA * jnp.dot(pre, loads[h].astype(BF16), preferred_element_type=F32))
    for sweep in range(1, ITMAX):
        misfits = []
        for h in range(halves):
            misfit = (
                jnp.dot(stiff, modes[h].astype(BF16), preferred_element_type=F32)
                + BETA * jnp.tanh(modes[h])
                - loads[h]
            )
            misfits.append(misfit.astype(BF16))
        for h in range(halves):
            update = modes[h] - OMEGA * jnp.dot(pre, misfits[h], preferred_element_type=F32)
            modes[h] = jnp.where(sweeps[h] > sweep, update, modes[h])
    couple, high, low = maps_ref[0], maps_ref[1], maps_ref[2]
    cols = cols_ref[...]
    for h in range(halves):
        at = slice(h * width, (h + 1) * width)
        bent = jnp.tanh(modes[h])
        slope = 1.0 - bent * bent
        slope_high = slope.astype(BF16)
        slope_low = (slope - slope_high.astype(F32)).astype(BF16)
        rows = (
            jnp.dot(couple, modes[h].astype(BF16), preferred_element_type=F32)
            + jnp.dot(high, slope_high, preferred_element_type=F32)
            + jnp.dot(low, slope_high, preferred_element_type=F32)
            + jnp.dot(high, slope_low, preferred_element_type=F32)
            + cols[:, 0:1]
        )
        part = strain_ref[:, at]
        trace = part[0:1] + part[1:2] + part[2:3]
        elastic = cols[:8, 1:2] * trace + cols[:8, 2:3] * part
        out_ref[:8, at] = rows[:8] + elastic
        out_ref[8:, at] = rows[8:]


def micro_solve(points, stiffness, precond, forcing, coupling, lame_first, lame_shear):
    modes = stiffness.shape[0]
    count = points.shape[1]
    tile = 512
    force = jnp.pad(forcing, ((0, 2), (0, 0))).T
    wide = coupling.astype(F32).T
    products = jnp.stack([wide[i] * wide[j] for i, j in PAIRS])
    high = products.astype(BF16)
    low = (products - high.astype(F32)).astype(BF16)
    maps = jnp.stack(
        [
            jnp.pad(coupling.T, ((0, 26), (0, 0))),
            jnp.pad(high, ((6, 5), (0, 0))),
            jnp.pad(low, ((6, 5), (0, 0))),
        ]
    )
    base_first = [0.0] * 6 + [float(i < 3 and j < 3) for i, j in PAIRS] + [0.0] * 5
    base_shear = (
        [0.0] * 6
        + [2.0 * float(i == j and i < 3) + float(i == j and i >= 3) for i, j in PAIRS]
        + [0.0] * 5
    )
    on_trace = [1.0] * 3 + [0.0] * 29
    on_strain = [2.0] * 3 + [1.0] * 3 + [0.0] * 26
    cols = jnp.stack(
        [
            lame_first * jnp.array(base_first, F32) + lame_shear * jnp.array(base_shear, F32),
            lame_first * jnp.array(on_trace, F32),
            lame_shear * jnp.array(on_strain, F32),
        ]
        + [jnp.zeros((32,), F32)] * 5,
        axis=1,
    )
    whole = lambda *shape: pl.BlockSpec(shape, lambda step: (0,) * len(shape))
    return pl.pallas_call(
        micro_kernel,
        grid=(count // tile,),
        in_specs=[
            pl.BlockSpec((8, tile), lambda step: (0, step)),
            whole(modes, modes),
            whole(modes, modes),
            whole(modes, 8),
            whole(3, 32, modes),
            whole(32, 8),
        ],
        out_specs=pl.BlockSpec((32, tile), lambda step: (0, step)),
        out_shape=jax.ShapeDtypeStruct((32, count), F32),
        compiler_params=pltpu.CompilerParams(vmem_limit_bytes=48 * 1024 * 1024),
        name="micro_solve",
    )(points, stiffness, precond, force, maps, cols)


def shifts(shape):
    plane = lax.broadcasted_iota(jnp.int32, shape, 0)
    column = lax.broadcasted_iota(jnp.int32, shape, 1)
    planes, columns = shape

    def next_x(v):
        return jnp.where(plane == planes - 1, 0.0, pltpu.roll(v, planes - 1, 0))

    def prev_x(v):
        return jnp.where(plane == 0, 0.0, pltpu.roll(v, 1, 0))

    def next_z(v):
        return jnp.where(column == columns - 1, 0.0, pltpu.roll(v, columns - 1, 1))

    def prev_z(v):
        return jnp.where(column == 0, 0.0, pltpu.roll(v, 1, 1))

    return next_x, prev_x, next_z, prev_z


def strain_rows(nodes, lower, upper, moves):
    next_x, _, next_z, _ = moves
    sums, diffs = {}, {}
    for y in range(lower, upper + 2):
        for c in range(3):
            v = nodes[y][c]
            w = next_z(v)
            sums[y, c] = v + w
            diffs[y, c] = w - v
    strain = {}
    for y in range(lower, upper + 1):
        grad = []
        for c in range(3):
            both = sums[y, c] + sums[y + 1, c]
            rise = sums[y + 1, c] - sums[y, c]
            turn = diffs[y, c] + diffs[y + 1, c]
            grad.append(
                (
                    0.25 * (next_x(both) - both),
                    0.25 * (next_x(rise) + rise),
                    0.25 * (next_x(turn) + turn),
                )
            )
        strain[y] = (
            grad[0][0],
            grad[1][1],
            grad[2][2],
            grad[1][2] + grad[2][1],
            grad[0][2] + grad[2][0],
            grad[0][1] + grad[1][0],
        )
    return strain


def force_rows(stress, lower, upper, moves):
    _, prev_x, _, prev_z = moves
    xs = {}
    for y in range(lower - 1, upper + 1):
        for c in range(3):
            a, b, d = (stress[y][VOIGT[c][k]] for k in range(3))
            xs[y, c] = (prev_x(a) - a, prev_x(b) + b, prev_x(d) + d)
    force = {}
    for y in range(lower, upper + 1):
        parts = []
        for c in range(3):
            a0, b0, d0 = xs[y - 1, c]
            a1, b1, d1 = xs[y, c]
            flat = (a0 + a1) + (b0 - b1)
            deep = d0 + d1
            parts.append(0.25 * (prev_z(flat + deep) + (flat - deep)))
        force[y] = tuple(parts)
    return force


def apply_rows(nodes, tangent, lower, upper, moves):
    strain = strain_rows(nodes, lower - 1, upper, moves)
    stress = {}
    for y in range(lower - 1, upper + 1):
        rows = []
        for i in range(6):
            total = tangent(y, TANGENT[i, 0]) * strain[y][0]
            for j in range(1, 6):
                total = total + tangent(y, TANGENT[i, j]) * strain[y][j]
            rows.append(total)
        stress[y] = tuple(rows)
    force = force_rows(stress, lower, upper, moves)
    return {
        y: tuple(MASS * nodes[y][c] + force[y][c] for c in range(3))
        for y in range(lower, upper + 1)
    }


def value_reader(low_ref, own_ref, high_ref):
    def read(y, c):
        if y < 0:
            return low_ref[c, y + 2]
        if y < 2:
            return own_ref[c, y]
        return high_ref[c, y - 2]

    return read


def read_rows(ref, lower, count):
    return {lower + k: tuple(ref[c, k] for c in range(3)) for k in range(count)}


def inside(rows, y, last_ref):
    keep = jnp.where(last_ref[0] == 1, 0.0, 1.0)
    rows[y] = tuple(v * keep for v in rows[y])


def write_rows(ref, rows, lower, count):
    for k in range(count):
        for c in range(3):
            ref[c, k] = rows[lower + k][c]


def row_dot(first, second):
    total = None
    for y in (0, 1):
        for c in range(3):
            term = first[y][c] * second[y][c]
            total = term if total is None else total + term
    return total


def pack_dots(ref, products):
    lane = lax.broadcasted_iota(jnp.int32, (1, DOTS), 1)
    packed = jnp.zeros((1, DOTS), F32)
    for k, product in enumerate(products):
        total = jnp.sum(jnp.sum(product, axis=0, keepdims=True), axis=1, keepdims=True)
        packed = packed + jnp.where(lane == k, total, 0.0)
    ref[...] = packed


def unpack_dots(ref, count):
    row = jnp.sum(ref[...], axis=0, keepdims=True)
    lane = lax.broadcasted_iota(jnp.int32, (1, DOTS), 1)
    return [
        jnp.sum(jnp.where(lane == k, row, 0.0), axis=1, keepdims=True) for k in range(count)
    ]


def first_kernel(last_ref, low_ref, own_ref, high_ref, v0_ref, v1_ref):
    read = value_reader(low_ref, own_ref, high_ref)
    moves = shifts(own_ref.shape[2:])
    stress = {y: tuple(read(y, i) for i in range(6)) for y in range(-2, 3)}
    force = force_rows(stress, -1, 2, moves)
    v0 = {y: tuple(read(y, LOAD + c) - force[y][c] for c in range(3)) for y in range(-1, 3)}
    inside(v0, 2, last_ref)
    v1 = apply_rows(v0, read, 0, 1, moves)
    write_rows(v0_ref, v0, -1, 4)
    write_rows(v1_ref, v1, 0, 2)


def second_kernel(
    last_ref, low_ref, own_ref, high_ref, v0_ref, v1_low_ref, v1_ref, v1_high_ref, v2_ref, dots_ref
):
    read = value_reader(low_ref, own_ref, high_ref)
    moves = shifts(own_ref.shape[2:])
    v1 = read_rows(v1_low_ref, -2, 2) | read_rows(v1_ref, 0, 2) | read_rows(v1_high_ref, 2, 2)
    v2 = apply_rows(v1, read, -1, 2, moves)
    inside(v2, 2, last_ref)
    v0 = read_rows(v0_ref, -1, 4)
    write_rows(v2_ref, v2, -1, 4)
    pack_dots(
        dots_ref,
        [
            row_dot(a, b)
            for a, b in ((v0, v0), (v0, v1), (v0, v2), (v1, v1), (v1, v2))
        ],
    )


def third_kernel(
    low_ref,
    own_ref,
    high_ref,
    v0_ref,
    v1_low_ref,
    v1_ref,
    v1_high_ref,
    v2_ref,
    sums_ref,
    r1_ref,
    r2_ref,
    w3_ref,
    coef_ref,
):
    read = value_reader(low_ref, own_ref, high_ref)
    moves = shifts(own_ref.shape[2:])
    m00, m01, m02, m11, m12 = unpack_dots(sums_ref, 5)
    a0 = m00 / m01
    n1 = m00 - 2.0 * a0 * m01 + a0 * a0 * m11
    b0 = n1 / m00
    e = 1.0 + b0
    a1 = n1 / (e * e * m01 - e * a0 * (m02 + m11) + a0 * a0 * m12)
    center = 0.5 * (1.0 / a0 + 1.0 / a1 + b0 / a0)
    v0 = read_rows(v0_ref, -1, 4)
    v1 = read_rows(v1_low_ref, -2, 2) | read_rows(v1_ref, 0, 2) | read_rows(v1_high_ref, 2, 2)
    v2 = read_rows(v2_ref, -1, 4)
    along, twice = a0 + a1 * e, a1 * a0
    r2 = {
        y: tuple(v0[y][c] - along * v1[y][c] + twice * v2[y][c] for c in range(3))
        for y in range(-1, 3)
    }
    image = apply_rows(r2, read, 0, 1, moves)
    scale = 1.0 / center
    w3 = {y: tuple(image[y][c] * scale - r2[y][c] for c in range(3)) for y in (0, 1)}
    r1 = {y: tuple(v0[y][c] - a0 * v1[y][c] for c in range(3)) for y in (0, 1)}
    write_rows(r1_ref, r1, 0, 2)
    write_rows(r2_ref, r2, 0, 2)
    write_rows(w3_ref, w3, 0, 2)
    lane = lax.broadcasted_iota(jnp.int32, (1, DOTS), 1)
    packed = jnp.zeros((1, DOTS), F32)
    for k, value in enumerate((a0, b0, a1, n1, center)):
        packed = packed + jnp.where(lane == k, value, 0.0)
    coef_ref[...] = packed


def basis_pairs():
    return [(i, j) for i in range(6) for j in range(i, 6)]


def fourth_kernel(
    last_ref,
    low_ref,
    own_ref,
    high_ref,
    coef_ref,
    v0_ref,
    r1_ref,
    r2_ref,
    w3_low_ref,
    w3_ref,
    w3_high_ref,
    w4_ref,
    w5_ref,
    dots_ref,
):
    read = value_reader(low_ref, own_ref, high_ref)
    moves = shifts(own_ref.shape[2:])
    scale = 1.0 / unpack_dots(coef_ref, 5)[4]
    w3 = read_rows(w3_low_ref, -2, 2) | read_rows(w3_ref, 0, 2) | read_rows(w3_high_ref, 2, 2)
    image = apply_rows(w3, read, -1, 2, moves)
    w4 = {y: tuple(image[y][c] * scale - w3[y][c] for c in range(3)) for y in range(-1, 3)}
    inside(w4, 2, last_ref)
    image = apply_rows(w4, read, 0, 1, moves)
    w5 = {y: tuple(image[y][c] * scale - w4[y][c] for c in range(3)) for y in (0, 1)}
    write_rows(w4_ref, w4, 0, 2)
    write_rows(w5_ref, w5, 0, 2)
    v0 = read_rows(v0_ref, -1, 4)
    basis = [v0, read_rows(r1_ref, 0, 2), read_rows(r2_ref, 0, 2), w3, w4, w5]
    pack_dots(dots_ref, [row_dot(basis[i], basis[j]) for i, j in basis_pairs()])


def total_of(terms):
    total = None
    for term in terms:
        total = term if total is None else total + term
    return total


def fifth_kernel(
    coef_ref, sums_ref, v0_ref, r1_ref, r2_ref, w3_ref, w4_ref, w5_ref, increment_ref, residual_ref
):
    a0, b0, a1, n1, center = unpack_dots(coef_ref, 5)
    dots = unpack_dots(sums_ref, 21)
    gram = {}
    for k, (i, j) in enumerate(basis_pairs()):
        gram[i, j] = gram[j, i] = dots[k]
    zero = jnp.zeros((1, 1), F32)
    one = jnp.ones((1, 1), F32)
    i0, i1 = 1.0 / a0, 1.0 / a1

    def image_of(p):
        return [
            i0 * p[0] - b0 * i0 * p[1],
            (i1 + b0 * i0) * p[1] - i0 * p[0],
            center * p[2] - i1 * p[1],
            center * (p[2] + p[3]),
            center * (p[3] + p[4]),
            center * p[4],
        ]

    def product(p, q):
        return total_of(
            p[i] * total_of(gram[i, j] * q[j] for j in range(6)) for i in range(6)
        )

    solved = [a0 + a1 * b0, a1, zero, zero, zero, zero]
    left = [zero, zero, one, zero, zero, zero]
    norm = gram[2, 2]
    ratio = norm / n1
    course = [ratio * b0, ratio, one, zero, zero, zero]
    for step in range(3):
        image = image_of(course)
        alpha = norm / product(course, image)
        solved = [s + alpha * p for s, p in zip(solved, course)]
        left = [r - alpha * q for r, q in zip(left, image)]
        if step < 2:
            fresh = product(left, left)
            ratio = fresh / norm
            course = [r + ratio * p for r, p in zip(left, course)]
            norm = fresh
    v0 = read_rows(v0_ref, -1, 4)
    basis = [v0] + [read_rows(ref, 0, 2) for ref in (r1_ref, r2_ref, w3_ref, w4_ref, w5_ref)]
    for y in (0, 1):
        for c in range(3):
            increment_ref[c, y] = total_of(solved[k] * basis[k][y][c] for k in range(6))
            residual_ref[c, y] = total_of(left[k] * basis[k][y][c] for k in range(6))


def local_call(kernel, outs, name, *args, flag=None):
    specs = [pl.BlockSpec(memory_space=pltpu.VMEM)] * len(args)
    if flag is not None:
        specs = [pl.BlockSpec(memory_space=pltpu.SMEM)] + specs
        args = (flag,) + args
    return pl.pallas_call(
        kernel,
        in_specs=specs,
        out_specs=[pl.BlockSpec(memory_space=pltpu.VMEM)] * len(outs),
        out_shape=[jax.ShapeDtypeStruct(shape, F32) for shape in outs],
        compiler_params=pltpu.CompilerParams(vmem_limit_bytes=48 * 1024 * 1024),
        name=name,
    )(*args)


def up_and_down(up, down):
    count = lax.axis_size(MICRO)
    forward = [(k, k + 1) for k in range(count - 1)]
    backward = [(k + 1, k) for k in range(count - 1)]
    return lax.ppermute(up, MICRO, forward), lax.ppermute(down, MICRO, backward)


def summands(packed):
    count = lax.axis_size(MICRO)
    sent = jnp.broadcast_to(packed[None], (count, 1, DOTS))
    got = lax.all_to_all(sent, MICRO, split_axis=0, concat_axis=0, tiled=True)
    return got.reshape(count, DOTS)


def gather_planes(block):
    count = lax.axis_size("macro")
    pieces = [block] + [
        lax.ppermute(block, "macro", [(k, (k - shift) % count) for k in range(count)])
        for shift in range(1, count)
    ]
    planes = block.shape[2]
    twice = jnp.concatenate(pieces + pieces[:-1], axis=2)
    start = (count - lax.axis_index("macro")) % count * planes
    return lax.dynamic_slice_in_dim(twice, start, count * planes, axis=2)


def element_strain(nodes):
    padded = jnp.pad(nodes, ((0, 0), (0, 0), (0, 0), (0, 1)))

    def pair(v, axis):
        size = v.shape[axis] - 1
        first = lax.slice_in_dim(v, 0, size, axis=axis)
        second = lax.slice_in_dim(v, 1, size + 1, axis=axis)
        return first + second, second - first

    sum_z, diff_z = pair(padded, 3)
    sum_yz, diff_yz = pair(sum_z, 2)
    sum_yd, _ = pair(diff_z, 2)
    grad_x = 0.25 * pair(sum_yz, 1)[1]
    grad_y = 0.25 * pair(diff_yz, 1)[0]
    grad_z = 0.25 * pair(sum_yd, 1)[0]
    return jnp.stack(
        [
            grad_x[0],
            grad_y[1],
            grad_z[2],
            grad_z[1] + grad_y[2],
            grad_z[0] + grad_x[2],
            grad_y[0] + grad_x[1],
        ]
    )


def with_next(block, axis, dim):
    count = lax.axis_size(axis)
    high = lax.ppermute(
        lax.slice_in_dim(block, 0, 1, axis=dim), axis, [(k + 1, k) for k in range(count - 1)]
    )
    return jnp.concatenate([block, high], axis=dim)


def shards(
    displacement,
    load,
    routes,
    counts,
    stiffness,
    precond,
    forcing,
    coupling,
    lame_first,
    lame_shear,
):
    planes, width, depth = displacement.shape[1:]
    points = planes * width * depth
    owners = lax.axis_size(MICRO)
    capacity = max(2, 2 * points // owners)
    slots = owners * capacity

    owner_of = routes.reshape(points)
    chosen = owner_of[:, None] == jnp.arange(owners, dtype=jnp.int32)[None, :]
    before = jnp.tri(points, points, -1, dtype=BF16)
    earlier = jnp.dot(before, chosen.astype(BF16), preferred_element_type=F32)
    ranks = jnp.sum(jnp.where(chosen, earlier, 0.0), axis=1).astype(jnp.int32)
    target = owner_of * capacity + ranks

    strain = element_strain(with_next(with_next(displacement, "macro", 1), MICRO, 2))
    leaving = jnp.concatenate(
        [strain.reshape(6, points), counts.reshape(1, points).astype(F32)], axis=0
    )
    send = jnp.zeros((7, slots), F32).at[:, target].set(
        leaving, unique_indices=True, mode="promise_in_bounds"
    )
    send = send.reshape(7, owners, capacity).transpose(1, 0, 2).reshape(owners, 1, 7 * capacity)
    got = lax.all_to_all(send, MICRO, split_axis=0, concat_axis=0, tiled=True)
    got = got.reshape(owners, 7, capacity).transpose(1, 0, 2).reshape(7, slots)
    rows = micro_solve(
        jnp.pad(got, ((0, 1), (0, 0))),
        stiffness[0],
        precond[0],
        forcing[0],
        coupling[0],
        lame_first[0],
        lame_shear[0],
    )
    back = rows[:ROWS].reshape(ROWS, owners, capacity).transpose(1, 0, 2)
    back = lax.all_to_all(
        back.reshape(owners, 1, ROWS * capacity), MICRO, split_axis=0, concat_axis=0, tiled=True
    )
    back = back.reshape(owners, ROWS, capacity).transpose(1, 0, 2).reshape(ROWS, slots)
    picked = jnp.take(back, target, axis=1, mode="clip")
    values = jnp.concatenate([picked.reshape(ROWS, planes, width, depth), load], axis=0)
    own = gather_planes(values.transpose(0, 2, 1, 3))
    low, high = up_and_down(own, own[:, :1])
    sets = (low, own, high)
    last = (lax.axis_index(MICRO) == owners - 1).astype(jnp.int32).reshape(1)
    whole = own.shape[2]
    two = (3, 2, whole, depth)
    four = (3, 4, whole, depth)
    line = (1, DOTS)
    v0, v1 = local_call(first_kernel, (four, two), "first_rows", *sets, flag=last)
    v1_low, v1_high = up_and_down(v1, v1)
    v2, dots = local_call(
        second_kernel, (four, line), "second_rows", *sets, v0, v1_low, v1, v1_high, flag=last
    )
    r1, r2, w3, coef = local_call(
        third_kernel,
        (two, two, two, line),
        "third_rows",
        *sets,
        v0,
        v1_low,
        v1,
        v1_high,
        v2,
        summands(dots),
    )
    w3_low, w3_high = up_and_down(w3, w3)
    w4, w5, dots = local_call(
        fourth_kernel,
        (two, two, line),
        "fourth_rows",
        *sets,
        coef,
        v0,
        r1,
        r2,
        w3_low,
        w3,
        w3_high,
        flag=last,
    )
    increment, residual = local_call(
        fifth_kernel, (two, two), "fifth_rows", coef, summands(dots), v0, r1, r2, w3, w4, w5
    )
    start = lax.axis_index("macro") * planes

    def mine(field):
        return lax.dynamic_slice_in_dim(field, start, planes, axis=2).transpose(0, 2, 1, 3)

    return (mine(increment), mine(residual))


def solution(mesh):
    split = Mesh(
        mesh.devices.reshape(mesh.shape["macro"], 4, 8, 2),
        ("macro", "micro_0", "micro_1", "micro_2"),
    )
    placed = (
        P(None, "macro", MICRO, None),
        P(None, "macro", MICRO, None),
        P("macro", MICRO, None, None),
        P("macro", MICRO, None),
        P(MICRO, None, None),
        P(MICRO, None, None),
        P(MICRO, None, None),
        P(MICRO, None, None),
        P(MICRO),
        P(MICRO),
    )
    return jax.shard_map(
        shards,
        mesh=split,
        in_specs=placed,
        out_specs=(P(None, "macro", MICRO, None), P(None, "macro", MICRO, None)),
        check_vma=False,
    )
```

time: 476 us -> 157 us (0.33)
  blocking collectives: 185 us -> 21.2 us
  starting transfers between devices: 107 us -> 54.2 us
  matrix products: 45.6 us -> 1.82 us
  other arithmetic: 38.4 us -> 1.74 us
  between operations: 21 us -> 2.56 us
  Pallas kernels: 0 us -> 15.7 us
  waiting for transfers between devices: 55.4 us -> 43.9 us
  local copies, waits for them, and re-layouts: 21.9 us -> 15.2 us
    psum x20 -> x0, blocking collectives: 185 us -> none  [by_axis(): return functools.reduce(lax.psum, axes, shard)]
    ppermute x26 -> x11, starting transfers between devices: 79.6 us -> 29.8 us  [the longest x3 11.2 us: up_and_down(): lax.ppermute(up, MICRO, forward)]
    dot_general x7 -> x1, matrix products: 45.6 us -> 1.82 us  [shards(): earlier = jnp.dot(before, chosen.astype(BF16), preferred_element_type=F32)]
    ppermute x26 -> x11, waiting for transfers between devices: 35.1 us -> 13.7 us  [the longest x3 5.58 us: up_and_down(): lax.ppermute(down, MICRO, backward)]
    all_to_all x0 -> x1, blocking collectives: none -> 21.2 us  [summands(): got = lax.all_to_all(sent, MICRO, split_axis=0, concat_axis=0, tiled=True)]
    another operation x20 -> x3, other arithmetic: 18.8 us -> 0.03 us  [the longest x1 0.01 us: micro_solve(): jnp.stack([jnp.pad(coupling.T, ((0, 26), (0, 0))), jnp.pad(high, ((6, 5),...]
    pallas_call x0 -> x6, Pallas kernels: none -> 15.7 us  [the longest x1 13.5 us: micro_solve(): pl.pallas_call(micro_kernel, grid=(count // tile,), in_specs=[pl.BlockSpe...]
    all_to_all x3, waiting for transfers between devices: 20.2 us -> 30.3 us  [the longest x1 11.2 us: shards(): lax.all_to_all(back.reshape(owners, 1, ROWS * capacity), MICRO, split_axi...]
  transfers between devices with their start and end apart: 29 -> 14, of which waited for: 15 -> 9; matrix products, arithmetic and copies ran while one was open for 7% -> 2% of each run, Pallas kernels for 0% -> 0%
where the time goes in v1:
time: 157 us; the launch traced here: 156 us
  starting transfers between devices  54.2 us (35%)
  waiting for transfers between devices  43.9 us (28%)
  blocking collectives  21.2 us (14%)
  Pallas kernels  15.7 us (10%)
  local copies, waits for them, and re-layouts  15.2 us (10%)
  between operations  2.56 us (2%)
  matrix products  1.82 us (1%)
  other arithmetic  1.74 us (1%)
    all_to_all x1, blocking collectives, summands(): got = lax.all_to_all(sent, MICRO, split_axis=0, concat_axis=0, tiled=True)  21.2 us
    pallas_call x1, Pallas kernels, micro_solve(): pl.pallas_call(micro_kernel, grid=(count // tile,), in_specs=[pl.BlockSpe...  13.5 us
    all_to_all x1, starting transfers between devices, shards(): got = lax.all_to_all(send, MICRO, split_axis=0, concat_axis=0, tiled=True)  12.1 us
    all_to_all x1, waiting for transfers between devices, shards(): lax.all_to_all(back.reshape(owners, 1, ROWS * capacity), MICRO, split_axi...  11.2 us
    ppermute x3, starting transfers between devices, up_and_down(): lax.ppermute(up, MICRO, forward)  11.2 us
    all_to_all x1, waiting for transfers between devices, shards(): got = lax.all_to_all(send, MICRO, split_axis=0, concat_axis=0, tiled=True)  9.75 us
    all_to_all x1, waiting for transfers between devices, summands(): got = lax.all_to_all(sent, MICRO, split_axis=0, concat_axis=0, tiled=True)  9.3 us
    all_to_all x1, starting transfers between devices, summands(): got = lax.all_to_all(sent, MICRO, split_axis=0, concat_axis=0, tiled=True)  7.89 us
  transfers between devices with their start and end apart: 14, of which 9 were waited for; matrix products, arithmetic and copies ran while one was open for 2% of the time, Pallas kernels for 0%

profile of v1, /device:TPU:1, one launch (start us, length us, event | category | flops | bytes accessed | tf_op | source)
XLA Modules:
  0.0 156.3 jit_solution(10884145727087198989)
XLA Ops:
  1.3 1.3 collective-permute-start
  5.4 1.8 %fusion.3 = f32[1024]{0:T(1024)S(1)} fusion(s32[1024]{0:T(1024)S(1)} %iota_add_fusion, s32[1024]{0:T(1024)} %bitcast.85), kind=kOutput, calls=%fused_computation.6 | convolution fusion | flops 135527424 | bytes 12288 | tf_op jit(solution)/shard_map/dot_general | solution.py:538
  7.8 5.2 %collective-permute-start.1 = (f32[3,3,1,256]{3,2,1,0:T(1,128)S(1)}, f32[3,3,1,256]{3,2,1,0:T(1,128)S(1)}, u32[]{:S(2)}, u32[]{:S(2)}) collective-permute-start(f32[3,3,1,256]{3,2,1,0:T(1,128)S(1)} %slice.159), channel_id=1, source_target_pairs={{1,0},{2,1},{3,2},{4,3},{5,4},{6,5},{7,6},{8,7},{9,8},{10,9},{11,1... | collective-permute-start | bytes 27656 | tf_op jit(solution)/shard_map/ppermute | solution.py:511
  13.1 1.0 collective-permute-done.1
  14.7 3.3 %scatter_custom_fusion = f32[7,2048]{0,1:T(8,128)S(1)} fusion(s32[1024]{0:T(1024)S(1)} %bitcast.86, f32[1024,7]{1,0:T(8,128)S(1)} %copy.43, f32[]{:T(128)} %constant.23.clone.1), kind=kCustom, calls=%fused_computation.7 | custom fusion | bytes 57348 | tf_op jit(solution)/shard_map/scatter | solution.py:546
  19.4 12.1 %all-to-all-start = ((f32[64,1,224]{2,1,0:T(1,128)}), f32[64,1,224]{2,1,0:T(1,128)S(1)}, u32[]{:S(2)}, u32[]{:S(2)}) async-start(f32[64,1,224]{2,1,0:T(1,128)} %copy.45), calls=%async_computation | async-start | bytes 131072 | tf_op jit(solution)/shard_map/all_to_all | solution.py:550
  31.5 9.8 %all-to-all-done = f32[64,1,224]{2,1,0:T(1,128)S(1)} async-done(((f32[64,1,224]{2,1,0:T(1,128)}), f32[64,1,224]{2,1,0:T(1,128)S(1)}, u32[]{:S(2)}, u32[]{:S(2)}) %all-to-all-start) | async-done | bytes 57376 | tf_op jit(solution)/shard_map/all_to_all | solution.py:550
  41.7 13.5 %micro_solve.1 = f32[32,2048]{1,0:T(8,128)S(1)} custom-call(f32[8,2048]{1,0:T(8,128)S(1)} %pad.24.strain_ref, bf16[512,512]{1,0:T(8,128)(2,1)S(1)} %bitcast.66, bf16[512,512]{1,0:T(8,128)(2,1)S(1)} %bitcast.67, bf16[512,8]{1,0:T(8,128)(2,1)S(1)} %pad_bitcast_fusion.force_ref, bf16[3,32,512]{2,1,0:T(8,128)(2,1)S(1)} %pad_maximum_fusion.maps_ref, ...), custom_call_target="tpu_custom_call" | custom-call | tf_op jit(solution)/shard_map/micro_solve/pallas_call | solution.py:109
  55.8 0.9 copy.51
  56.7 4.4 %all-to-all-start.1 = ((f32[64,1,864]{2,1,0:T(1,128)}), f32[64,1,864]{2,1,0:T(1,128)S(1)}, u32[]{:S(2)}, u32[]{:S(2)}) async-start(f32[64,1,864]{2,1,0:T(1,128)} %copy.51), calls=%async_computation.1 | async-start | bytes 458752 | tf_op jit(solution)/shard_map/all_to_all | solution.py:562
  61.2 11.2 %all-to-all-done.1 = f32[64,1,864]{2,1,0:T(1,128)S(1)} async-done(((f32[64,1,864]{2,1,0:T(1,128)}), f32[64,1,864]{2,1,0:T(1,128)S(1)}, u32[]{:S(2)}, u32[]{:S(2)}) %all-to-all-start.1) | async-done | bytes 221216 | tf_op jit(solution)/shard_map/all_to_all | solution.py:562
  72.6 1.0 copy.53
  73.6 2.8 %gather_fusion = f32[1024,27]{1,0:T(8,128)S(1)} fusion(f32[27,2048]{0,1:T(8,128)S(1)} %bitcast.73, s32[1024]{0:T(1024)S(1)} %broadcast_clamp_fusion), kind=kCustom, calls=%fused_computation | custom fusion | bytes 225280 | tf_op jit(solution)/shard_map/jit(_take)/gather | solution.py:566
  76.7 2.2 %collective-permute-start.4 = (f32[30,2,2,256]{3,2,1,0:T(2,128)S(1)}, f32[30,2,2,256]{3,2,1,0:T(2,128)S(1)}, u32[]{:S(2)}, u32[]{:S(2)}) collective-permute-start(f32[30,2,2,256]{3,2,1,0:T(2,128)S(1)} %maximum_bitcast_fusion), channel_id=1, source_target_pairs={{0,64},{64,128},{128,192},{192,0},{1,65},{65,129},{129,193},{193,1... | collective-permute-start | bytes 368648 | tf_op jit(solution)/shard_map/ppermute | solution.py:473
  78.9 2.7 %collective-permute-start.3 = (f32[30,2,2,256]{3,2,1,0:T(2,128)S(1)}, f32[30,2,2,256]{3,2,1,0:T(2,128)S(1)}, u32[]{:S(2)}, u32[]{:S(2)}) collective-permute-start(f32[30,2,2,256]{3,2,1,0:T(2,128)S(1)} %maximum_bitcast_fusion), channel_id=1, source_target_pairs={{0,128},{64,192},{128,0},{192,64},{1,129},{65,193},{129,1},{193,65... | collective-permute-start | bytes 368648 | tf_op jit(solution)/shard_map/ppermute | solution.py:473
  81.6 0.8 collective-permute-start.2
  82.4 1.3 collective-permute-done.4
  83.8 3.5 %collective-permute-done.3 = f32[30,2,2,256]{3,2,1,0:T(2,128)S(1)} collective-permute-done((f32[30,2,2,256]{3,2,1,0:T(2,128)S(1)}, f32[30,2,2,256]{3,2,1,0:T(2,128)S(1)}, u32[]{:S(2)}, u32[]{:S(2)}) %collective-permute-start.3) | collective-permute-done | bytes 122912 | tf_op jit(solution)/shard_map/ppermute | solution.py:473
  87.3 0.8 concatenate.21
  88.2 4.6 %collective-permute-start.5 = (f32[30,2,8,256]{3,2,1,0:T(8,128)S(1)}, f32[30,2,8,256]{3,2,1,0:T(8,128)S(1)}, u32[]{:S(2)}, u32[]{:S(2)}) collective-permute-start(f32[30,2,8,256]{3,2,1,0:T(8,128)S(1)} %constant_dynamic-slice_fusion.1.own_ref), channel_id=1, source_target_pairs={{0,1},{1,2},{2,3},{3,4},{4,5},{5,6},{6,7},{7,8},{8,9},{9,10},{10,1... | collective-permute-start | bytes 1474568 | tf_op jit(solution)/shard_map/ppermute | solution.py:460
  92.8 1.9 %collective-permute-start.6 = (f32[30,1,8,256]{3,2,1,0:T(8,128)S(1)}, f32[30,1,8,256]{3,2,1,0:T(8,128)S(1)}, u32[]{:S(2)}, u32[]{:S(2)}) collective-permute-start(f32[30,1,8,256]{3,2,1,0:T(8,128)S(1)} %constant_dynamic-slice_fusion), channel_id=1, source_target_pairs={{1,0},{2,1},{3,2},{4,3},{5,4},{6,5},{7,6},{8,7},{9,8},{10,9},{11,1... | collective-permute-start | bytes 737288 | tf_op jit(solution)/shard_map/ppermute | solution.py:460
  94.7 5.6 %collective-permute-done.6.high_ref = f32[30,1,8,256]{3,2,1,0:T(8,128)S(1)} collective-permute-done((f32[30,1,8,256]{3,2,1,0:T(8,128)S(1)}, f32[30,1,8,256]{3,2,1,0:T(8,128)S(1)}, u32[]{:S(2)}, u32[]{:S(2)}) %collective-permute-start.6) | collective-permute-done | bytes 245792 | tf_op jit(solution)/shard_map/ppermute | solution.py:460
  100.7 1.9 %collective-permute-start.8 = (f32[3,2,8,256]{3,2,1,0:T(8,128)S(1)}, f32[3,2,8,256]{3,2,1,0:T(8,128)S(1)}, u32[]{:S(2)}, u32[]{:S(2)}) collective-permute-start(f32[3,2,8,256]{3,2,1,0:T(8,128)S(1)} %get-tuple-element.16.v1_ref), channel_id=1, source_target_pairs={{1,0},{2,1},{3,2},{4,3},{5,4},{6,5},{7,6},{8,7},{9,8},{10,9},{11,1... | collective-permute-start | bytes 147464 | tf_op jit(solution)/shard_map/ppermute | solution.py:460
  102.6 3.6 %collective-permute-start.7 = (f32[3,2,8,256]{3,2,1,0:T(8,128)S(1)}, f32[3,2,8,256]{3,2,1,0:T(8,128)S(1)}, u32[]{:S(2)}, u32[]{:S(2)}) collective-permute-start(f32[3,2,8,256]{3,2,1,0:T(8,128)S(1)} %get-tuple-element.16.v1_ref), channel_id=1, source_target_pairs={{0,1},{1,2},{2,3},{3,4},{4,5},{5,6},{6,7},{7,8},{8,9},{9,10},{10,1... | collective-permute-start | bytes 147464 | tf_op jit(solution)/shard_map/ppermute | solution.py:460
  106.3 1.1 collective-permute-done.7.v1_low_ref
  107.9 21.2 %all_to_all.20 = f32[64,1,128]{2,1,0:T(1,128)S(1)} all-to-all(f32[64,1,128]{2,1,0:T(1,128)S(1)} %broadcast_in_dim.30), channel_id=1, replica_groups=mesh['macro'=4,'micro_0'=4,'micro_1'=8,'micro_2'=2] {'micro_0','micro_1'..., dimensions={0} | all-to-all | bytes 65536 | tf_op jit(solution)/shard_map/all_to_all | solution.py:466
  129.5 2.6 %collective-permute-start.10 = (f32[3,2,8,256]{3,2,1,0:T(8,128)S(1)}, f32[3,2,8,256]{3,2,1,0:T(8,128)S(1)}, u32[]{:S(2)}, u32[]{:S(2)}) collective-permute-start(f32[3,2,8,256]{3,2,1,0:T(8,128)S(1)} %get-tuple-element.22.w3_ref), channel_id=1, source_target_pairs={{1,0},{2,1},{3,2},{4,3},{5,4},{6,5},{7,6},{8,7},{9,8},{10,9},{11,1... | collective-permute-start | bytes 147464 | tf_op jit(solution)/shard_map/ppermute | solution.py:460
  132.0 3.0 %collective-permute-start.9 = (f32[3,2,8,256]{3,2,1,0:T(8,128)S(1)}, f32[3,2,8,256]{3,2,1,0:T(8,128)S(1)}, u32[]{:S(2)}, u32[]{:S(2)}) collective-permute-start(f32[3,2,8,256]{3,2,1,0:T(8,128)S(1)} %get-tuple-element.22.w3_ref), channel_id=1, source_target_pairs={{0,1},{1,2},{2,3},{3,4},{4,5},{5,6},{6,7},{7,8},{8,9},{9,10},{10,1... | collective-permute-start | bytes 147464 | tf_op jit(solution)/shard_map/ppermute | solution.py:460
  135.0 1.1 collective-permute-done.9.w3_low_ref
  136.2 0.8 fourth_rows.1
  137.6 7.9 %all-to-all-start.3 = ((f32[64,1,128]{2,1,0:T(1,128)}), f32[64,1,128]{2,1,0:T(1,128)S(1)}, u32[]{:S(2)}, u32[]{:S(2)}) async-start(f32[64,1,128]{2,1,0:T(1,128)} %broadcast_in_dim.32), calls=%async_computation.3 | async-start | bytes 65536 | tf_op jit(solution)/shard_map/all_to_all | solution.py:466
  145.5 9.3 %all-to-all-done.3 = f32[64,1,128]{2,1,0:T(1,128)S(1)} async-done(((f32[64,1,128]{2,1,0:T(1,128)}), f32[64,1,128]{2,1,0:T(1,128)S(1)}, u32[]{:S(2)}, u32[]{:S(2)}) %all-to-all-start.3) | async-done | bytes 32800 | tf_op jit(solution)/shard_map/all_to_all | solution.py:466
  (91 shorter events, 9.5 us)
Async XLA Ops:
  0.6 6.6 %copy-start.6 = (s32[1,1,1024,1]{2,3,1,0:T(1,128)S(1)}, s32[1,1,1024,1]{2,3,1,0:T(1,128)}, u32[]{:S(2)}) copy-start(s32[1,1,1024,1]{2,3,1,0:T(1,128)} %param.16) | copy-start | bytes 12292
  1.3 6.4 %collective-permute-start = (f32[3,1,2,256]{3,2,1,0:T(2,128)S(1)}, f32[3,1,2,256]{3,2,1,0:T(2,128)S(1)}, u32[]{:S(2)}, u32[]{:S(2)}) collective-permute-start(f32[3,1,2,256]{3,2,1,0:T(2,128)S(1)} %slice.60), channel_id=1, source_target_pairs={{64,0},{128,64},{192,128},{65,1},{129,65},{193,129},{66,2},{130,66... | collective-permute-start | bytes 18440 | tf_op jit(solution)/shard_map/ppermute | solution.py:511
  3.3 4.1 %copy-start.5 = (bf16[1,6,512]{2,1,0:T(8,128)(2,1)S(1)}, bf16[1,6,512]{2,1,0:T(8,128)(2,1)}, u32[]{:S(2)}) copy-start(bf16[1,6,512]{2,1,0:T(8,128)(2,1)} %param.20) | copy-start | bytes 18436
  5.4 2.3 %copy-start.10 = (f32[32]{0:T(128)S(1)}, f32[32]{0:T(128)}, u32[]{:S(2)}) copy-start(f32[32]{0:T(128)} %constant.69.clone) | copy-start | bytes 388
  5.4 2.3 %copy-start.7 = (f32[32]{0:T(128)S(1)}, f32[32]{0:T(128)}, u32[]{:S(2)}) copy-start(f32[32]{0:T(128)} %constant.70.clone) | copy-start | bytes 388
  5.4 2.3 %copy-start.8 = (f32[32]{0:T(128)S(1)}, f32[32]{0:T(128)}, u32[]{:S(2)}) copy-start(f32[32]{0:T(128)} %constant.68.clone) | copy-start | bytes 388
  5.4 2.3 %copy-start.9 = (f32[32]{0:T(128)S(1)}, f32[32]{0:T(128)}, u32[]{:S(2)}) copy-start(f32[32]{0:T(128)} %constant.67.clone) | copy-start | bytes 388
  5.4 2.3 %copy-start.3 = (f32[3,2,2,256]{3,2,1,0:T(2,128)S(1)}, f32[3,2,2,256]{3,2,1,0:T(2,128)}, u32[]{:S(2)}) copy-start(f32[3,2,2,256]{3,2,1,0:T(2,128)} %param.14) | copy-start | bytes 36868
  5.4 7.5 %copy-start.2 = (bf16[1,512,6]{1,2,0:T(8,128)(2,1)S(1)}, bf16[1,512,6]{1,2,0:T(8,128)(2,1)}, u32[]{:S(2)}) copy-start(bf16[1,512,6]{1,2,0:T(8,128)(2,1)} %param.21) | copy-start | bytes 18436
  7.8 6.3 %collective-permute-start.1 = (f32[3,3,1,256]{3,2,1,0:T(1,128)S(1)}, f32[3,3,1,256]{3,2,1,0:T(1,128)S(1)}, u32[]{:S(2)}, u32[]{:S(2)}) collective-permute-start(f32[3,3,1,256]{3,2,1,0:T(1,128)S(1)} %slice.159), channel_id=1, source_target_pairs={{1,0},{2,1},{3,2},{4,3},{5,4},{6,5},{7,6},{8,7},{9,8},{10,9},{11,1... | collective-permute-start | bytes 27656 | tf_op jit(solution)/shard_map/ppermute | solution.py:511
  18.0 23.6 %copy-start = (bf16[1,512,512]{2,1,0:T(8,128)(2,1)S(1)}, bf16[1,512,512]{2,1,0:T(8,128)(2,1)}, u32[]{:S(2)}) copy-start(bf16[1,512,512]{2,1,0:T(8,128)(2,1)} %param.18) | copy-start | bytes 1572868
  18.1 23.6 %copy-start.1 = (bf16[1,512,512]{2,1,0:T(8,128)(2,1)S(1)}, bf16[1,512,512]{2,1,0:T(8,128)(2,1)}, u32[]{:S(2)}) copy-start(bf16[1,512,512]{2,1,0:T(8,128)(2,1)} %param.19) | copy-start | bytes 1572868
  19.4 21.9 %all-to-all-start = ((f32[64,1,224]{2,1,0:T(1,128)}), f32[64,1,224]{2,1,0:T(1,128)S(1)}, u32[]{:S(2)}, u32[]{:S(2)}) async-start(f32[64,1,224]{2,1,0:T(1,128)} %copy.45), calls=%async_computation | async-start | bytes 131072 | tf_op jit(solution)/shard_map/all_to_all | solution.py:550
  55.5 5.6 %copy-start.4 = (f32[3,2,2,256]{3,2,1,0:T(2,128)S(1)}, f32[3,2,2,256]{3,2,1,0:T(2,128)}, u32[]{:S(2)}) copy-start(f32[3,2,2,256]{3,2,1,0:T(2,128)} %param.15) | copy-start | bytes 36868
  56.7 15.7 %all-to-all-start.1 = ((f32[64,1,864]{2,1,0:T(1,128)}), f32[64,1,864]{2,1,0:T(1,128)S(1)}, u32[]{:S(2)}, u32[]{:S(2)}) async-start(f32[64,1,864]{2,1,0:T(1,128)} %copy.51), calls=%async_computation.1 | async-start | bytes 458752 | tf_op jit(solution)/shard_map/all_to_all | solution.py:562
  76.7 7.1 %collective-permute-start.4 = (f32[30,2,2,256]{3,2,1,0:T(2,128)S(1)}, f32[30,2,2,256]{3,2,1,0:T(2,128)S(1)}, u32[]{:S(2)}, u32[]{:S(2)}) collective-permute-start(f32[30,2,2,256]{3,2,1,0:T(2,128)S(1)} %maximum_bitcast_fusion), channel_id=1, source_target_pairs={{0,64},{64,128},{128,192},{192,0},{1,65},{65,129},{129,193},{193,1... | collective-permute-start | bytes 368648 | tf_op jit(solution)/shard_map/ppermute | solution.py:473
  78.9 8.4 %collective-permute-start.3 = (f32[30,2,2,256]{3,2,1,0:T(2,128)S(1)}, f32[30,2,2,256]{3,2,1,0:T(2,128)S(1)}, u32[]{:S(2)}, u32[]{:S(2)}) collective-permute-start(f32[30,2,2,256]{3,2,1,0:T(2,128)S(1)} %maximum_bitcast_fusion), channel_id=1, source_target_pairs={{0,128},{64,192},{128,0},{192,64},{1,129},{65,193},{129,1},{193,65... | collective-permute-start | bytes 368648 | tf_op jit(solution)/shard_map/ppermute | solution.py:473
  81.6 5.7 %collective-permute-start.2 = (f32[30,2,2,256]{3,2,1,0:T(2,128)S(1)}, f32[30,2,2,256]{3,2,1,0:T(2,128)S(1)}, u32[]{:S(2)}, u32[]{:S(2)}) collective-permute-start(f32[30,2,2,256]{3,2,1,0:T(2,128)S(1)} %maximum_bitcast_fusion), channel_id=1, source_target_pairs={{0,192},{64,0},{128,64},{192,128},{1,193},{65,1},{129,65},{193,129... | collective-permute-start | bytes 368648 | tf_op jit(solution)/shard_map/ppermute | solution.py:473
  88.2 12.1 %collective-permute-start.5 = (f32[30,2,8,256]{3,2,1,0:T(8,128)S(1)}, f32[30,2,8,256]{3,2,1,0:T(8,128)S(1)}, u32[]{:S(2)}, u32[]{:S(2)}) collective-permute-start(f32[30,2,8,256]{3,2,1,0:T(8,128)S(1)} %constant_dynamic-slice_fusion.1.own_ref), channel_id=1, source_target_pairs={{0,1},{1,2},{2,3},{3,4},{4,5},{5,6},{6,7},{7,8},{8,9},{9,10},{10,1... | collective-permute-start | bytes 1474568 | tf_op jit(solution)/shard_map/ppermute | solution.py:460
  92.8 7.5 %collective-permute-start.6 = (f32[30,1,8,256]{3,2,1,0:T(8,128)S(1)}, f32[30,1,8,256]{3,2,1,0:T(8,128)S(1)}, u32[]{:S(2)}, u32[]{:S(2)}) collective-permute-start(f32[30,1,8,256]{3,2,1,0:T(8,128)S(1)} %constant_dynamic-slice_fusion), channel_id=1, source_target_pairs={{1,0},{2,1},{3,2},{4,3},{5,4},{6,5},{7,6},{8,7},{9,8},{10,9},{11,1... | collective-permute-start | bytes 737288 | tf_op jit(solution)/shard_map/ppermute | solution.py:460
  100.7 5.6 %collective-permute-start.8 = (f32[3,2,8,256]{3,2,1,0:T(8,128)S(1)}, f32[3,2,8,256]{3,2,1,0:T(8,128)S(1)}, u32[]{:S(2)}, u32[]{:S(2)}) collective-permute-start(f32[3,2,8,256]{3,2,1,0:T(8,128)S(1)} %get-tuple-element.16.v1_ref), channel_id=1, source_target_pairs={{1,0},{2,1},{3,2},{4,3},{5,4},{6,5},{7,6},{8,7},{9,8},{10,9},{11,1... | collective-permute-start | bytes 147464 | tf_op jit(solution)/shard_map/ppermute | solution.py:460
  102.6 4.8 %collective-permute-start.7 = (f32[3,2,8,256]{3,2,1,0:T(8,128)S(1)}, f32[3,2,8,256]{3,2,1,0:T(8,128)S(1)}, u32[]{:S(2)}, u32[]{:S(2)}) collective-permute-start(f32[3,2,8,256]{3,2,1,0:T(8,128)S(1)} %get-tuple-element.16.v1_ref), channel_id=1, source_target_pairs={{0,1},{1,2},{2,3},{3,4},{4,5},{5,6},{6,7},{7,8},{8,9},{9,10},{10,1... | collective-permute-start | bytes 147464 | tf_op jit(solution)/shard_map/ppermute | solution.py:460
  129.5 5.6 %collective-permute-start.10 = (f32[3,2,8,256]{3,2,1,0:T(8,128)S(1)}, f32[3,2,8,256]{3,2,1,0:T(8,128)S(1)}, u32[]{:S(2)}, u32[]{:S(2)}) collective-permute-start(f32[3,2,8,256]{3,2,1,0:T(8,128)S(1)} %get-tuple-element.22.w3_ref), channel_id=1, source_target_pairs={{1,0},{2,1},{3,2},{4,3},{5,4},{6,5},{7,6},{8,7},{9,8},{10,9},{11,1... | collective-permute-start | bytes 147464 | tf_op jit(solution)/shard_map/ppermute | solution.py:460
  132.0 4.2 %collective-permute-start.9 = (f32[3,2,8,256]{3,2,1,0:T(8,128)S(1)}, f32[3,2,8,256]{3,2,1,0:T(8,128)S(1)}, u32[]{:S(2)}, u32[]{:S(2)}) collective-permute-start(f32[3,2,8,256]{3,2,1,0:T(8,128)S(1)} %get-tuple-element.22.w3_ref), channel_id=1, source_target_pairs={{0,1},{1,2},{2,3},{3,4},{4,5},{5,6},{6,7},{7,8},{8,9},{9,10},{10,1... | collective-permute-start | bytes 147464 | tf_op jit(solution)/shard_map/ppermute | solution.py:460
  137.6 17.2 %all-to-all-start.3 = ((f32[64,1,128]{2,1,0:T(1,128)}), f32[64,1,128]{2,1,0:T(1,128)S(1)}, u32[]{:S(2)}, u32[]{:S(2)}) async-start(f32[64,1,128]{2,1,0:T(1,128)} %broadcast_in_dim.32), calls=%async_computation.3 | async-start | bytes 65536 | tf_op jit(solution)/shard_map/all_to_all | solution.py:466

commit v2 on v1

v2 whole, which is shorter than its diff:
```python
import jax
import jax.numpy as jnp
import numpy as np
from jax import lax
from jax.experimental import pallas as pl
from jax.experimental.pallas import tpu as pltpu
from jax.sharding import Mesh
from jax.sharding import PartitionSpec as P

ITMAX = 4
MICRO = ("micro_0", "micro_1", "micro_2")

BETA = 0.1
OMEGA = 0.8
MASS = 0.1
VOIGT = ((0, 5, 4), (5, 1, 3), (4, 3, 2))
PAIRS = tuple((i, j) for i in range(6) for j in range(i, 6))
TANGENT = {}
for number, (i, j) in enumerate(PAIRS):
    TANGENT[i, j] = TANGENT[j, i] = 6 + number
ROWS = 27
LOAD = 27
FIELDS = 30
DOTS = 128
BASIS = 3.2
MARK = 7 * 32 - 128
F32 = jnp.float32
BF16 = jnp.bfloat16


def three_parts(value):
    high = value.astype(BF16)
    rest = value - high.astype(F32)
    middle = rest.astype(BF16)
    return high, middle, (rest - middle.astype(F32)).astype(BF16)


def hot_rows(count, index):
    return lax.broadcasted_iota(jnp.int32, (count, index.shape[1]), 0) == index


def dispatch_kernel(
    mark_ref, routes_ref, counts_ref, own_ref, right_ref, above_ref, corner_ref, send_ref, place_ref
):
    owners = send_ref.shape[0]
    depth = own_ref.shape[3]
    capacity = 32
    column = lax.broadcasted_iota(jnp.int32, (3, depth), 1)
    sums, diffs = {}, {}
    for x in range(3):
        for y in range(3):
            ref = ((own_ref, above_ref), (right_ref, corner_ref))[x // 2][y // 2]
            node = ref[:, x % 2, y % 2, :]
            after = jnp.where(column == depth - 1, 0.0, pltpu.roll(node, depth - 1, 1))
            sums[x, y] = node + after
            diffs[x, y] = after - node
    blocks = []
    for x in range(2):
        for y in range(2):
            s00, s01, s10, s11 = sums[x, y], sums[x, y + 1], sums[x + 1, y], sums[x + 1, y + 1]
            grad_x = 0.25 * ((s10 + s11) - (s00 + s01))
            grad_y = 0.25 * ((s01 + s11) - (s00 + s10))
            grad_z = 0.25 * (
                (diffs[x, y] + diffs[x, y + 1]) + (diffs[x + 1, y] + diffs[x + 1, y + 1])
            )
            blocks.append(
                jnp.concatenate(
                    [
                        grad_x[0:1],
                        grad_y[1:2],
                        grad_z[2:3],
                        grad_z[1:2] + grad_y[2:3],
                        grad_z[0:1] + grad_x[2:3],
                        grad_y[0:1] + grad_x[1:2],
                    ],
                    axis=0,
                )
            )
    values = jnp.concatenate(blocks, axis=1)
    owner = routes_ref[...]
    chosen = jnp.where(hot_rows(owners, owner), 1.0, 0.0)
    pieces = [chosen[:, k * depth : (k + 1) * depth] for k in range(4)]
    earlier = lax.broadcasted_iota(jnp.int32, (depth, depth), 0) < lax.broadcasted_iota(
        jnp.int32, (depth, depth), 1
    )
    within = jnp.dot(
        jnp.concatenate(pieces, axis=0).astype(BF16),
        jnp.where(earlier, 1.0, 0.0).astype(BF16),
        preferred_element_type=F32,
    )
    running = jnp.zeros((owners, 1), F32)
    ranks = []
    for k in range(4):
        seen = within[k * owners : (k + 1) * owners] + running
        ranks.append(jnp.sum(pieces[k] * seen, axis=0, keepdims=True))
        running = running + jnp.sum(pieces[k], axis=1, keepdims=True)
    rank = jnp.concatenate(ranks, axis=1).astype(jnp.int32)
    place_ref[0:1] = owner
    place_ref[1:2] = rank
    at_rank = hot_rows(capacity, rank)
    leaving = jnp.concatenate([values, counts_ref[...].astype(F32)], axis=0)
    chosen = chosen.astype(BF16)
    total = None
    for part in three_parts(leaving):
        part = part.astype(F32)
        spread = [jnp.where(at_rank, part[c : c + 1], 0.0) for c in range(7)]
        spread.append(jnp.zeros_like(spread[0]))
        term = lax.dot_general(
            chosen,
            jnp.concatenate(spread, axis=0).astype(BF16),
            (((1,), (1,)), ((), ())),
            preferred_element_type=F32,
        )
        total = term if total is None else total + term
    lane = lax.broadcasted_iota(jnp.int32, (owners, 128), 1)
    send_ref[:, 0, :] = total[:, :128]
    send_ref[:, 1, :] = jnp.where(lane >= MARK, mark_ref[...], total[:, 128:])


def micro_kernel(
    got_ref,
    stiff_ref,
    pre_ref,
    force_ref,
    couple_ref,
    products_ref,
    cols_ref,
    out_ref,
    marks_ref,
    points_ref,
):
    tile = pl.program_id(0)
    owners = got_ref.shape[0]

    @pl.when(tile == 0)
    def _():
        points_ref[:128] = got_ref[:, 0, :].T
        second = got_ref[:, 1, :]
        points_ref[128:] = second.T
        marks_ref[...] = jnp.sum(second, axis=0, keepdims=True)

    stiff = stiff_ref[...]
    pre = pre_ref[...]
    halves = 2
    parts, loads, modes, sweeps = [], [], [], []
    for h in range(halves):
        part = jnp.concatenate(
            [points_ref[pl.ds(tile * 8 + h * 4 + k, 8, stride=32), :] for k in range(4)], axis=1
        )
        parts.append(part)
        loads.append(jnp.dot(force_ref[...], part.astype(BF16), preferred_element_type=F32))
        sweeps.append(part[6:7])
    for h in range(halves):
        modes.append(OMEGA * jnp.dot(pre, loads[h].astype(BF16), preferred_element_type=F32))
    for sweep in range(1, ITMAX):
        misfits = []
        for h in range(halves):
            misfit = (
                jnp.dot(stiff, modes[h].astype(BF16), preferred_element_type=F32)
                + BETA * jnp.tanh(modes[h])
                - loads[h]
            )
            misfits.append(misfit.astype(BF16))
        for h in range(halves):
            update = modes[h] - OMEGA * jnp.dot(pre, misfits[h], preferred_element_type=F32)
            modes[h] = jnp.where(sweeps[h] > sweep, update, modes[h])
    couple = couple_ref[...]
    products = products_ref[...]
    high = products.astype(BF16)
    low = (products - high.astype(F32)).astype(BF16)
    cols = cols_ref[...]
    for h in range(halves):
        bent = jnp.tanh(modes[h])
        slope = 1.0 - bent * bent
        slope_high = slope.astype(BF16)
        slope_low = (slope - slope_high.astype(F32)).astype(BF16)
        rows = (
            jnp.dot(couple, modes[h].astype(BF16), preferred_element_type=F32)
            + jnp.dot(high, slope_high, preferred_element_type=F32)
            + jnp.dot(low, slope_high, preferred_element_type=F32)
            + jnp.dot(high, slope_low, preferred_element_type=F32)
            + cols[:, 0:1]
        )
        part = parts[h]
        trace = part[0:1] + part[1:2] + part[2:3]
        elastic = cols[:8, 1:2] * trace + cols[:8, 2:3] * part
        rows = jnp.concatenate([rows[:8] + elastic, rows[8:]], axis=0)
        turned = []
        for k in range(2):
            pair = rows[:, k * 2 * owners : (k + 1) * 2 * owners].T
            turned += [pair[:owners], pair[owners:]]
        out_ref[:, pl.ds(tile * 2 + h, 1), :] = jnp.concatenate(turned, axis=1)[:, None, :]


def micro_solve(got, stiffness, precond, forcing, coupling, lame_first, lame_shear):
    modes = stiffness.shape[0]
    owners = got.shape[0]
    force = jnp.pad(forcing, ((0, 2), (0, 0))).T
    wide = coupling.astype(F32).T
    products = jnp.pad(jnp.stack([wide[i] * wide[j] for i, j in PAIRS]), ((6, 5), (0, 0)))
    couple = jnp.pad(coupling.T, ((0, 26), (0, 0)))
    base_first = [0.0] * 6 + [float(i < 3 and j < 3) for i, j in PAIRS] + [0.0] * 5
    base_shear = (
        [0.0] * 6
        + [2.0 * float(i == j and i < 3) + float(i == j and i >= 3) for i, j in PAIRS]
        + [0.0] * 5
    )
    on_trace = [1.0] * 3 + [0.0] * 29
    on_strain = [2.0] * 3 + [1.0] * 3 + [0.0] * 26
    firsts = np.zeros((32, 8), np.float32)
    shears = np.zeros((32, 8), np.float32)
    firsts[:, 0], firsts[:, 1] = base_first, on_trace
    shears[:, 0], shears[:, 2] = base_shear, on_strain
    cols = lame_first * firsts + lame_shear * shears
    whole = lambda *shape: pl.BlockSpec(shape, lambda step: (0,) * len(shape))
    return pl.pallas_call(
        micro_kernel,
        grid=(4,),
        in_specs=[
            whole(owners, 2, 128),
            whole(modes, modes),
            whole(modes, modes),
            whole(modes, 8),
            whole(32, modes),
            whole(32, modes),
            whole(32, 8),
        ],
        out_specs=[whole(owners, 8, 128), whole(1, 128)],
        out_shape=[
            jax.ShapeDtypeStruct((owners, 8, 128), F32),
            jax.ShapeDtypeStruct((1, 128), F32),
        ],
        scratch_shapes=[pltpu.VMEM((256, owners), F32)],
        compiler_params=pltpu.CompilerParams(vmem_limit_bytes=48 * 1024 * 1024),
        name="micro_solve",
    )(got, stiffness, precond, force, couple, products, cols)


def pick_kernel(back_ref, place_ref, load_ref, out_ref):
    owners = back_ref.shape[0]
    depth = out_ref.shape[3]
    owner = place_ref[0:1]
    rank = place_ref[1:2]
    chosen = jnp.where(hot_rows(owners, owner), 1.0, 0.0).astype(BF16)
    chosen = jnp.concatenate([chosen] * 3, axis=0)
    total = jnp.zeros((32, owner.shape[1]), F32)
    for s in range(8):
        turned = back_ref[:, s, :].T
        split = jnp.concatenate(three_parts(turned), axis=1)
        candidates = jnp.dot(split, chosen, preferred_element_type=F32)
        for k in range(4):
            total = total + jnp.where(
                rank == s * 4 + k, candidates[k * 32 : (k + 1) * 32], 0.0
            )
    for x in range(2):
        for y in range(2):
            at = (x * 2 + y) * depth
            out_ref[:ROWS, y, x, :] = total[:ROWS, at : at + depth]
            out_ref[ROWS:, y, x, :] = load_ref[:, x, y, :]


def shifts(shape):
    plane = lax.broadcasted_iota(jnp.int32, shape, 0)
    column = lax.broadcasted_iota(jnp.int32, shape, 1)
    planes, columns = shape

    def next_x(v):
        return jnp.where(plane == planes - 1, 0.0, pltpu.roll(v, planes - 1, 0))

    def prev_x(v):
        return jnp.where(plane == 0, 0.0, pltpu.roll(v, 1, 0))

    def next_z(v):
        return jnp.where(column == columns - 1, 0.0, pltpu.roll(v, columns - 1, 1))

    def prev_z(v):
        return jnp.where(column == 0, 0.0, pltpu.roll(v, 1, 1))

    return next_x, prev_x, next_z, prev_z


def strain_rows(nodes, lower, upper, moves):
    next_x, _, next_z, _ = moves
    sums, diffs = {}, {}
    for y in range(lower, upper + 2):
        for c in range(3):
            v = nodes[y][c]
            w = next_z(v)
            sums[y, c] = v + w
            diffs[y, c] = w - v
    strain = {}
    for y in range(lower, upper + 1):
        grad = []
        for c in range(3):
            both = sums[y, c] + sums[y + 1, c]
            rise = sums[y + 1, c] - sums[y, c]
            turn = diffs[y, c] + diffs[y + 1, c]
            grad.append(
                (
                    0.25 * (next_x(both) - both),
                    0.25 * (next_x(rise) + rise),
                    0.25 * (next_x(turn) + turn),
                )
            )
        strain[y] = (
            grad[0][0],
            grad[1][1],
            grad[2][2],
            grad[1][2] + grad[2][1],
            grad[0][2] + grad[2][0],
            grad[0][1] + grad[1][0],
        )
    return strain


def force_rows(stress, lower, upper, moves):
    _, prev_x, _, prev_z = moves
    xs = {}
    for y in range(lower - 1, upper + 1):
        for c in range(3):
            a, b, d = (stress[y][VOIGT[c][k]] for k in range(3))
            xs[y, c] = (prev_x(a) - a, prev_x(b) + b, prev_x(d) + d)
    force = {}
    for y in range(lower, upper + 1):
        parts = []
        for c in range(3):
            a0, b0, d0 = xs[y - 1, c]
            a1, b1, d1 = xs[y, c]
            flat = (a0 + a1) + (b0 - b1)
            deep = d0 + d1
            parts.append(0.25 * (prev_z(flat + deep) + (flat - deep)))
        force[y] = tuple(parts)
    return force


def apply_rows(nodes, tangent, lower, upper, moves):
    strain = strain_rows(nodes, lower - 1, upper, moves)
    stress = {}
    for y in range(lower - 1, upper + 1):
        rows = []
        for i in range(6):
            total = tangent(y, TANGENT[i, 0]) * strain[y][0]
            for j in range(1, 6):
                total = total + tangent(y, TANGENT[i, j]) * strain[y][j]
            rows.append(total)
        stress[y] = tuple(rows)
    force = force_rows(stress, lower, upper, moves)
    return {
        y: tuple(MASS * nodes[y][c] + force[y][c] for c in range(3))
        for y in range(lower, upper + 1)
    }


def value_reader(low_ref, own_ref, high_ref):
    def read(y, c):
        if y < 0:
            return low_ref[c, y + 2]
        if y < 2:
            return own_ref[c, y]
        return high_ref[c, y - 2]

    return read


def read_rows(ref, lower, count):
    return {lower + k: tuple(ref[c, k] for c in range(3)) for k in range(count)}


def inside(rows, y, last_ref):
    keep = jnp.where(last_ref[0] == 1, 0.0, 1.0)
    rows[y] = tuple(v * keep for v in rows[y])


def write_rows(ref, rows, lower, count):
    for k in range(count):
        for c in range(3):
            ref[c, k] = rows[lower + k][c]


def row_dot(first, second):
    total = None
    for y in (0, 1):
        for c in range(3):
            term = first[y][c] * second[y][c]
            total = term if total is None else total + term
    return total


def pack_dots(ref, products):
    lane = lax.broadcasted_iota(jnp.int32, (1, DOTS), 1)
    packed = jnp.zeros((1, DOTS), F32)
    for k, product in enumerate(products):
        total = jnp.sum(jnp.sum(product, axis=0, keepdims=True), axis=1, keepdims=True)
        packed = packed + jnp.where(lane == k, total, 0.0)
    ref[...] = jnp.broadcast_to(packed[None], ref.shape)


def unpack_dots(ref, count):
    row = jnp.sum(ref[...], axis=0)
    lane = lax.broadcasted_iota(jnp.int32, (1, DOTS), 1)
    return [
        jnp.sum(jnp.where(lane == k, row, 0.0), axis=1, keepdims=True) for k in range(count)
    ]


def basis_steps(marks_ref):
    lane = lax.broadcasted_iota(jnp.int32, (1, DOTS), 1)
    mark = jnp.sum(jnp.where(lane == MARK, marks_ref[...], 0.0), axis=1, keepdims=True)
    reach = 0.5 * BASIS * mark
    return MASS + reach, reach


def chebyshev(image, now, before, center, half):
    scale = 2.0 / half
    return {
        y: tuple((image[y][c] - center * now[y][c]) * scale - before[y][c] for c in range(3))
        for y in image
    }


def first_kernel(flags_ref, marks_ref, low_ref, own_ref, high_ref, v0_ref, v1_ref):
    read = value_reader(low_ref, own_ref, high_ref)
    moves = shifts(own_ref.shape[2:])
    center, half = basis_steps(marks_ref)
    stress = {y: tuple(read(y, i) for i in range(6)) for y in range(-2, 3)}
    force = force_rows(stress, -1, 2, moves)
    v0 = {y: tuple(read(y, LOAD + c) - force[y][c] for c in range(3)) for y in range(-1, 3)}
    inside(v0, 2, flags_ref)
    image = apply_rows(v0, read, 0, 1, moves)
    scale = 1.0 / half
    v1 = {y: tuple((image[y][c] - center * v0[y][c]) * scale for c in range(3)) for y in (0, 1)}
    write_rows(v0_ref, v0, -1, 4)
    write_rows(v1_ref, v1, 0, 2)


def next_two(flags_ref, marks_ref, read, moves, before, low_ref, own_ref, high_ref):
    center, half = basis_steps(marks_ref)
    now = read_rows(low_ref, -2, 2) | read_rows(own_ref, 0, 2) | read_rows(high_ref, 2, 2)
    after = chebyshev(apply_rows(now, read, -1, 2, moves), now, before, center, half)
    inside(after, 2, flags_ref)
    last = chebyshev(apply_rows(after, read, 0, 1, moves), after, now, center, half)
    return now, after, last


def second_kernel(
    flags_ref,
    marks_ref,
    low_ref,
    own_ref,
    high_ref,
    v0_ref,
    v1_low_ref,
    v1_ref,
    v1_high_ref,
    v2_ref,
    v3_ref,
):
    read = value_reader(low_ref, own_ref, high_ref)
    moves = shifts(own_ref.shape[2:])
    _, v2, v3 = next_two(
        flags_ref,
        marks_ref,
        read,
        moves,
        read_rows(v0_ref, -1, 4),
        v1_low_ref,
        v1_ref,
        v1_high_ref,
    )
    write_rows(v2_ref, v2, -1, 4)
    write_rows(v3_ref, v3, 0, 2)


def basis_pairs():
    return [(i, j) for i in range(6) for j in range(i, 6)]


def third_kernel(
    flags_ref,
    marks_ref,
    low_ref,
    own_ref,
    high_ref,
    v0_ref,
    v1_ref,
    v2_ref,
    v3_low_ref,
    v3_ref,
    v3_high_ref,
    v4_ref,
    v5_ref,
    dots_ref,
):
    read = value_reader(low_ref, own_ref, high_ref)
    moves = shifts(own_ref.shape[2:])
    v2 = read_rows(v2_ref, -1, 4)
    v3, v4, v5 = next_two(
        flags_ref, marks_ref, read, moves, v2, v3_low_ref, v3_ref, v3_high_ref
    )
    write_rows(v4_ref, v4, 0, 2)
    write_rows(v5_ref, v5, 0, 2)
    basis = [read_rows(v0_ref, -1, 4), read_rows(v1_ref, 0, 2), v2, v3, v4, v5]
    pack_dots(dots_ref, [row_dot(basis[i], basis[j]) for i, j in basis_pairs()])


def total_of(terms):
    total = None
    for term in terms:
        total = term if total is None else total + term
    return total


def fourth_kernel(
    flags_ref,
    marks_ref,
    sums_ref,
    v0_ref,
    v1_ref,
    v2_ref,
    v3_ref,
    v4_ref,
    v5_ref,
    increment_ref,
    residual_ref,
    rows_ref,
):
    center, half = basis_steps(marks_ref)
    dots = unpack_dots(sums_ref, 21)
    gram = {}
    for k, (i, j) in enumerate(basis_pairs()):
        gram[i, j] = gram[j, i] = dots[k]

    def image_of(p):
        count = len(p)
        image = []
        for i in range(count + 1):
            terms = []
            if i < count:
                terms.append(center * p[i])
            if i > 0:
                terms.append((half if i == 1 else 0.5 * half) * p[i - 1])
            if i + 1 < count:
                terms.append(0.5 * half * p[i + 1])
            image.append(total_of(terms))
        return image

    def product(p, q):
        return total_of(
            p[i] * total_of(gram[i, j] * q[j] for j in range(len(q))) for i in range(len(p))
        )

    def combine(p, factor, q):
        longer = max(len(p), len(q))
        return [
            (p[k] + factor * q[k] if k < len(p) else factor * q[k]) if k < len(q) else p[k]
            for k in range(longer)
        ]

    solved = []
    left = [jnp.ones((1, 1), F32)]
    course = left
    norm = gram[0, 0]
    for step in range(5):
        image = image_of(course)
        alpha = norm / product(course, image)
        solved = combine(solved, alpha, course)
        left = combine(left, -alpha, image)
        if step < 4:
            fresh = product(left, left)
            course = combine(left, fresh / norm, course)
            norm = fresh
    basis = [
        read_rows(v0_ref, -1, 4),
        read_rows(v1_ref, 0, 2),
        read_rows(v2_ref, -1, 4),
        read_rows(v3_ref, 0, 2),
        read_rows(v4_ref, 0, 2),
        read_rows(v5_ref, 0, 2),
    ]
    first = flags_ref[1]
    for ref, weights in ((increment_ref, solved), (residual_ref, left)):
        for y in (0, 1):
            for c in range(3):
                rows_ref[...] = total_of(w * basis[k][y][c] for k, w in enumerate(weights))
                for x in (0, 1):
                    ref[c, x, pl.ds(y, 1), :] = rows_ref[pl.ds(first + x, 1), :]


def local_call(kernel, outs, name, *args, flags=None, scratch=()):
    specs = [pl.BlockSpec(memory_space=pltpu.VMEM)] * len(args)
    if flags is not None:
        specs = [pl.BlockSpec(memory_space=pltpu.SMEM)] + specs
        args = (flags,) + args
    return pl.pallas_call(
        kernel,
        in_specs=specs,
        out_specs=[pl.BlockSpec(memory_space=pltpu.VMEM)] * len(outs),
        out_shape=[jax.ShapeDtypeStruct(*out) if isinstance(out[0], tuple) else jax.ShapeDtypeStruct(out, F32) for out in outs],
        scratch_shapes=scratch,
        compiler_params=pltpu.CompilerParams(vmem_limit_bytes=48 * 1024 * 1024),
        name=name,
    )(*args)


def up_and_down(up, down):
    count = lax.axis_size(MICRO)
    forward = [(k, k + 1) for k in range(count - 1)]
    backward = [(k + 1, k) for k in range(count - 1)]
    return lax.ppermute(up, MICRO, forward), lax.ppermute(down, MICRO, backward)


def swapped(block):
    return lax.all_to_all(block, MICRO, split_axis=0, concat_axis=0, tiled=True)


def gather_planes(block):
    count = lax.axis_size("macro")
    pieces = [block] + [
        lax.ppermute(block, "macro", [(k, (k - shift) % count) for k in range(count)])
        for shift in range(1, count)
    ]
    planes = block.shape[2]
    twice = jnp.concatenate(pieces + pieces[:-1], axis=2)
    start = (count - lax.axis_index("macro")) % count * planes
    return lax.dynamic_slice_in_dim(twice, start, count * planes, axis=2)


def shards(
    displacement,
    load,
    routes,
    counts,
    stiffness,
    precond,
    forcing,
    coupling,
    lame_first,
    lame_shear,
):
    planes, width, depth = displacement.shape[1:]
    points = planes * width * depth
    rows_x = lax.axis_size("macro")
    owners = lax.axis_size(MICRO)
    stretch = jnp.sum(jnp.square(coupling[0, :, :3].astype(F32)))
    mark = ((lame_first[0] + 2.0 * lame_shear[0] + stretch / 6.0) / owners).reshape(1, 1)
    right = lax.ppermute(displacement, "macro", [(a + 1, a) for a in range(rows_x - 1)])
    above = lax.ppermute(displacement, MICRO, [(b + 1, b) for b in range(owners - 1)])
    corner = lax.ppermute(
        displacement,
        ("macro",) + MICRO,
        [
            ((a + 1) * owners + b + 1, a * owners + b)
            for a in range(rows_x - 1)
            for b in range(owners - 1)
        ],
    )
    send, place = local_call(
        dispatch_kernel,
        ((owners, 2, 128), ((8, points), jnp.int32)),
        "dispatch",
        mark,
        routes.reshape(1, points),
        counts.reshape(1, points),
        displacement,
        right,
        above,
        corner,
    )
    back, marks = micro_solve(
        swapped(send),
        stiffness[0],
        precond[0],
        forcing[0],
        coupling[0],
        lame_first[0],
        lame_shear[0],
    )
    (values,) = local_call(
        pick_kernel, ((FIELDS, width, planes, depth),), "pick", swapped(back), place, load
    )
    own = gather_planes(values)
    low, high = up_and_down(own, own[:, :1])
    flags = jnp.stack(
        [
            (lax.axis_index(MICRO) == owners - 1).astype(jnp.int32),
            (lax.axis_index("macro") * planes).astype(jnp.int32),
        ]
    )
    sets = (marks, low, own, high)
    whole = own.shape[2]
    two = (3, 2, whole, depth)
    four = (3, 4, whole, depth)
    v0, v1 = local_call(first_kernel, (four, two), "first_rows", *sets, flags=flags)
    v1_low, v1_high = up_and_down(v1, v1)
    v2, v3 = local_call(
        second_kernel, (four, two), "second_rows", *sets, v0, v1_low, v1, v1_high, flags=flags
    )
    v3_low, v3_high = up_and_down(v3, v3)
    v4, v5, dots = local_call(
        third_kernel,
        (two, two, (owners, 1, DOTS)),
        "third_rows",
        *sets,
        v0,
        v1,
        v2,
        v3_low,
        v3,
        v3_high,
        flags=flags,
    )
    mine = (3, planes, width, depth)
    return tuple(
        local_call(
            fourth_kernel,
            (mine, mine),
            "fourth_rows",
            marks,
            swapped(dots),
            v0,
            v1,
            v2,
            v3,
            v4,
            v5,
            flags=flags,
            scratch=[pltpu.VMEM((whole, depth), F32)],
        )
    )


def solution(mesh):
    split = Mesh(
        mesh.devices.reshape(mesh.shape["macro"], 4, 8, 2),
        ("macro", "micro_0", "micro_1", "micro_2"),
    )
    placed = (
        P(None, "macro", MICRO, None),
        P(None, "macro", MICRO, None),
        P("macro", MICRO, None, None),
        P("macro", MICRO, None),
        P(MICRO, None, None),
        P(MICRO, None, None),
        P(MICRO, None, None),
        P(MICRO, None, None),
        P(MICRO),
        P(MICRO),
    )
    return jax.shard_map(
        shards,
        mesh=split,
        in_specs=placed,
        out_specs=(P(None, "macro", MICRO, None), P(None, "macro", MICRO, None)),
        check_vma=False,
    )
```

time: 157 us -> 135 us (0.86)
  waiting for transfers between devices: 43.9 us -> 21 us
  blocking collectives: 21.2 us -> 39.3 us
  starting transfers between devices: 54.2 us -> 42.2 us
  local copies, waits for them, and re-layouts: 15.2 us -> 4.05 us
  Pallas kernels: 15.7 us -> 22.4 us
  matrix products: 1.82 us -> 0 us
    all_to_all x3 -> x1, waiting for transfers between devices: 30.3 us -> 8.02 us  [swapped(): return lax.all_to_all(block, MICRO, split_axis=0, concat_axis=0, tiled=True)]
    all_to_all x1 -> x2, blocking collectives: 21.2 us -> 39.3 us  [swapped(): return lax.all_to_all(block, MICRO, split_axis=0, concat_axis=0, tiled=True)]
    all_to_all x3 -> x1, starting transfers between devices: 24.4 us -> 11.3 us  [swapped(): return lax.all_to_all(block, MICRO, split_axis=0, concat_axis=0, tiled=True)]
    pallas_call x5 -> x6, Pallas kernels: 2.2 us -> 7.62 us  [local_call(): pl.pallas_call(kernel, in_specs=specs, out_specs=[pl.BlockSpec(memory_spa...]
    scatter x1 -> x0, local copies, waits for them, and re-layouts: 3.34 us -> none  [shards(): jnp.zeros((7, slots), F32).at[:, target]]
    reshape x6 -> x0, local copies, waits for them, and re-layouts: 2.85 us -> none  [the longest x2 1.35 us: shards(): send.reshape(7, owners, capacity).transpose(1, 0, 2)]
    gather x1 -> x0, local copies, waits for them, and re-layouts: 2.81 us -> none  [shards(): picked = jnp.take(back, target, axis=1, mode='clip')]
    dot_general x1 -> x0, matrix products: 1.82 us -> none  [shards(): earlier = jnp.dot(before, chosen.astype(BF16), preferred_element_type=F32)]
  transfers between devices with their start and end apart: 14 -> 13, of which waited for: 9 -> 7; matrix products, arithmetic and copies ran while one was open for 2% -> 3% of each run, Pallas kernels for 0% -> 0%
where the time goes in v2:
time: 135 us; the launch traced here: 134 us
  starting transfers between devices  42.2 us (31%)
  blocking collectives  39.3 us (29%)
  Pallas kernels  22.4 us (17%)
  waiting for transfers between devices  21 us (16%)
  local copies, waits for them, and re-layouts  4.05 us (3%)
  between operations  2.81 us (2%)
  other arithmetic  2.22 us (2%)
    all_to_all x2, blocking collectives, swapped(): return lax.all_to_all(block, MICRO, split_axis=0, concat_axis=0, tiled=True)  39.3 us
    pallas_call x1, Pallas kernels, micro_solve(): pl.pallas_call(micro_kernel, grid=(4,), in_specs=[whole(owners, 2, 128),...  14.8 us
    ppermute x3, starting transfers between devices, up_and_down(): lax.ppermute(up, MICRO, forward)  12.2 us
    all_to_all x1, starting transfers between devices, swapped(): return lax.all_to_all(block, MICRO, split_axis=0, concat_axis=0, tiled=True)  11.3 us
    all_to_all x1, waiting for transfers between devices, swapped(): return lax.all_to_all(block, MICRO, split_axis=0, concat_axis=0, tiled=True)  8.02 us
    pallas_call x6, Pallas kernels, local_call(): pl.pallas_call(kernel, in_specs=specs, out_specs=[pl.BlockSpec(memory_spa...  7.62 us
    ppermute x3, starting transfers between devices, up_and_down(): lax.ppermute(down, MICRO, backward)  5.76 us
    ppermute x3, waiting for transfers between devices, up_and_down(): lax.ppermute(down, MICRO, backward)  5.5 us
  transfers between devices with their start and end apart: 13, of which 7 were waited for; matrix products, arithmetic and copies ran while one was open for 3% of the time, Pallas kernels for 0%

profile of v2, /device:TPU:1, one launch (start us, length us, event | category | flops | bytes accessed | tf_op | source)
XLA Modules:
  0.0 134.0 jit_solution(1677876425965212038)
XLA Ops:
  0.7 5.1 %collective-permute-start.1 = (f32[3,2,2,256]{3,2,1,0:T(2,128)}, f32[3,2,2,256]{3,2,1,0:T(2,128)S(1)}, u32[]{:S(2)}, u32[]{:S(2)}) collective-permute-start(f32[3,2,2,256]{3,2,1,0:T(2,128)} %own_ref.1), channel_id=1, source_target_pairs={{1,0},{2,1},{3,2},{4,3},{5,4},{6,5},{7,6},{8,7},{9,8},{10,9},{11,1... | collective-permute-start | bytes 36872 | tf_op jit(solution)/shard_map/ppermute | solution.py:647
  5.8 1.3 collective-permute-start
  7.1 1.3 collective-permute-start.2
  9.7 0.8 bitcast_convert_fusion
  10.6 1.3 multiply_reduce_fusion
  14.6 1.4 %dispatch.1 = (f32[64,2,128]{2,1,0:T(2,128)}, s32[8,1024]{1,0:T(8,128)S(1)}) custom-call(f32[1,1]{1,0:T(1,128)} %bitcast.4.mark_ref, s32[1,1024]{1,0:T(1,128)S(1)} %bitcast.22, s32[1,1024]{1,0:T(1,128)S(1)} %bitcast.23, f32[3,2,2,256]{3,2,1,0:T(2,128)S(1)} %copy-done.2, f32[3,2,2,256]{3,2,1,0:T(2,128)S(1)} %collective-permute-done.right_ref, ...), custom_call_target="tpu_custom_call" | custom-call | tf_op jit(solution)/shard_map/dispatch/pallas_call | solution.py:594
  16.0 11.3 %all-to-all-start = ((f32[64,2,128]{2,1,0:T(2,128)}), f32[64,2,128]{2,1,0:T(2,128)S(1)}, u32[]{:S(2)}, u32[]{:S(2)}) async-start(f32[64,2,128]{2,1,0:T(2,128)} %get-tuple-element.13), calls=%async_computation | async-start | bytes 131072 | tf_op jit(solution)/shard_map/all_to_all | solution.py:613
  27.4 0.9 copy.15
  29.1 8.0 %all-to-all-done.got_ref = f32[64,2,128]{2,1,0:T(2,128)S(1)} async-done(((f32[64,2,128]{2,1,0:T(2,128)}), f32[64,2,128]{2,1,0:T(2,128)S(1)}, u32[]{:S(2)}, u32[]{:S(2)}) %all-to-all-start) | async-done | bytes 65568 | tf_op jit(solution)/shard_map/all_to_all | solution.py:613
  37.1 14.8 %micro_solve.1 = (f32[64,8,128]{2,1,0:T(8,128)S(1)}, f32[1,128]{1,0:T(1,128)S(1)}) custom-call(f32[64,2,128]{2,1,0:T(2,128)S(1)} %all-to-all-done.got_ref, bf16[512,512]{1,0:T(8,128)(2,1)S(1)} %bitcast.20, bf16[512,512]{1,0:T(8,128)(2,1)S(1)} %bitcast.21, bf16[512,8]{1,0:T(8,128)(2,1)S(1)} %pad_bitcast_fusion.force_ref, bf16[32,512]{1,0:T(8,128)(2,1)S(1)} %pad.13.couple_ref, ...), custom_call_target="tpu_custom_call" | custom-call | tf_op jit(solution)/shard_map/micro_solve/pallas_call | solution.py:216
  51.9 15.9 %all_to_all.15.back_ref = f32[64,8,128]{2,1,0:T(8,128)S(1)} all-to-all(f32[64,8,128]{2,1,0:T(8,128)S(1)} %get-tuple-element.15), channel_id=1, replica_groups=mesh['macro'=4,'micro_0'=4,'micro_1'=8,'micro_2'=2] {'micro_0','micro_1'..., dimensions={0} | all-to-all | bytes 524288 | tf_op jit(solution)/shard_map/all_to_all | solution.py:613
  67.8 1.3 pick.1
  69.1 1.7 %collective-permute-start.5 = (f32[30,2,2,256]{3,2,1,0:T(2,128)S(1)}, f32[30,2,2,256]{3,2,1,0:T(2,128)S(1)}, u32[]{:S(2)}, u32[]{:S(2)}) collective-permute-start(f32[30,2,2,256]{3,2,1,0:T(2,128)S(1)} %pick.1), channel_id=1, source_target_pairs={{0,64},{64,128},{128,192},{192,0},{1,65},{65,129},{129,193},{193,1... | collective-permute-start | bytes 368648 | tf_op jit(solution)/shard_map/ppermute | solution.py:619
  70.8 2.4 %collective-permute-start.4 = (f32[30,2,2,256]{3,2,1,0:T(2,128)S(1)}, f32[30,2,2,256]{3,2,1,0:T(2,128)S(1)}, u32[]{:S(2)}, u32[]{:S(2)}) collective-permute-start(f32[30,2,2,256]{3,2,1,0:T(2,128)S(1)} %pick.1), channel_id=1, source_target_pairs={{0,128},{64,192},{128,0},{192,64},{1,129},{65,193},{129,1},{193,65... | collective-permute-start | bytes 368648 | tf_op jit(solution)/shard_map/ppermute | solution.py:619
  73.2 1.2 collective-permute-start.3
  74.3 0.8 collective-permute-done.5
  75.1 3.7 %collective-permute-done.4 = f32[30,2,2,256]{3,2,1,0:T(2,128)S(1)} collective-permute-done((f32[30,2,2,256]{3,2,1,0:T(2,128)S(1)}, f32[30,2,2,256]{3,2,1,0:T(2,128)S(1)}, u32[]{:S(2)}, u32[]{:S(2)}) %collective-permute-start.4) | collective-permute-done | bytes 122912 | tf_op jit(solution)/shard_map/ppermute | solution.py:619
  78.8 0.8 concatenate.3
  79.7 4.3 %collective-permute-start.6 = (f32[30,2,8,256]{3,2,1,0:T(8,128)S(1)}, f32[30,2,8,256]{3,2,1,0:T(8,128)S(1)}, u32[]{:S(2)}, u32[]{:S(2)}) collective-permute-start(f32[30,2,8,256]{3,2,1,0:T(8,128)S(1)} %constant_dynamic-slice_fusion.1.own_ref), channel_id=1, source_target_pairs={{0,1},{1,2},{2,3},{3,4},{4,5},{5,6},{6,7},{7,8},{8,9},{9,10},{10,1... | collective-permute-start | bytes 1474568 | tf_op jit(solution)/shard_map/ppermute | solution.py:609
  84.0 1.9 %collective-permute-start.7 = (f32[30,1,8,256]{3,2,1,0:T(8,128)S(1)}, f32[30,1,8,256]{3,2,1,0:T(8,128)S(1)}, u32[]{:S(2)}, u32[]{:S(2)}) collective-permute-start(f32[30,1,8,256]{3,2,1,0:T(8,128)S(1)} %constant_dynamic-slice_fusion), channel_id=1, source_target_pairs={{1,0},{2,1},{3,2},{4,3},{5,4},{6,5},{7,6},{8,7},{9,8},{10,9},{11,1... | collective-permute-start | bytes 737288 | tf_op jit(solution)/shard_map/ppermute | solution.py:609
  86.0 5.5 %collective-permute-done.7.high_ref = f32[30,1,8,256]{3,2,1,0:T(8,128)S(1)} collective-permute-done((f32[30,1,8,256]{3,2,1,0:T(8,128)S(1)}, f32[30,1,8,256]{3,2,1,0:T(8,128)S(1)}, u32[]{:S(2)}, u32[]{:S(2)}) %collective-permute-start.7) | collective-permute-done | bytes 245792 | tf_op jit(solution)/shard_map/ppermute | solution.py:609
  91.5 0.9 first_rows.1
  92.5 1.9 %collective-permute-start.9 = (f32[3,2,8,256]{3,2,1,0:T(8,128)S(1)}, f32[3,2,8,256]{3,2,1,0:T(8,128)S(1)}, u32[]{:S(2)}, u32[]{:S(2)}) collective-permute-start(f32[3,2,8,256]{3,2,1,0:T(8,128)S(1)} %get-tuple-element.18.v1_ref), channel_id=1, source_target_pairs={{1,0},{2,1},{3,2},{4,3},{5,4},{6,5},{7,6},{8,7},{9,8},{10,9},{11,1... | collective-permute-start | bytes 147464 | tf_op jit(solution)/shard_map/ppermute | solution.py:609
  94.4 3.6 %collective-permute-start.8 = (f32[3,2,8,256]{3,2,1,0:T(8,128)S(1)}, f32[3,2,8,256]{3,2,1,0:T(8,128)S(1)}, u32[]{:S(2)}, u32[]{:S(2)}) collective-permute-start(f32[3,2,8,256]{3,2,1,0:T(8,128)S(1)} %get-tuple-element.18.v1_ref), channel_id=1, source_target_pairs={{0,1},{1,2},{2,3},{3,4},{4,5},{5,6},{6,7},{7,8},{8,9},{9,10},{10,1... | collective-permute-start | bytes 147464 | tf_op jit(solution)/shard_map/ppermute | solution.py:609
  98.0 1.1 collective-permute-done.8.v1_low_ref
  99.2 1.2 second_rows.1
  100.4 1.9 %collective-permute-start.11 = (f32[3,2,8,256]{3,2,1,0:T(8,128)S(1)}, f32[3,2,8,256]{3,2,1,0:T(8,128)S(1)}, u32[]{:S(2)}, u32[]{:S(2)}) collective-permute-start(f32[3,2,8,256]{3,2,1,0:T(8,128)S(1)} %get-tuple-element.20.v3_ref), channel_id=1, source_target_pairs={{1,0},{2,1},{3,2},{4,3},{5,4},{6,5},{7,6},{8,7},{9,8},{10,9},{11,1... | collective-permute-start | bytes 147464 | tf_op jit(solution)/shard_map/ppermute | solution.py:609
  102.3 4.2 %collective-permute-start.10 = (f32[3,2,8,256]{3,2,1,0:T(8,128)S(1)}, f32[3,2,8,256]{3,2,1,0:T(8,128)S(1)}, u32[]{:S(2)}, u32[]{:S(2)}) collective-permute-start(f32[3,2,8,256]{3,2,1,0:T(8,128)S(1)} %get-tuple-element.20.v3_ref), channel_id=1, source_target_pairs={{0,1},{1,2},{2,3},{3,4},{4,5},{5,6},{6,7},{7,8},{8,9},{9,10},{10,1... | collective-permute-start | bytes 147464 | tf_op jit(solution)/shard_map/ppermute | solution.py:609
  106.6 1.1 collective-permute-done.10.v3_low_ref
  107.7 1.3 third_rows.1
  109.1 23.4 %all_to_all.16.sums_ref = f32[64,1,128]{2,1,0:T(1,128)S(1)} all-to-all(f32[64,1,128]{2,1,0:T(1,128)S(1)} %get-tuple-element.21), channel_id=1, replica_groups=mesh['macro'=4,'micro_0'=4,'micro_1'=8,'micro_2'=2] {'micro_0','micro_1'..., dimensions={0} | all-to-all | bytes 65536 | tf_op jit(solution)/shard_map/all_to_all | solution.py:613
  132.5 1.5 %fourth_rows.1 = (f32[3,2,2,256]{3,2,1,0:T(2,128)}, f32[3,2,2,256]{3,2,1,0:T(2,128)}) custom-call(s32[2]{0:T(128)S(1)} %pad_add_fusion.flags_ref, f32[1,128]{1,0:T(1,128)S(1)} %get-tuple-element.14.marks_ref, f32[64,1,128]{2,1,0:T(1,128)S(1)} %all_to_all.16.sums_ref, f32[3,4,8,256]{3,2,1,0:T(8,128)S(1)} %get-tuple-element.17.v0_ref, ...), custom_call_target="tpu_custom_call" | custom-call | tf_op jit(solution)/shard_map/fourth_rows/pallas_call | solution.py:594
  (33 shorter events, 3.2 us)
Async XLA Ops:
  0.6 9.9 %copy-start.7 = (f32[32,8]{1,0:T(8,128)S(1)}, f32[32,8]{1,0:T(8,128)}, u32[]{:S(2)}) copy-start(f32[32,8]{1,0:T(8,128)} %constant.57.clone) | copy-start | bytes 3076
  0.6 9.9 %copy-start.6 = (f32[32,8]{1,0:T(8,128)S(1)}, f32[32,8]{1,0:T(8,128)}, u32[]{:S(2)}) copy-start(f32[32,8]{1,0:T(8,128)} %constant.58.clone) | copy-start | bytes 3076
  0.7 11.8 %collective-permute-start.1 = (f32[3,2,2,256]{3,2,1,0:T(2,128)}, f32[3,2,2,256]{3,2,1,0:T(2,128)S(1)}, u32[]{:S(2)}, u32[]{:S(2)}) collective-permute-start(f32[3,2,2,256]{3,2,1,0:T(2,128)} %own_ref.1), channel_id=1, source_target_pairs={{1,0},{2,1},{3,2},{4,3},{5,4},{6,5},{7,6},{8,7},{9,8},{10,9},{11,1... | collective-permute-start | bytes 36872 | tf_op jit(solution)/shard_map/ppermute | solution.py:647
  5.8 6.7 %collective-permute-start = (f32[3,2,2,256]{3,2,1,0:T(2,128)}, f32[3,2,2,256]{3,2,1,0:T(2,128)S(1)}, u32[]{:S(2)}, u32[]{:S(2)}) collective-permute-start(f32[3,2,2,256]{3,2,1,0:T(2,128)} %own_ref.1), channel_id=1, source_target_pairs={{64,0},{128,64},{192,128},{65,1},{129,65},{193,129},{66,2},{130,66... | collective-permute-start | bytes 36872 | tf_op jit(solution)/shard_map/ppermute | solution.py:646
  7.1 6.1 %collective-permute-start.2 = (f32[3,2,2,256]{3,2,1,0:T(2,128)}, f32[3,2,2,256]{3,2,1,0:T(2,128)S(1)}, u32[]{:S(2)}, u32[]{:S(2)}) collective-permute-start(f32[3,2,2,256]{3,2,1,0:T(2,128)} %own_ref.1), channel_id=1, source_target_pairs={{65,0},{66,1},{67,2},{68,3},{69,4},{70,5},{71,6},{72,7},{73,8},{74... | collective-permute-start | bytes 36872 | tf_op jit(solution)/shard_map/ppermute | solution.py:648
  8.4 4.8 %copy-start.2 = (f32[3,2,2,256]{3,2,1,0:T(2,128)S(1)}, f32[3,2,2,256]{3,2,1,0:T(2,128)}, u32[]{:S(2)}) copy-start(f32[3,2,2,256]{3,2,1,0:T(2,128)} %own_ref.1) | copy-start | bytes 36868
  9.7 27.4 %copy-start = (bf16[1,512,512]{2,1,0:T(8,128)(2,1)S(1)}, bf16[1,512,512]{2,1,0:T(8,128)(2,1)}, u32[]{:S(2)}) copy-start(bf16[1,512,512]{2,1,0:T(8,128)(2,1)} %param.16) | copy-start | bytes 1572868
  9.7 27.4 %copy-start.1 = (bf16[1,512,512]{2,1,0:T(8,128)(2,1)S(1)}, bf16[1,512,512]{2,1,0:T(8,128)(2,1)}, u32[]{:S(2)}) copy-start(bf16[1,512,512]{2,1,0:T(8,128)(2,1)} %param.17) | copy-start | bytes 1572868
  13.2 0.7 copy-start.4
  13.9 0.7 copy-start.5
  16.0 21.1 %all-to-all-start = ((f32[64,2,128]{2,1,0:T(2,128)}), f32[64,2,128]{2,1,0:T(2,128)S(1)}, u32[]{:S(2)}, u32[]{:S(2)}) async-start(f32[64,2,128]{2,1,0:T(2,128)} %get-tuple-element.13), calls=%async_computation | async-start | bytes 131072 | tf_op jit(solution)/shard_map/all_to_all | solution.py:613
  51.9 15.9 %copy-start.3 = (f32[3,2,2,256]{3,2,1,0:T(2,128)S(1)}, f32[3,2,2,256]{3,2,1,0:T(2,128)}, u32[]{:S(2)}) copy-start(f32[3,2,2,256]{3,2,1,0:T(2,128)} %load_ref.1) | copy-start | bytes 36868
  69.1 6.0 %collective-permute-start.5 = (f32[30,2,2,256]{3,2,1,0:T(2,128)S(1)}, f32[30,2,2,256]{3,2,1,0:T(2,128)S(1)}, u32[]{:S(2)}, u32[]{:S(2)}) collective-permute-start(f32[30,2,2,256]{3,2,1,0:T(2,128)S(1)} %pick.1), channel_id=1, source_target_pairs={{0,64},{64,128},{128,192},{192,0},{1,65},{65,129},{129,193},{193,1... | collective-permute-start | bytes 368648 | tf_op jit(solution)/shard_map/ppermute | solution.py:619
  70.8 8.0 %collective-permute-start.4 = (f32[30,2,2,256]{3,2,1,0:T(2,128)S(1)}, f32[30,2,2,256]{3,2,1,0:T(2,128)S(1)}, u32[]{:S(2)}, u32[]{:S(2)}) collective-permute-start(f32[30,2,2,256]{3,2,1,0:T(2,128)S(1)} %pick.1), channel_id=1, source_target_pairs={{0,128},{64,192},{128,0},{192,64},{1,129},{65,193},{129,1},{193,65... | collective-permute-start | bytes 368648 | tf_op jit(solution)/shard_map/ppermute | solution.py:619
  73.2 5.6 %collective-permute-start.3 = (f32[30,2,2,256]{3,2,1,0:T(2,128)S(1)}, f32[30,2,2,256]{3,2,1,0:T(2,128)S(1)}, u32[]{:S(2)}, u32[]{:S(2)}) collective-permute-start(f32[30,2,2,256]{3,2,1,0:T(2,128)S(1)} %pick.1), channel_id=1, source_target_pairs={{0,192},{64,0},{128,64},{192,128},{1,193},{65,1},{129,65},{193,129... | collective-permute-start | bytes 368648 | tf_op jit(solution)/shard_map/ppermute | solution.py:619
  79.7 11.9 %collective-permute-start.6 = (f32[30,2,8,256]{3,2,1,0:T(8,128)S(1)}, f32[30,2,8,256]{3,2,1,0:T(8,128)S(1)}, u32[]{:S(2)}, u32[]{:S(2)}) collective-permute-start(f32[30,2,8,256]{3,2,1,0:T(8,128)S(1)} %constant_dynamic-slice_fusion.1.own_ref), channel_id=1, source_target_pairs={{0,1},{1,2},{2,3},{3,4},{4,5},{5,6},{6,7},{7,8},{8,9},{9,10},{10,1... | collective-permute-start | bytes 1474568 | tf_op jit(solution)/shard_map/ppermute | solution.py:609
  84.0 7.5 %collective-permute-start.7 = (f32[30,1,8,256]{3,2,1,0:T(8,128)S(1)}, f32[30,1,8,256]{3,2,1,0:T(8,128)S(1)}, u32[]{:S(2)}, u32[]{:S(2)}) collective-permute-start(f32[30,1,8,256]{3,2,1,0:T(8,128)S(1)} %constant_dynamic-slice_fusion), channel_id=1, source_target_pairs={{1,0},{2,1},{3,2},{4,3},{5,4},{6,5},{7,6},{8,7},{9,8},{10,9},{11,1... | collective-permute-start | bytes 737288 | tf_op jit(solution)/shard_map/ppermute | solution.py:609
  92.5 5.6 %collective-permute-start.9 = (f32[3,2,8,256]{3,2,1,0:T(8,128)S(1)}, f32[3,2,8,256]{3,2,1,0:T(8,128)S(1)}, u32[]{:S(2)}, u32[]{:S(2)}) collective-permute-start(f32[3,2,8,256]{3,2,1,0:T(8,128)S(1)} %get-tuple-element.18.v1_ref), channel_id=1, source_target_pairs={{1,0},{2,1},{3,2},{4,3},{5,4},{6,5},{7,6},{8,7},{9,8},{10,9},{11,1... | collective-permute-start | bytes 147464 | tf_op jit(solution)/shard_map/ppermute | solution.py:609
  94.4 4.8 %collective-permute-start.8 = (f32[3,2,8,256]{3,2,1,0:T(8,128)S(1)}, f32[3,2,8,256]{3,2,1,0:T(8,128)S(1)}, u32[]{:S(2)}, u32[]{:S(2)}) collective-permute-start(f32[3,2,8,256]{3,2,1,0:T(8,128)S(1)} %get-tuple-element.18.v1_ref), channel_id=1, source_target_pairs={{0,1},{1,2},{2,3},{3,4},{4,5},{5,6},{6,7},{7,8},{8,9},{9,10},{10,1... | collective-permute-start | bytes 147464 | tf_op jit(solution)/shard_map/ppermute | solution.py:609
  100.4 6.2 %collective-permute-start.11 = (f32[3,2,8,256]{3,2,1,0:T(8,128)S(1)}, f32[3,2,8,256]{3,2,1,0:T(8,128)S(1)}, u32[]{:S(2)}, u32[]{:S(2)}) collective-permute-start(f32[3,2,8,256]{3,2,1,0:T(8,128)S(1)} %get-tuple-element.20.v3_ref), channel_id=1, source_target_pairs={{1,0},{2,1},{3,2},{4,3},{5,4},{6,5},{7,6},{8,7},{9,8},{10,9},{11,1... | collective-permute-start | bytes 147464 | tf_op jit(solution)/shard_map/ppermute | solution.py:609
  102.3 5.4 %collective-permute-start.10 = (f32[3,2,8,256]{3,2,1,0:T(8,128)S(1)}, f32[3,2,8,256]{3,2,1,0:T(8,128)S(1)}, u32[]{:S(2)}, u32[]{:S(2)}) collective-permute-start(f32[3,2,8,256]{3,2,1,0:T(8,128)S(1)} %get-tuple-element.20.v3_ref), channel_id=1, source_target_pairs={{0,1},{1,2},{2,3},{3,4},{4,5},{5,6},{6,7},{7,8},{8,9},{9,10},{10,1... | collective-permute-start | bytes 147464 | tf_op jit(solution)/shard_map/ppermute | solution.py:609

commit v3 on v2

--- a/solution.py
+++ b/solution.py
@@ -22,7 +22,8 @@
 LOAD = 27
 FIELDS = 30
 DOTS = 128
-BASIS = 3.2
+BASIS = 3.5
+TRUST = 2e4
 MARK = 7 * 32 - 128
 F32 = jnp.float32
 BF16 = jnp.bfloat16
@@ -40,7 +41,7 @@
 
 
 def dispatch_kernel(
-    mark_ref, routes_ref, counts_ref, own_ref, right_ref, above_ref, corner_ref, send_ref, place_ref
+    first_ref, shear_ref, couple_ref, routes_ref, counts_ref, own_ref, right_ref, above_ref, corner_ref, send_ref, place_ref
 ):
     owners = send_ref.shape[0]
     depth = own_ref.shape[3]
@@ -114,7 +115,10 @@
         total = term if total is None else total + term
     lane = lax.broadcasted_iota(jnp.int32, (owners, 128), 1)
     send_ref[:, 0, :] = total[:, :128]
-    send_ref[:, 1, :] = jnp.where(lane >= MARK, mark_ref[...], total[:, 128:])
+    axial = couple_ref[...].astype(F32)[:3]
+    stretch = jnp.sum(jnp.sum(axial * axial, axis=0, keepdims=True), axis=1, keepdims=True)
+    mark = (first_ref[...] + 2.0 * shear_ref[...] + stretch / 6.0) / owners
+    send_ref[:, 1, :] = jnp.where(lane >= MARK, mark, total[:, 128:])
 
 
 def micro_kernel(
@@ -141,11 +145,11 @@
 
     stiff = stiff_ref[...]
     pre = pre_ref[...]
-    halves = 2
+    halves = 4
     parts, loads, modes, sweeps = [], [], [], []
     for h in range(halves):
         part = jnp.concatenate(
-            [points_ref[pl.ds(tile * 8 + h * 4 + k, 8, stride=32), :] for k in range(4)], axis=1
+            [points_ref[pl.ds(tile * 16 + h * 4 + k, 8, stride=32), :] for k in range(4)], axis=1
         )
         parts.append(part)
         loads.append(jnp.dot(force_ref[...], part.astype(BF16), preferred_element_type=F32))
@@ -189,7 +193,7 @@
         for k in range(2):
             pair = rows[:, k * 2 * owners : (k + 1) * 2 * owners].T
             turned += [pair[:owners], pair[owners:]]
-        out_ref[:, pl.ds(tile * 2 + h, 1), :] = jnp.concatenate(turned, axis=1)[:, None, :]
+        out_ref[:, pl.ds(tile * 4 + h, 1), :] = jnp.concatenate(turned, axis=1)[:, None, :]
 
 
 def micro_solve(got, stiffness, precond, forcing, coupling, lame_first, lame_shear):
@@ -215,7 +219,7 @@
     whole = lambda *shape: pl.BlockSpec(shape, lambda step: (0,) * len(shape))
     return pl.pallas_call(
         micro_kernel,
-        grid=(4,),
+        grid=(2,),
         in_specs=[
             whole(owners, 2, 128),
             whole(modes, modes),
@@ -396,7 +400,7 @@
 
 
 def unpack_dots(ref, count):
-    row = jnp.sum(ref[...], axis=0)
+    row = jnp.sum(ref[...].reshape(-1, DOTS), axis=0, keepdims=True)
     lane = lax.broadcasted_iota(jnp.int32, (1, DOTS), 1)
     return [
         jnp.sum(jnp.where(lane == k, row, 0.0), axis=1, keepdims=True) for k in range(count)
@@ -510,6 +514,15 @@
     return total
 
 
+def place_planes(increment_ref, residual_ref, solved, left, basis, rows_ref, first):
+    for ref, weights in ((increment_ref, solved), (residual_ref, left)):
+        for y in (0, 1):
+            for c in range(3):
+                rows_ref[...] = total_of(w * basis[k][y][c] for k, w in enumerate(weights))
+                for x in (0, 1):
+                    ref[c, x, pl.ds(y, 1), :] = rows_ref[pl.ds(first + x, 1), :]
+
+
 def fourth_kernel(
     flags_ref,
     marks_ref,
@@ -522,6 +535,7 @@
     v5_ref,
     increment_ref,
     residual_ref,
+    trust_ref,
     rows_ref,
 ):
     center, half = basis_steps(marks_ref)
@@ -549,6 +563,12 @@
             p[i] * total_of(gram[i, j] * q[j] for j in range(len(q))) for i in range(len(p))
         )
 
+    def size(p, q):
+        return total_of(
+            jnp.abs(p[i]) * total_of(jnp.abs(gram[i, j]) * jnp.abs(q[j]) for j in range(len(q)))
+            for i in range(len(p))
+        )
+
     def combine(p, factor, q):
         longer = max(len(p), len(q))
         return [
@@ -562,11 +582,18 @@
     norm = gram[0, 0]
     for step in range(5):
         image = image_of(course)
-        alpha = norm / product(course, image)
+        bend = product(course, image)
+        if step == 4:
+            spread = size(course, image) / bend
+            trusted = jnp.where((spread > 0.0) & (spread < TRUST) & trusted, 1, 0)
+        alpha = norm / bend
         solved = combine(solved, alpha, course)
         left = combine(left, -alpha, image)
         if step < 4:
             fresh = product(left, left)
+            if step == 3:
+                spread = size(left, left) / fresh
+                trusted = (spread > 0.0) & (spread < TRUST)
             course = combine(left, fresh / norm, course)
             norm = fresh
     basis = [
@@ -577,16 +604,173 @@
         read_rows(v4_ref, 0, 2),
         read_rows(v5_ref, 0, 2),
     ]
-    first = flags_ref[1]
-    for ref, weights in ((increment_ref, solved), (residual_ref, left)):
-        for y in (0, 1):
-            for c in range(3):
-                rows_ref[...] = total_of(w * basis[k][y][c] for k, w in enumerate(weights))
-                for x in (0, 1):
-                    ref[c, x, pl.ds(y, 1), :] = rows_ref[pl.ds(first + x, 1), :]
+    trust_ref[...] = trusted
+    place_planes(increment_ref, residual_ref, solved, left, basis, rows_ref, flags_ref[1])
+
+
+def careful_first(low_ref, own_ref, high_ref, v0_ref, v1_ref):
+    read = value_reader(low_ref, own_ref, high_ref)
+    moves = shifts(own_ref.shape[2:])
+    write_rows(v1_ref, apply_rows(read_rows(v0_ref, -1, 4), read, 0, 1, moves), 0, 2)
+
+
+def careful_second(
+    last_ref, low_ref, own_ref, high_ref, v0_ref, v1_low_ref, v1_ref, v1_high_ref, v2_ref, dots_ref
+):
+    read = value_reader(low_ref, own_ref, high_ref)
+    moves = shifts(own_ref.shape[2:])
+    v1 = read_rows(v1_low_ref, -2, 2) | read_rows(v1_ref, 0, 2) | read_rows(v1_high_ref, 2, 2)
+    v2 = apply_rows(v1, read, -1, 2, moves)
+    inside(v2, 2, last_ref)
+    v0 = read_rows(v0_ref, -1, 4)
+    write_rows(v2_ref, v2, -1, 4)
+    pack_dots(
+        dots_ref,
+        [
+            row_dot(a, b)
+            for a, b in ((v0, v0), (v0, v1), (v0, v2), (v1, v1), (v1, v2))
+        ],
+    )
+
+
+def careful_third(
+    low_ref,
+    own_ref,
+    high_ref,
+    v0_ref,
+    v1_low_ref,
+    v1_ref,
+    v1_high_ref,
+    v2_ref,
+    sums_ref,
+    r1_ref,
+    r2_ref,
+    w3_ref,
+    coef_ref,
+):
+    read = value_reader(low_ref, own_ref, high_ref)
+    moves = shifts(own_ref.shape[2:])
+    m00, m01, m02, m11, m12 = unpack_dots(sums_ref, 5)
+    a0 = m00 / m01
+    n1 = m00 - 2.0 * a0 * m01 + a0 * a0 * m11
+    b0 = n1 / m00
+    e = 1.0 + b0
+    a1 = n1 / (e * e * m01 - e * a0 * (m02 + m11) + a0 * a0 * m12)
+    center = 0.5 * (1.0 / a0 + 1.0 / a1 + b0 / a0)
+    v0 = read_rows(v0_ref, -1, 4)
+    v1 = read_rows(v1_low_ref, -2, 2) | read_rows(v1_ref, 0, 2) | read_rows(v1_high_ref, 2, 2)
+    v2 = read_rows(v2_ref, -1, 4)
+    along, twice = a0 + a1 * e, a1 * a0
+    r2 = {
+        y: tuple(v0[y][c] - along * v1[y][c] + twice * v2[y][c] for c in range(3))
+        for y in range(-1, 3)
+    }
+    image = apply_rows(r2, read, 0, 1, moves)
+    scale = 1.0 / center
+    w3 = {y: tuple(image[y][c] * scale - r2[y][c] for c in range(3)) for y in (0, 1)}
+    r1 = {y: tuple(v0[y][c] - a0 * v1[y][c] for c in range(3)) for y in (0, 1)}
+    write_rows(r1_ref, r1, 0, 2)
+    write_rows(r2_ref, r2, 0, 2)
+    write_rows(w3_ref, w3, 0, 2)
+    lane = lax.broadcasted_iota(jnp.int32, (1, DOTS), 1)
+    packed = jnp.zeros((1, DOTS), F32)
+    for k, value in enumerate((a0, b0, a1, n1, center)):
+        packed = packed + jnp.where(lane == k, value, 0.0)
+    coef_ref[...] = packed
+
+
+def careful_fourth(
+    last_ref,
+    low_ref,
+    own_ref,
+    high_ref,
+    coef_ref,
+    v0_ref,
+    r1_ref,
+    r2_ref,
+    w3_low_ref,
+    w3_ref,
+    w3_high_ref,
+    w4_ref,
+    w5_ref,
+    dots_ref,
+):
+    read = value_reader(low_ref, own_ref, high_ref)
+    moves = shifts(own_ref.shape[2:])
+    scale = 1.0 / unpack_dots(coef_ref, 5)[4]
+    w3 = read_rows(w3_low_ref, -2, 2) | read_rows(w3_ref, 0, 2) | read_rows(w3_high_ref, 2, 2)
+    image = apply_rows(w3, read, -1, 2, moves)
+    w4 = {y: tuple(image[y][c] * scale - w3[y][c] for c in range(3)) for y in range(-1, 3)}
+    inside(w4, 2, last_ref)
+    image = apply_rows(w4, read, 0, 1, moves)
+    w5 = {y: tuple(image[y][c] * scale - w4[y][c] for c in range(3)) for y in (0, 1)}
+    write_rows(w4_ref, w4, 0, 2)
+    write_rows(w5_ref, w5, 0, 2)
+    v0 = read_rows(v0_ref, -1, 4)
+    basis = [v0, read_rows(r1_ref, 0, 2), read_rows(r2_ref, 0, 2), w3, w4, w5]
+    pack_dots(dots_ref, [row_dot(basis[i], basis[j]) for i, j in basis_pairs()])
+
+
+def careful_fifth(
+    flags_ref,
+    coef_ref,
+    sums_ref,
+    v0_ref,
+    r1_ref,
+    r2_ref,
+    w3_ref,
+    w4_ref,
+    w5_ref,
+    increment_ref,
+    residual_ref,
+    rows_ref,
+):
+    a0, b0, a1, n1, center = unpack_dots(coef_ref, 5)
+    dots = unpack_dots(sums_ref, 21)
+    gram = {}
+    for k, (i, j) in enumerate(basis_pairs()):
+        gram[i, j] = gram[j, i] = dots[k]
+    zero = jnp.zeros((1, 1), F32)
+    one = jnp.ones((1, 1), F32)
+    i0, i1 = 1.0 / a0, 1.0 / a1
+
+    def image_of(p):
+        return [
+            i0 * p[0] - b0 * i0 * p[1],
+            (i1 + b0 * i0) * p[1] - i0 * p[0],
+            center * p[2] - i1 * p[1],
+            center * (p[2] + p[3]),
+            center * (p[3] + p[4]),
+            center * p[4],
+        ]
+
+    def product(p, q):
+        return total_of(
+            p[i] * total_of(gram[i, j] * q[j] for j in range(6)) for i in range(6)
+        )
+
+    solved = [a0 + a1 * b0, a1, zero, zero, zero, zero]
+    left = [zero, zero, one, zero, zero, zero]
+    norm = gram[2, 2]
+    ratio = norm / n1
+    course = [ratio * b0, ratio, one, zero, zero, zero]
+    for step in range(3):
+        image = image_of(course)
+        alpha = norm / product(course, image)
+        solved = [s + alpha * p for s, p in zip(solved, course)]
+        left = [r - alpha * q for r, q in zip(left, image)]
+        if step < 2:
+            fresh = product(left, left)
+            ratio = fresh / norm
+            course = [r + ratio * p for r, p in zip(left, course)]
+            norm = fresh
+    v0 = read_rows(v0_ref, -1, 4)
+    basis = [v0] + [read_rows(ref, 0, 2) for ref in (r1_ref, r2_ref, w3_ref, w4_ref, w5_ref)]
+    place_planes(increment_ref, residual_ref, solved, left, basis, rows_ref, flags_ref[1])
 
 
 def local_call(kernel, outs, name, *args, flags=None, scratch=()):
+    typed = [out if isinstance(out[0], tuple) else (out, F32) for out in outs]
     specs = [pl.BlockSpec(memory_space=pltpu.VMEM)] * len(args)
     if flags is not None:
         specs = [pl.BlockSpec(memory_space=pltpu.SMEM)] + specs
@@ -595,7 +779,7 @@
         kernel,
         in_specs=specs,
         out_specs=[pl.BlockSpec(memory_space=pltpu.VMEM)] * len(outs),
-        out_shape=[jax.ShapeDtypeStruct(*out) if isinstance(out[0], tuple) else jax.ShapeDtypeStruct(out, F32) for out in outs],
+        out_shape=[jax.ShapeDtypeStruct(*out) for out in typed],
         scratch_shapes=scratch,
         compiler_params=pltpu.CompilerParams(vmem_limit_bytes=48 * 1024 * 1024),
         name=name,
@@ -641,8 +825,6 @@
     points = planes * width * depth
     rows_x = lax.axis_size("macro")
     owners = lax.axis_size(MICRO)
-    stretch = jnp.sum(jnp.square(coupling[0, :, :3].astype(F32)))
-    mark = ((lame_first[0] + 2.0 * lame_shear[0] + stretch / 6.0) / owners).reshape(1, 1)
     right = lax.ppermute(displacement, "macro", [(a + 1, a) for a in range(rows_x - 1)])
     above = lax.ppermute(displacement, MICRO, [(b + 1, b) for b in range(owners - 1)])
     corner = lax.ppermute(
@@ -658,7 +840,9 @@
         dispatch_kernel,
         ((owners, 2, 128), ((8, points), jnp.int32)),
         "dispatch",
-        mark,
+        lame_first.reshape(1, 1),
+        lame_shear.reshape(1, 1),
+        coupling[0].T,
         routes.reshape(1, points),
         counts.reshape(1, points),
         displacement,
@@ -710,23 +894,85 @@
         flags=flags,
     )
     mine = (3, planes, width, depth)
-    return tuple(
-        local_call(
-            fourth_kernel,
-            (mine, mine),
-            "fourth_rows",
-            marks,
+    scratch = [pltpu.VMEM((whole, depth), F32)]
+    increment, residual, trust = local_call(
+        fourth_kernel,
+        (mine, mine, ((1, 1), jnp.int32)),
+        "fourth_rows",
+        marks,
+        swapped(dots),
+        v0,
+        v1,
+        v2,
+        v3,
+        v4,
+        v5,
+        flags=flags,
+        scratch=scratch,
+    )
+
+    def careful():
+        sets = (low, own, high)
+        line = (1, DOTS)
+        (u1,) = local_call(careful_first, (two,), "careful_first", *sets, v0)
+        u1_low, u1_high = up_and_down(u1, u1)
+        u2, dots = local_call(
+            careful_second,
+            (four, (owners, 1, DOTS)),
+            "careful_second",
+            *sets,
+            v0,
+            u1_low,
+            u1,
+            u1_high,
+            flags=flags,
+        )
+        r1, r2, w3, coef = local_call(
+            careful_third,
+            (two, two, two, line),
+            "careful_third",
+            *sets,
+            v0,
+            u1_low,
+            u1,
+            u1_high,
+            u2,
             swapped(dots),
+        )
+        w3_low, w3_high = up_and_down(w3, w3)
+        w4, w5, dots = local_call(
+            careful_fourth,
+            (two, two, (owners, 1, DOTS)),
+            "careful_fourth",
+            *sets,
+            coef,
             v0,
-            v1,
-            v2,
-            v3,
-            v4,
-            v5,
+            r1,
+            r2,
+            w3_low,
+            w3,
+            w3_high,
             flags=flags,
-            scratch=[pltpu.VMEM((whole, depth), F32)],
         )
-    )
+        return tuple(
+            local_call(
+                careful_fifth,
+                (mine, mine),
+                "careful_fifth",
+                coef,
+                swapped(dots),
+                v0,
+                r1,
+                r2,
+                w3,
+                w4,
+                w5,
+                flags=flags,
+                scratch=scratch,
+            )
+        )
+
+    return lax.cond(trust[0, 0] == 1, lambda: (increment, residual), careful)
 
 
 def solution(mesh):

time: 135 us -> 135 us (level)
  blocking collectives: 39.3 us -> 15.9 us
  starting transfers between devices: 42.2 us -> 56.4 us
  waiting for transfers between devices: 21 us -> 31.6 us
  Pallas kernels: 22.4 us -> 20.6 us
  local copies, waits for them, and re-layouts: 4.05 us -> 5.45 us
    all_to_all x2 -> x1, blocking collectives: 39.3 us -> 15.9 us  [swapped(): return lax.all_to_all(block, MICRO, split_axis=0, concat_axis=0, tiled=True)]
    all_to_all x1 -> x2, starting transfers between devices: 11.3 us -> 25.7 us  [swapped(): return lax.all_to_all(block, MICRO, split_axis=0, concat_axis=0, tiled=True)]
    all_to_all x1 -> x2, waiting for transfers between devices: 8.02 us -> 17.3 us  [swapped(): return lax.all_to_all(block, MICRO, split_axis=0, concat_axis=0, tiled=True)]
    pallas_call x1, Pallas kernels: 14.8 us -> 12.4 us  [micro_solve(): pl.pallas_call(micro_kernel, grid=(2,), in_specs=[whole(owners, 2, 128),...]
    ppermute x1, waiting for transfers between devices: 0.73 us -> 2.64 us  [shards(): lax.ppermute(displacement, ('macro',) + MICRO, [((a + 1) * owners + b + 1...]
    unnamed x17 -> x19, local copies, waits for them, and re-layouts: 2.28 us -> 3.67 us
  transfers between devices with their start and end apart: 13 -> 14, of which waited for: 7 -> 8; matrix products, arithmetic and copies ran while one was open for 3% -> 2% of each run, Pallas kernels for 0% -> 0%
where the time goes in v3:
time: 135 us; the launch traced here: 134 us
  starting transfers between devices  56.4 us (42%)
  waiting for transfers between devices  31.6 us (23%)
  Pallas kernels  20.6 us (15%)
  blocking collectives  15.9 us (12%)
  local copies, waits for them, and re-layouts  5.45 us (4%)
  between operations  3 us (2%)
    all_to_all x2, starting transfers between devices, swapped(): return lax.all_to_all(block, MICRO, split_axis=0, concat_axis=0, tiled=True)  25.7 us
    all_to_all x2, waiting for transfers between devices, swapped(): return lax.all_to_all(block, MICRO, split_axis=0, concat_axis=0, tiled=True)  17.3 us
    all_to_all x1, blocking collectives, swapped(): return lax.all_to_all(block, MICRO, split_axis=0, concat_axis=0, tiled=True)  15.9 us
    pallas_call x1, Pallas kernels, micro_solve(): pl.pallas_call(micro_kernel, grid=(2,), in_specs=[whole(owners, 2, 128),...  12.4 us
    ppermute x3, starting transfers between devices, up_and_down(): lax.ppermute(up, MICRO, forward)  12 us
    pallas_call x6, Pallas kernels, local_call(): pl.pallas_call(kernel, in_specs=specs, out_specs=[pl.BlockSpec(memory_spa...  8.22 us
    ppermute x3, starting transfers between devices, up_and_down(): lax.ppermute(down, MICRO, backward)  5.76 us
    ppermute x3, waiting for transfers between devices, up_and_down(): lax.ppermute(down, MICRO, backward)  5.5 us
  transfers between devices with their start and end apart: 14, of which 8 were waited for; matrix products, arithmetic and copies ran while one was open for 2% of the time, Pallas kernels for 0%

profile of v3, /device:TPU:1, one launch (start us, length us, event | category | flops | bytes accessed | tf_op | source)
XLA Modules:
  0.0 133.9 jit_solution(5350153176794889936)
XLA Ops:
  0.7 5.2 %collective-permute-start.5 = (f32[3,2,2,256]{3,2,1,0:T(2,128)}, f32[3,2,2,256]{3,2,1,0:T(2,128)S(1)}, u32[]{:S(2)}, u32[]{:S(2)}) collective-permute-start(f32[3,2,2,256]{3,2,1,0:T(2,128)} %own_ref.1), channel_id=1, source_target_pairs={{1,0},{2,1},{3,2},{4,3},{5,4},{6,5},{7,6},{8,7},{9,8},{10,9},{11,1... | collective-permute-start | bytes 36872 | tf_op jit(solution)/shard_map/ppermute | solution.py:829
  5.8 1.3 collective-permute-start.4
  7.1 1.3 collective-permute-start.6
  9.7 0.8 bitcast_convert_fusion
  10.6 2.6 %collective-permute-done.6.corner_ref = f32[3,2,2,256]{3,2,1,0:T(2,128)S(1)} collective-permute-done((f32[3,2,2,256]{3,2,1,0:T(2,128)}, f32[3,2,2,256]{3,2,1,0:T(2,128)S(1)}, u32[]{:S(2)}, u32[]{:S(2)}) %collective-permute-start.6) | collective-permute-done | bytes 12320 | tf_op jit(solution)/shard_map/ppermute | solution.py:830
  16.0 1.4 %dispatch.1 = (f32[64,2,128]{2,1,0:T(2,128)}, s32[8,1024]{1,0:T(8,128)S(1)}) custom-call(f32[1,1]{1,0:T(1,128)} %bitcast.18.first_ref, f32[1,1]{1,0:T(1,128)} %bitcast.20.shear_ref, bf16[6,512]{1,0:T(8,128)(2,1)S(1)} %bitcast.25, s32[1,1024]{1,0:T(1,128)S(1)} %bitcast.26, s32[1,1024]{1,0:T(1,128)S(1)} %bitcast.27, f32[3,2,2,256]{3,2,1,0:T(2,128)S(1)} %copy-done.3, ...), custom_call_target="tpu_custom_call" | custom-call | tf_op jit(solution)/shard_map/dispatch/pallas_call | solution.py:778
  17.4 11.3 %all-to-all-start.2 = ((f32[64,2,128]{2,1,0:T(2,128)}), f32[64,2,128]{2,1,0:T(2,128)S(1)}, u32[]{:S(2)}, u32[]{:S(2)}) async-start(f32[64,2,128]{2,1,0:T(2,128)} %get-tuple-element.44), calls=%async_computation.2 | async-start | bytes 131072 | tf_op jit(solution)/shard_map/all_to_all | solution.py:797
  29.5 0.9 copy.19
  30.5 8.0 %all-to-all-done.2.got_ref = f32[64,2,128]{2,1,0:T(2,128)S(1)} async-done(((f32[64,2,128]{2,1,0:T(2,128)}), f32[64,2,128]{2,1,0:T(2,128)S(1)}, u32[]{:S(2)}, u32[]{:S(2)}) %all-to-all-start.2) | async-done | bytes 65568 | tf_op jit(solution)/shard_map/all_to_all | solution.py:797
  38.5 12.4 %micro_solve.1 = (f32[64,8,128]{2,1,0:T(8,128)S(1)}, f32[1,128]{1,0:T(1,128)S(1)}) custom-call(f32[64,2,128]{2,1,0:T(2,128)S(1)} %all-to-all-done.2.got_ref, bf16[512,512]{1,0:T(8,128)(2,1)S(1)} %bitcast.22, bf16[512,512]{1,0:T(8,128)(2,1)S(1)} %bitcast.23, bf16[512,8]{1,0:T(8,128)(2,1)S(1)} %pad_bitcast_fusion.force_ref, ...), custom_call_target="tpu_custom_call" | custom-call | tf_op jit(solution)/shard_map/micro_solve/pallas_call | solution.py:220
  51.0 15.9 %all_to_all.25.back_ref = f32[64,8,128]{2,1,0:T(8,128)S(1)} all-to-all(f32[64,8,128]{2,1,0:T(8,128)S(1)} %get-tuple-element.46), channel_id=1, replica_groups=mesh['macro'=4,'micro_0'=4,'micro_1'=8,'micro_2'=2] {'micro_0','micro_1'..., dimensions={0} | all-to-all | bytes 524288 | tf_op jit(solution)/shard_map/all_to_all | solution.py:797
  66.8 1.3 pick.1
  68.1 1.6 %collective-permute-start.9 = (f32[30,2,2,256]{3,2,1,0:T(2,128)S(1)}, f32[30,2,2,256]{3,2,1,0:T(2,128)S(1)}, u32[]{:S(2)}, u32[]{:S(2)}) collective-permute-start(f32[30,2,2,256]{3,2,1,0:T(2,128)S(1)} %pick.1), channel_id=1, source_target_pairs={{0,64},{64,128},{128,192},{192,0},{1,65},{65,129},{129,193},{193,1... | collective-permute-start | bytes 368648 | tf_op jit(solution)/shard_map/ppermute | solution.py:803
  69.8 1.6 %collective-permute-start.8 = (f32[30,2,2,256]{3,2,1,0:T(2,128)S(1)}, f32[30,2,2,256]{3,2,1,0:T(2,128)S(1)}, u32[]{:S(2)}, u32[]{:S(2)}) collective-permute-start(f32[30,2,2,256]{3,2,1,0:T(2,128)S(1)} %pick.1), channel_id=1, source_target_pairs={{0,128},{64,192},{128,0},{192,64},{1,129},{65,193},{129,1},{193,65... | collective-permute-start | bytes 368648 | tf_op jit(solution)/shard_map/ppermute | solution.py:803
  71.4 2.0 %collective-permute-start.7 = (f32[30,2,2,256]{3,2,1,0:T(2,128)S(1)}, f32[30,2,2,256]{3,2,1,0:T(2,128)S(1)}, u32[]{:S(2)}, u32[]{:S(2)}) collective-permute-start(f32[30,2,2,256]{3,2,1,0:T(2,128)S(1)} %pick.1), channel_id=1, source_target_pairs={{0,192},{64,0},{128,64},{192,128},{1,193},{65,1},{129,65},{193,129... | collective-permute-start | bytes 368648 | tf_op jit(solution)/shard_map/ppermute | solution.py:803
  73.9 3.3 %collective-permute-done.8 = f32[30,2,2,256]{3,2,1,0:T(2,128)S(1)} collective-permute-done((f32[30,2,2,256]{3,2,1,0:T(2,128)S(1)}, f32[30,2,2,256]{3,2,1,0:T(2,128)S(1)}, u32[]{:S(2)}, u32[]{:S(2)}) %collective-permute-start.8) | collective-permute-done | bytes 122912 | tf_op jit(solution)/shard_map/ppermute | solution.py:803
  77.2 0.8 concatenate.3
  78.1 4.1 %collective-permute-start.10 = (f32[30,2,8,256]{3,2,1,0:T(8,128)S(1)}, f32[30,2,8,256]{3,2,1,0:T(8,128)S(1)}, u32[]{:S(2)}, u32[]{:S(2)}) collective-permute-start(f32[30,2,8,256]{3,2,1,0:T(8,128)S(1)} %constant_dynamic-slice_fusion.1.own_ref), channel_id=1, source_target_pairs={{0,1},{1,2},{2,3},{3,4},{4,5},{5,6},{6,7},{7,8},{8,9},{9,10},{10,1... | collective-permute-start | bytes 1474568 | tf_op jit(solution)/shard_map/ppermute | solution.py:793
  82.3 1.9 %collective-permute-start.11 = (f32[30,1,8,256]{3,2,1,0:T(8,128)S(1)}, f32[30,1,8,256]{3,2,1,0:T(8,128)S(1)}, u32[]{:S(2)}, u32[]{:S(2)}) collective-permute-start(f32[30,1,8,256]{3,2,1,0:T(8,128)S(1)} %constant_dynamic-slice_fusion), channel_id=1, source_target_pairs={{1,0},{2,1},{3,2},{4,3},{5,4},{6,5},{7,6},{8,7},{9,8},{10,9},{11,1... | collective-permute-start | bytes 737288 | tf_op jit(solution)/shard_map/ppermute | solution.py:793
  84.3 5.5 %collective-permute-done.11.high_ref = f32[30,1,8,256]{3,2,1,0:T(8,128)S(1)} collective-permute-done((f32[30,1,8,256]{3,2,1,0:T(8,128)S(1)}, f32[30,1,8,256]{3,2,1,0:T(8,128)S(1)}, u32[]{:S(2)}, u32[]{:S(2)}) %collective-permute-start.11) | collective-permute-done | bytes 245792 | tf_op jit(solution)/shard_map/ppermute | solution.py:793
  89.8 0.9 first_rows.1
  90.7 1.9 %collective-permute-start.13 = (f32[3,2,8,256]{3,2,1,0:T(8,128)S(1)}, f32[3,2,8,256]{3,2,1,0:T(8,128)S(1)}, u32[]{:S(2)}, u32[]{:S(2)}) collective-permute-start(f32[3,2,8,256]{3,2,1,0:T(8,128)S(1)} %get-tuple-element.49.v1_ref), channel_id=1, source_target_pairs={{1,0},{2,1},{3,2},{4,3},{5,4},{6,5},{7,6},{8,7},{9,8},{10,9},{11,1... | collective-permute-start | bytes 147464 | tf_op jit(solution)/shard_map/ppermute | solution.py:793
  92.7 3.6 %collective-permute-start.12 = (f32[3,2,8,256]{3,2,1,0:T(8,128)S(1)}, f32[3,2,8,256]{3,2,1,0:T(8,128)S(1)}, u32[]{:S(2)}, u32[]{:S(2)}) collective-permute-start(f32[3,2,8,256]{3,2,1,0:T(8,128)S(1)} %get-tuple-element.49.v1_ref), channel_id=1, source_target_pairs={{0,1},{1,2},{2,3},{3,4},{4,5},{5,6},{6,7},{7,8},{8,9},{9,10},{10,1... | collective-permute-start | bytes 147464 | tf_op jit(solution)/shard_map/ppermute | solution.py:793
  96.3 1.1 collective-permute-done.12.v1_low_ref
  97.5 1.2 second_rows.1
  98.7 1.9 %collective-permute-start.15 = (f32[3,2,8,256]{3,2,1,0:T(8,128)S(1)}, f32[3,2,8,256]{3,2,1,0:T(8,128)S(1)}, u32[]{:S(2)}, u32[]{:S(2)}) collective-permute-start(f32[3,2,8,256]{3,2,1,0:T(8,128)S(1)} %get-tuple-element.51.v3_ref), channel_id=1, source_target_pairs={{1,0},{2,1},{3,2},{4,3},{5,4},{6,5},{7,6},{8,7},{9,8},{10,9},{11,1... | collective-permute-start | bytes 147464 | tf_op jit(solution)/shard_map/ppermute | solution.py:793
  100.6 4.2 %collective-permute-start.14 = (f32[3,2,8,256]{3,2,1,0:T(8,128)S(1)}, f32[3,2,8,256]{3,2,1,0:T(8,128)S(1)}, u32[]{:S(2)}, u32[]{:S(2)}) collective-permute-start(f32[3,2,8,256]{3,2,1,0:T(8,128)S(1)} %get-tuple-element.51.v3_ref), channel_id=1, source_target_pairs={{0,1},{1,2},{2,3},{3,4},{4,5},{5,6},{6,7},{7,8},{8,9},{9,10},{10,1... | collective-permute-start | bytes 147464 | tf_op jit(solution)/shard_map/ppermute | solution.py:793
  104.9 1.1 collective-permute-done.14.v3_low_ref
  106.0 1.9 %third_rows.1 = (f32[3,2,8,256]{3,2,1,0:T(8,128)S(1)}, f32[3,2,8,256]{3,2,1,0:T(8,128)S(1)}, f32[64,1,128]{2,1,0:T(1,128)}) custom-call(s32[2]{0:T(128)S(1)} %pad_add_fusion.flags_ref, f32[1,128]{1,0:T(1,128)S(1)} %get-tuple-element.45.marks_ref, f32[30,2,8,256]{3,2,1,0:T(8,128)S(1)} %collective-permute-done.10.low_ref, ...), custom_call_target="tpu_custom_call" | custom-call | tf_op jit(solution)/shard_map/third_rows/pallas_call | solution.py:778
  108.0 14.3 %all-to-all-start.4 = ((f32[64,1,128]{2,1,0:T(1,128)}), f32[64,1,128]{2,1,0:T(1,128)S(1)}, u32[]{:S(2)}, u32[]{:S(2)}) async-start(f32[64,1,128]{2,1,0:T(1,128)} %get-tuple-element.52), calls=%async_computation.4 | async-start | bytes 65536 | tf_op jit(solution)/shard_map/all_to_all | solution.py:797
  122.3 9.3 %all-to-all-done.4.sums_ref = f32[64,1,128]{2,1,0:T(1,128)S(1)} async-done(((f32[64,1,128]{2,1,0:T(1,128)}), f32[64,1,128]{2,1,0:T(1,128)S(1)}, u32[]{:S(2)}, u32[]{:S(2)}) %all-to-all-start.4) | async-done | bytes 32800 | tf_op jit(solution)/shard_map/all_to_all | solution.py:797
  131.6 1.5 %fourth_rows.1 = (f32[3,2,2,256]{3,2,1,0:T(2,128)}, f32[3,2,2,256]{3,2,1,0:T(2,128)}, s32[1,1]{1,0:T(1,128)}) custom-call(s32[2]{0:T(128)S(1)} %pad_add_fusion.flags_ref, f32[1,128]{1,0:T(1,128)S(1)} %get-tuple-element.45.marks_ref, f32[64,1,128]{2,1,0:T(1,128)S(1)} %all-to-all-done.4.sums_ref, f32[3,4,8,256]{3,2,1,0:T(8,128)S(1)} %get-tuple-element.48.v0_ref, ...), custom_call_target="tpu_custom_call" | custom-call | tf_op jit(solution)/shard_map/fourth_rows/pallas_call | solution.py:778
  (36 shorter events, 4.5 us)
Async XLA Ops:
  0.6 9.9 %copy-start.8 = (f32[32,8]{1,0:T(8,128)S(1)}, f32[32,8]{1,0:T(8,128)}, u32[]{:S(2)}) copy-start(f32[32,8]{1,0:T(8,128)} %constant.51.clone) | copy-start | bytes 3076
  0.6 9.9 %copy-start.7 = (f32[32,8]{1,0:T(8,128)S(1)}, f32[32,8]{1,0:T(8,128)}, u32[]{:S(2)}) copy-start(f32[32,8]{1,0:T(8,128)} %constant.52.clone) | copy-start | bytes 3076
  0.7 9.9 %collective-permute-start.5 = (f32[3,2,2,256]{3,2,1,0:T(2,128)}, f32[3,2,2,256]{3,2,1,0:T(2,128)S(1)}, u32[]{:S(2)}, u32[]{:S(2)}) collective-permute-start(f32[3,2,2,256]{3,2,1,0:T(2,128)} %own_ref.1), channel_id=1, source_target_pairs={{1,0},{2,1},{3,2},{4,3},{5,4},{6,5},{7,6},{8,7},{9,8},{10,9},{11,1... | collective-permute-start | bytes 36872 | tf_op jit(solution)/shard_map/ppermute | solution.py:829
  5.8 4.8 %collective-permute-start.4 = (f32[3,2,2,256]{3,2,1,0:T(2,128)}, f32[3,2,2,256]{3,2,1,0:T(2,128)S(1)}, u32[]{:S(2)}, u32[]{:S(2)}) collective-permute-start(f32[3,2,2,256]{3,2,1,0:T(2,128)} %own_ref.1), channel_id=1, source_target_pairs={{64,0},{128,64},{192,128},{65,1},{129,65},{193,129},{66,2},{130,66... | collective-permute-start | bytes 36872 | tf_op jit(solution)/shard_map/ppermute | solution.py:828
  7.1 6.1 %collective-permute-start.6 = (f32[3,2,2,256]{3,2,1,0:T(2,128)}, f32[3,2,2,256]{3,2,1,0:T(2,128)S(1)}, u32[]{:S(2)}, u32[]{:S(2)}) collective-permute-start(f32[3,2,2,256]{3,2,1,0:T(2,128)} %own_ref.1), channel_id=1, source_target_pairs={{65,0},{66,1},{67,2},{68,3},{69,4},{70,5},{71,6},{72,7},{73,8},{74... | collective-permute-start | bytes 36872 | tf_op jit(solution)/shard_map/ppermute | solution.py:830
  9.7 28.8 %copy-start = (bf16[1,512,512]{2,1,0:T(8,128)(2,1)S(1)}, bf16[1,512,512]{2,1,0:T(8,128)(2,1)}, u32[]{:S(2)}) copy-start(bf16[1,512,512]{2,1,0:T(8,128)(2,1)} %param.18) | copy-start | bytes 1572868
  9.7 28.8 %copy-start.1 = (bf16[1,512,512]{2,1,0:T(8,128)(2,1)S(1)}, bf16[1,512,512]{2,1,0:T(8,128)(2,1)}, u32[]{:S(2)}) copy-start(bf16[1,512,512]{2,1,0:T(8,128)(2,1)} %param.19) | copy-start | bytes 1572868
  13.2 0.7 copy-start.2
  13.9 0.7 copy-start.3
  14.6 0.7 copy-start.5
  15.3 0.7 copy-start.6
  17.4 21.1 %all-to-all-start.2 = ((f32[64,2,128]{2,1,0:T(2,128)}), f32[64,2,128]{2,1,0:T(2,128)S(1)}, u32[]{:S(2)}, u32[]{:S(2)}) async-start(f32[64,2,128]{2,1,0:T(2,128)} %get-tuple-element.44), calls=%async_computation.2 | async-start | bytes 131072 | tf_op jit(solution)/shard_map/all_to_all | solution.py:797
  50.9 15.9 %copy-start.4 = (f32[3,2,2,256]{3,2,1,0:T(2,128)S(1)}, f32[3,2,2,256]{3,2,1,0:T(2,128)}, u32[]{:S(2)}) copy-start(f32[3,2,2,256]{3,2,1,0:T(2,128)} %load_ref.1) | copy-start | bytes 36868
  68.1 5.7 %collective-permute-start.9 = (f32[30,2,2,256]{3,2,1,0:T(2,128)S(1)}, f32[30,2,2,256]{3,2,1,0:T(2,128)S(1)}, u32[]{:S(2)}, u32[]{:S(2)}) collective-permute-start(f32[30,2,2,256]{3,2,1,0:T(2,128)S(1)} %pick.1), channel_id=1, source_target_pairs={{0,64},{64,128},{128,192},{192,0},{1,65},{65,129},{129,193},{193,1... | collective-permute-start | bytes 368648 | tf_op jit(solution)/shard_map/ppermute | solution.py:803
  69.8 7.5 %collective-permute-start.8 = (f32[30,2,2,256]{3,2,1,0:T(2,128)S(1)}, f32[30,2,2,256]{3,2,1,0:T(2,128)S(1)}, u32[]{:S(2)}, u32[]{:S(2)}) collective-permute-start(f32[30,2,2,256]{3,2,1,0:T(2,128)S(1)} %pick.1), channel_id=1, source_target_pairs={{0,128},{64,192},{128,0},{192,64},{1,129},{65,193},{129,1},{193,65... | collective-permute-start | bytes 368648 | tf_op jit(solution)/shard_map/ppermute | solution.py:803
  71.4 5.8 %collective-permute-start.7 = (f32[30,2,2,256]{3,2,1,0:T(2,128)S(1)}, f32[30,2,2,256]{3,2,1,0:T(2,128)S(1)}, u32[]{:S(2)}, u32[]{:S(2)}) collective-permute-start(f32[30,2,2,256]{3,2,1,0:T(2,128)S(1)} %pick.1), channel_id=1, source_target_pairs={{0,192},{64,0},{128,64},{192,128},{1,193},{65,1},{129,65},{193,129... | collective-permute-start | bytes 368648 | tf_op jit(solution)/shard_map/ppermute | solution.py:803
  78.1 11.7 %collective-permute-start.10 = (f32[30,2,8,256]{3,2,1,0:T(8,128)S(1)}, f32[30,2,8,256]{3,2,1,0:T(8,128)S(1)}, u32[]{:S(2)}, u32[]{:S(2)}) collective-permute-start(f32[30,2,8,256]{3,2,1,0:T(8,128)S(1)} %constant_dynamic-slice_fusion.1.own_ref), channel_id=1, source_target_pairs={{0,1},{1,2},{2,3},{3,4},{4,5},{5,6},{6,7},{7,8},{8,9},{9,10},{10,1... | collective-permute-start | bytes 1474568 | tf_op jit(solution)/shard_map/ppermute | solution.py:793
  82.3 7.5 %collective-permute-start.11 = (f32[30,1,8,256]{3,2,1,0:T(8,128)S(1)}, f32[30,1,8,256]{3,2,1,0:T(8,128)S(1)}, u32[]{:S(2)}, u32[]{:S(2)}) collective-permute-start(f32[30,1,8,256]{3,2,1,0:T(8,128)S(1)} %constant_dynamic-slice_fusion), channel_id=1, source_target_pairs={{1,0},{2,1},{3,2},{4,3},{5,4},{6,5},{7,6},{8,7},{9,8},{10,9},{11,1... | collective-permute-start | bytes 737288 | tf_op jit(solution)/shard_map/ppermute | solution.py:793
  90.7 5.6 %collective-permute-start.13 = (f32[3,2,8,256]{3,2,1,0:T(8,128)S(1)}, f32[3,2,8,256]{3,2,1,0:T(8,128)S(1)}, u32[]{:S(2)}, u32[]{:S(2)}) collective-permute-start(f32[3,2,8,256]{3,2,1,0:T(8,128)S(1)} %get-tuple-element.49.v1_ref), channel_id=1, source_target_pairs={{1,0},{2,1},{3,2},{4,3},{5,4},{6,5},{7,6},{8,7},{9,8},{10,9},{11,1... | collective-permute-start | bytes 147464 | tf_op jit(solution)/shard_map/ppermute | solution.py:793
  92.7 4.8 %collective-permute-start.12 = (f32[3,2,8,256]{3,2,1,0:T(8,128)S(1)}, f32[3,2,8,256]{3,2,1,0:T(8,128)S(1)}, u32[]{:S(2)}, u32[]{:S(2)}) collective-permute-start(f32[3,2,8,256]{3,2,1,0:T(8,128)S(1)} %get-tuple-element.49.v1_ref), channel_id=1, source_target_pairs={{0,1},{1,2},{2,3},{3,4},{4,5},{5,6},{6,7},{7,8},{8,9},{9,10},{10,1... | collective-permute-start | bytes 147464 | tf_op jit(solution)/shard_map/ppermute | solution.py:793
  98.7 6.2 %collective-permute-start.15 = (f32[3,2,8,256]{3,2,1,0:T(8,128)S(1)}, f32[3,2,8,256]{3,2,1,0:T(8,128)S(1)}, u32[]{:S(2)}, u32[]{:S(2)}) collective-permute-start(f32[3,2,8,256]{3,2,1,0:T(8,128)S(1)} %get-tuple-element.51.v3_ref), channel_id=1, source_target_pairs={{1,0},{2,1},{3,2},{4,3},{5,4},{6,5},{7,6},{8,7},{9,8},{10,9},{11,1... | collective-permute-start | bytes 147464 | tf_op jit(solution)/shard_map/ppermute | solution.py:793
  100.6 5.4 %collective-permute-start.14 = (f32[3,2,8,256]{3,2,1,0:T(8,128)S(1)}, f32[3,2,8,256]{3,2,1,0:T(8,128)S(1)}, u32[]{:S(2)}, u32[]{:S(2)}) collective-permute-start(f32[3,2,8,256]{3,2,1,0:T(8,128)S(1)} %get-tuple-element.51.v3_ref), channel_id=1, source_target_pairs={{0,1},{1,2},{2,3},{3,4},{4,5},{5,6},{6,7},{7,8},{8,9},{9,10},{10,1... | collective-permute-start | bytes 147464 | tf_op jit(solution)/shard_map/ppermute | solution.py:793
  108.0 23.6 %all-to-all-start.4 = ((f32[64,1,128]{2,1,0:T(1,128)}), f32[64,1,128]{2,1,0:T(1,128)S(1)}, u32[]{:S(2)}, u32[]{:S(2)}) async-start(f32[64,1,128]{2,1,0:T(1,128)} %get-tuple-element.52), calls=%async_computation.4 | async-start | bytes 65536 | tf_op jit(solution)/shard_map/all_to_all | solution.py:797

commit v4 on v3

--- a/solution.py
+++ b/solution.py
@@ -1,3 +1,5 @@
+import functools
+
 import jax
 import jax.numpy as jnp
 import numpy as np
@@ -40,8 +42,40 @@
     return lax.broadcasted_iota(jnp.int32, (count, index.shape[1]), 0) == index
 
 
+def rank_kernel(
+    owners, first_ref, shear_ref, couple_ref, routes_ref, counts_ref, here_ref, place_ref, mark_ref, own_ref
+):
+    depth = here_ref.shape[3]
+    own_ref[...] = here_ref[...]
+    owner = routes_ref[...]
+    chosen = jnp.where(hot_rows(owners, owner), 1.0, 0.0)
+    pieces = [chosen[:, k * depth : (k + 1) * depth] for k in range(4)]
+    earlier = lax.broadcasted_iota(jnp.int32, (depth, depth), 0) < lax.broadcasted_iota(
+        jnp.int32, (depth, depth), 1
+    )
+    within = jnp.dot(
+        jnp.concatenate(pieces, axis=0).astype(BF16),
+        jnp.where(earlier, 1.0, 0.0).astype(BF16),
+        preferred_element_type=F32,
+    )
+    running = jnp.zeros((owners, 1), F32)
+    ranks = []
+    for k in range(4):
+        seen = within[k * owners : (k + 1) * owners] + running
+        ranks.append(jnp.sum(pieces[k] * seen, axis=0, keepdims=True))
+        running = running + jnp.sum(pieces[k], axis=1, keepdims=True)
+    rank = jnp.concatenate(ranks, axis=1).astype(jnp.int32)
+    place_ref[0:1] = owner
+    place_ref[1:2] = rank
+    place_ref[2:3] = counts_ref[...]
+    axial = couple_ref[...].astype(F32)[:3]
+    stretch = jnp.sum(jnp.sum(axial * axial, axis=0, keepdims=True), axis=1, keepdims=True)
+    mark = (first_ref[...] + 2.0 * shear_ref[...] + stretch / 6.0) / owners
+    mark_ref[...] = mark
+
+
 def dispatch_kernel(
-    first_ref, shear_ref, couple_ref, routes_ref, counts_ref, own_ref, right_ref, above_ref, corner_ref, send_ref, place_ref
+    place_ref, mark_ref, own_ref, right_ref, above_ref, corner_ref, send_ref
 ):
     owners = send_ref.shape[0]
     depth = own_ref.shape[3]
@@ -78,28 +112,10 @@
                 )
             )
     values = jnp.concatenate(blocks, axis=1)
-    owner = routes_ref[...]
-    chosen = jnp.where(hot_rows(owners, owner), 1.0, 0.0)
-    pieces = [chosen[:, k * depth : (k + 1) * depth] for k in range(4)]
-    earlier = lax.broadcasted_iota(jnp.int32, (depth, depth), 0) < lax.broadcasted_iota(
-        jnp.int32, (depth, depth), 1
-    )
-    within = jnp.dot(
-        jnp.concatenate(pieces, axis=0).astype(BF16),
-        jnp.where(earlier, 1.0, 0.0).astype(BF16),
-        preferred_element_type=F32,
-    )
-    running = jnp.zeros((owners, 1), F32)
-    ranks = []
-    for k in range(4):
-        seen = within[k * owners : (k + 1) * owners] + running
-        ranks.append(jnp.sum(pieces[k] * seen, axis=0, keepdims=True))
-        running = running + jnp.sum(pieces[k], axis=1, keepdims=True)
-    rank = jnp.concatenate(ranks, axis=1).astype(jnp.int32)
-    place_ref[0:1] = owner
-    place_ref[1:2] = rank
+    chosen = jnp.where(hot_rows(owners, place_ref[0:1]), 1.0, 0.0)
+    rank = place_ref[1:2]
     at_rank = hot_rows(capacity, rank)
-    leaving = jnp.concatenate([values, counts_ref[...].astype(F32)], axis=0)
+    leaving = jnp.concatenate([values, place_ref[2:3].astype(F32)], axis=0)
     chosen = chosen.astype(BF16)
     total = None
     for part in three_parts(leaving):
@@ -115,10 +131,7 @@
         total = term if total is None else total + term
     lane = lax.broadcasted_iota(jnp.int32, (owners, 128), 1)
     send_ref[:, 0, :] = total[:, :128]
-    axial = couple_ref[...].astype(F32)[:3]
-    stretch = jnp.sum(jnp.sum(axial * axial, axis=0, keepdims=True), axis=1, keepdims=True)
-    mark = (first_ref[...] + 2.0 * shear_ref[...] + stretch / 6.0) / owners
-    send_ref[:, 1, :] = jnp.where(lane >= MARK, mark, total[:, 128:])
+    send_ref[:, 1, :] = jnp.where(lane >= MARK, mark_ref[...], total[:, 128:])
 
 
 def micro_kernel(
@@ -836,16 +849,24 @@
             for b in range(owners - 1)
         ],
     )
-    send, place = local_call(
-        dispatch_kernel,
-        ((owners, 2, 128), ((8, points), jnp.int32)),
-        "dispatch",
+    place, mark, kept = local_call(
+        functools.partial(rank_kernel, owners),
+        (((8, points), jnp.int32), (1, 1), displacement.shape),
+        "rank",
         lame_first.reshape(1, 1),
         lame_shear.reshape(1, 1),
         coupling[0].T,
         routes.reshape(1, points),
         counts.reshape(1, points),
         displacement,
+    )
+    (send,) = local_call(
+        dispatch_kernel,
+        ((owners, 2, 128),),
+        "dispatch",
+        place,
+        mark,
+        kept,
         right,
         above,
         corner,

time: 135 us -> 133 us (0.985)
  local copies, waits for them, and re-layouts: 5.45 us -> 1.93 us
    unnamed x19 -> x21, local copies, waits for them, and re-layouts: 3.67 us -> 0.85 us
    ppermute x1, waiting for transfers between devices: 2.64 us -> 0.01 us  [shards(): lax.ppermute(displacement, ('macro',) + MICRO, [((a + 1) * owners + b + 1...]
    ppermute x3, starting transfers between devices: 5.23 us -> 7.48 us  [gather_planes(): lax.ppermute(block, 'macro', [(k, (k - shift) % count) for k in range(cou...]
    all_to_all x2, waiting for transfers between devices: 17.3 us -> 18.7 us  [swapped(): return lax.all_to_all(block, MICRO, split_axis=0, concat_axis=0, tiled=True)]
    pallas_call x6 -> x7, Pallas kernels: 8.22 us -> 9.29 us  [local_call(): pl.pallas_call(kernel, in_specs=specs, out_specs=[pl.BlockSpec(memory_spa...]
  transfers between devices with their start and end apart: 14 -> 14, of which waited for: 8 -> 7; matrix products, arithmetic and copies ran while one was open for 2% -> 1% of each run, Pallas kernels for 0% -> 0%
where the time goes in v4:
time: 133 us; the launch traced here: 132 us
  starting transfers between devices  57.6 us (43%)
  waiting for transfers between devices  31.2 us (23%)
  Pallas kernels  21.7 us (16%)
  blocking collectives  15.9 us (12%)
  between operations  2.99 us (2%)
  local copies, waits for them, and re-layouts  1.93 us (1%)
    all_to_all x2, starting transfers between devices, swapped(): return lax.all_to_all(block, MICRO, split_axis=0, concat_axis=0, tiled=True)  24.4 us
    all_to_all x2, waiting for transfers between devices, swapped(): return lax.all_to_all(block, MICRO, split_axis=0, concat_axis=0, tiled=True)  18.7 us
    all_to_all x1, blocking collectives, swapped(): return lax.all_to_all(block, MICRO, split_axis=0, concat_axis=0, tiled=True)  15.9 us
    pallas_call x1, Pallas kernels, micro_solve(): pl.pallas_call(micro_kernel, grid=(2,), in_specs=[whole(owners, 2, 128),...  12.4 us
    ppermute x3, starting transfers between devices, up_and_down(): lax.ppermute(up, MICRO, forward)  12.2 us
    pallas_call x7, Pallas kernels, local_call(): pl.pallas_call(kernel, in_specs=specs, out_specs=[pl.BlockSpec(memory_spa...  9.29 us
    ppermute x3, starting transfers between devices, gather_planes(): lax.ppermute(block, 'macro', [(k, (k - shift) % count) for k in range(cou...  7.48 us
    ppermute x3, starting transfers between devices, up_and_down(): lax.ppermute(down, MICRO, backward)  5.76 us
  transfers between devices with their start and end apart: 14, of which 7 were waited for; matrix products, arithmetic and copies ran while one was open for 1% of the time, Pallas kernels for 0%

profile of v4, /device:TPU:1, one launch (start us, length us, event | category | flops | bytes accessed | tf_op | source)
XLA Modules:
  0.0 132.1 jit_solution(17457751566287844296)
XLA Ops:
  0.7 1.3 collective-permute-start.4
  2.0 1.3 collective-permute-start.6
  3.3 5.2 %collective-permute-start.5 = (f32[3,2,2,256]{3,2,1,0:T(2,128)}, f32[3,2,2,256]{3,2,1,0:T(2,128)S(1)}, u32[]{:S(2)}, u32[]{:S(2)}) collective-permute-start(f32[3,2,2,256]{3,2,1,0:T(2,128)} %here_ref.1), channel_id=1, source_target_pairs={{1,0},{2,1},{3,2},{4,3},{5,4},{6,5},{7,6},{8,7},{9,8},{10,9},{11,1... | collective-permute-start | bytes 36872 | tf_op jit(solution)/shard_map/ppermute | solution.py:842
  9.7 0.7 bitcast_convert_fusion
  11.2 0.6 rank.1
  11.8 1.9 %dispatch.1 = f32[64,2,128]{2,1,0:T(2,128)} custom-call(s32[8,1024]{1,0:T(8,128)S(1)} %get-tuple-element.45.place_ref, f32[1,1]{1,0:T(1,128)} %get-tuple-element.46.mark_ref, f32[3,2,2,256]{3,2,1,0:T(2,128)S(1)} %get-tuple-element.47.own_ref, f32[3,2,2,256]{3,2,1,0:T(2,128)S(1)} %collective-permute-done.4.right_ref, ...), custom_call_target="tpu_custom_call" | custom-call | tf_op jit(solution)/shard_map/dispatch/pallas_call | solution.py:791
  13.6 10.1 %all-to-all-start.2 = ((f32[64,2,128]{2,1,0:T(2,128)}), f32[64,2,128]{2,1,0:T(2,128)S(1)}, u32[]{:S(2)}, u32[]{:S(2)}) async-start(f32[64,2,128]{2,1,0:T(2,128)} %dispatch.1), calls=%async_computation.2 | async-start | bytes 131072 | tf_op jit(solution)/shard_map/all_to_all | solution.py:810
  24.1 9.4 %all-to-all-done.2.got_ref = f32[64,2,128]{2,1,0:T(2,128)S(1)} async-done(((f32[64,2,128]{2,1,0:T(2,128)}), f32[64,2,128]{2,1,0:T(2,128)S(1)}, u32[]{:S(2)}, u32[]{:S(2)}) %all-to-all-start.2) | async-done | bytes 65568 | tf_op jit(solution)/shard_map/all_to_all | solution.py:810
  33.5 12.4 %micro_solve.1 = (f32[64,8,128]{2,1,0:T(8,128)S(1)}, f32[1,128]{1,0:T(1,128)S(1)}) custom-call(f32[64,2,128]{2,1,0:T(2,128)S(1)} %all-to-all-done.2.got_ref, bf16[512,512]{1,0:T(8,128)(2,1)S(1)} %bitcast.22, bf16[512,512]{1,0:T(8,128)(2,1)S(1)} %bitcast.23, bf16[512,8]{1,0:T(8,128)(2,1)S(1)} %pad_bitcast_fusion.force_ref, ...), custom_call_target="tpu_custom_call" | custom-call | tf_op jit(solution)/shard_map/micro_solve/pallas_call | solution.py:233
  45.9 15.9 %all_to_all.25.back_ref = f32[64,8,128]{2,1,0:T(8,128)S(1)} all-to-all(f32[64,8,128]{2,1,0:T(8,128)S(1)} %get-tuple-element.49), channel_id=1, replica_groups=mesh['macro'=4,'micro_0'=4,'micro_1'=8,'micro_2'=2] {'micro_0','micro_1'..., dimensions={0} | all-to-all | bytes 524288 | tf_op jit(solution)/shard_map/all_to_all | solution.py:810
  61.8 1.3 pick.1
  63.1 3.0 %collective-permute-start.9 = (f32[30,2,2,256]{3,2,1,0:T(2,128)S(1)}, f32[30,2,2,256]{3,2,1,0:T(2,128)S(1)}, u32[]{:S(2)}, u32[]{:S(2)}) collective-permute-start(f32[30,2,2,256]{3,2,1,0:T(2,128)S(1)} %pick.1), channel_id=1, source_target_pairs={{0,64},{64,128},{128,192},{192,0},{1,65},{65,129},{129,193},{193,1... | collective-permute-start | bytes 368648 | tf_op jit(solution)/shard_map/ppermute | solution.py:816
  66.1 3.6 %collective-permute-start.8 = (f32[30,2,2,256]{3,2,1,0:T(2,128)S(1)}, f32[30,2,2,256]{3,2,1,0:T(2,128)S(1)}, u32[]{:S(2)}, u32[]{:S(2)}) collective-permute-start(f32[30,2,2,256]{3,2,1,0:T(2,128)S(1)} %pick.1), channel_id=1, source_target_pairs={{0,128},{64,192},{128,0},{192,64},{1,129},{65,193},{129,1},{193,65... | collective-permute-start | bytes 368648 | tf_op jit(solution)/shard_map/ppermute | solution.py:816
  69.7 0.9 collective-permute-start.7
  70.6 1.2 collective-permute-done.9
  71.8 3.5 %collective-permute-done.8 = f32[30,2,2,256]{3,2,1,0:T(2,128)S(1)} collective-permute-done((f32[30,2,2,256]{3,2,1,0:T(2,128)S(1)}, f32[30,2,2,256]{3,2,1,0:T(2,128)S(1)}, u32[]{:S(2)}, u32[]{:S(2)}) %collective-permute-start.8) | collective-permute-done | bytes 122912 | tf_op jit(solution)/shard_map/ppermute | solution.py:816
  75.3 0.8 concatenate.3
  76.2 4.3 %collective-permute-start.10 = (f32[30,2,8,256]{3,2,1,0:T(8,128)S(1)}, f32[30,2,8,256]{3,2,1,0:T(8,128)S(1)}, u32[]{:S(2)}, u32[]{:S(2)}) collective-permute-start(f32[30,2,8,256]{3,2,1,0:T(8,128)S(1)} %constant_dynamic-slice_fusion.1.own_ref), channel_id=1, source_target_pairs={{0,1},{1,2},{2,3},{3,4},{4,5},{5,6},{6,7},{7,8},{8,9},{9,10},{10,1... | collective-permute-start | bytes 1474568 | tf_op jit(solution)/shard_map/ppermute | solution.py:806
  80.6 1.9 %collective-permute-start.11 = (f32[30,1,8,256]{3,2,1,0:T(8,128)S(1)}, f32[30,1,8,256]{3,2,1,0:T(8,128)S(1)}, u32[]{:S(2)}, u32[]{:S(2)}) collective-permute-start(f32[30,1,8,256]{3,2,1,0:T(8,128)S(1)} %constant_dynamic-slice_fusion), channel_id=1, source_target_pairs={{1,0},{2,1},{3,2},{4,3},{5,4},{6,5},{7,6},{8,7},{9,8},{10,9},{11,1... | collective-permute-start | bytes 737288 | tf_op jit(solution)/shard_map/ppermute | solution.py:806
  82.6 5.5 %collective-permute-done.11.high_ref = f32[30,1,8,256]{3,2,1,0:T(8,128)S(1)} collective-permute-done((f32[30,1,8,256]{3,2,1,0:T(8,128)S(1)}, f32[30,1,8,256]{3,2,1,0:T(8,128)S(1)}, u32[]{:S(2)}, u32[]{:S(2)}) %collective-permute-start.11) | collective-permute-done | bytes 245792 | tf_op jit(solution)/shard_map/ppermute | solution.py:806
  88.1 0.9 first_rows.1
  89.0 1.9 %collective-permute-start.13 = (f32[3,2,8,256]{3,2,1,0:T(8,128)S(1)}, f32[3,2,8,256]{3,2,1,0:T(8,128)S(1)}, u32[]{:S(2)}, u32[]{:S(2)}) collective-permute-start(f32[3,2,8,256]{3,2,1,0:T(8,128)S(1)} %get-tuple-element.51.v1_ref), channel_id=1, source_target_pairs={{1,0},{2,1},{3,2},{4,3},{5,4},{6,5},{7,6},{8,7},{9,8},{10,9},{11,1... | collective-permute-start | bytes 147464 | tf_op jit(solution)/shard_map/ppermute | solution.py:806
  90.9 3.6 %collective-permute-start.12 = (f32[3,2,8,256]{3,2,1,0:T(8,128)S(1)}, f32[3,2,8,256]{3,2,1,0:T(8,128)S(1)}, u32[]{:S(2)}, u32[]{:S(2)}) collective-permute-start(f32[3,2,8,256]{3,2,1,0:T(8,128)S(1)} %get-tuple-element.51.v1_ref), channel_id=1, source_target_pairs={{0,1},{1,2},{2,3},{3,4},{4,5},{5,6},{6,7},{7,8},{8,9},{9,10},{10,1... | collective-permute-start | bytes 147464 | tf_op jit(solution)/shard_map/ppermute | solution.py:806
  94.6 1.1 collective-permute-done.12.v1_low_ref
  95.7 1.2 second_rows.1
  97.0 1.9 %collective-permute-start.15 = (f32[3,2,8,256]{3,2,1,0:T(8,128)S(1)}, f32[3,2,8,256]{3,2,1,0:T(8,128)S(1)}, u32[]{:S(2)}, u32[]{:S(2)}) collective-permute-start(f32[3,2,8,256]{3,2,1,0:T(8,128)S(1)} %get-tuple-element.53.v3_ref), channel_id=1, source_target_pairs={{1,0},{2,1},{3,2},{4,3},{5,4},{6,5},{7,6},{8,7},{9,8},{10,9},{11,1... | collective-permute-start | bytes 147464 | tf_op jit(solution)/shard_map/ppermute | solution.py:806
  98.9 4.2 %collective-permute-start.14 = (f32[3,2,8,256]{3,2,1,0:T(8,128)S(1)}, f32[3,2,8,256]{3,2,1,0:T(8,128)S(1)}, u32[]{:S(2)}, u32[]{:S(2)}) collective-permute-start(f32[3,2,8,256]{3,2,1,0:T(8,128)S(1)} %get-tuple-element.53.v3_ref), channel_id=1, source_target_pairs={{0,1},{1,2},{2,3},{3,4},{4,5},{5,6},{6,7},{7,8},{8,9},{9,10},{10,1... | collective-permute-start | bytes 147464 | tf_op jit(solution)/shard_map/ppermute | solution.py:806
  103.2 1.1 collective-permute-done.14.v3_low_ref
  104.3 1.9 %third_rows.1 = (f32[3,2,8,256]{3,2,1,0:T(8,128)S(1)}, f32[3,2,8,256]{3,2,1,0:T(8,128)S(1)}, f32[64,1,128]{2,1,0:T(1,128)}) custom-call(s32[2]{0:T(128)S(1)} %pad_add_fusion.flags_ref, f32[1,128]{1,0:T(1,128)S(1)} %get-tuple-element.48.marks_ref, f32[30,2,8,256]{3,2,1,0:T(8,128)S(1)} %collective-permute-done.10.low_ref, ...), custom_call_target="tpu_custom_call" | custom-call | tf_op jit(solution)/shard_map/third_rows/pallas_call | solution.py:791
  106.2 14.4 %all-to-all-start.4 = ((f32[64,1,128]{2,1,0:T(1,128)}), f32[64,1,128]{2,1,0:T(1,128)S(1)}, u32[]{:S(2)}, u32[]{:S(2)}) async-start(f32[64,1,128]{2,1,0:T(1,128)} %get-tuple-element.54), calls=%async_computation.4 | async-start | bytes 65536 | tf_op jit(solution)/shard_map/all_to_all | solution.py:810
  120.6 9.3 %all-to-all-done.4.sums_ref = f32[64,1,128]{2,1,0:T(1,128)S(1)} async-done(((f32[64,1,128]{2,1,0:T(1,128)}), f32[64,1,128]{2,1,0:T(1,128)S(1)}, u32[]{:S(2)}, u32[]{:S(2)}) %all-to-all-start.4) | async-done | bytes 32800 | tf_op jit(solution)/shard_map/all_to_all | solution.py:810
  129.9 1.5 %fourth_rows.1 = (f32[3,2,2,256]{3,2,1,0:T(2,128)}, f32[3,2,2,256]{3,2,1,0:T(2,128)}, s32[1,1]{1,0:T(1,128)}) custom-call(s32[2]{0:T(128)S(1)} %pad_add_fusion.flags_ref, f32[1,128]{1,0:T(1,128)S(1)} %get-tuple-element.48.marks_ref, f32[64,1,128]{2,1,0:T(1,128)S(1)} %all-to-all-done.4.sums_ref, f32[3,4,8,256]{3,2,1,0:T(8,128)S(1)} %get-tuple-element.50.v0_ref, ...), custom_call_target="tpu_custom_call" | custom-call | tf_op jit(solution)/shard_map/fourth_rows/pallas_call | solution.py:791
  (39 shorter events, 1.3 us)
Async XLA Ops:
  0.6 9.8 %copy-start.8 = (f32[32,8]{1,0:T(8,128)S(1)}, f32[32,8]{1,0:T(8,128)}, u32[]{:S(2)}) copy-start(f32[32,8]{1,0:T(8,128)} %constant.51.clone) | copy-start | bytes 3076
  0.6 9.8 %copy-start.7 = (f32[32,8]{1,0:T(8,128)S(1)}, f32[32,8]{1,0:T(8,128)}, u32[]{:S(2)}) copy-start(f32[32,8]{1,0:T(8,128)} %constant.52.clone) | copy-start | bytes 3076
  0.7 11.1 %collective-permute-start.4 = (f32[3,2,2,256]{3,2,1,0:T(2,128)}, f32[3,2,2,256]{3,2,1,0:T(2,128)S(1)}, u32[]{:S(2)}, u32[]{:S(2)}) collective-permute-start(f32[3,2,2,256]{3,2,1,0:T(2,128)} %here_ref.1), channel_id=1, source_target_pairs={{64,0},{128,64},{192,128},{65,1},{129,65},{193,129},{66,2},{130,66... | collective-permute-start | bytes 36872 | tf_op jit(solution)/shard_map/ppermute | solution.py:841
  2.0 9.8 %collective-permute-start.6 = (f32[3,2,2,256]{3,2,1,0:T(2,128)}, f32[3,2,2,256]{3,2,1,0:T(2,128)S(1)}, u32[]{:S(2)}, u32[]{:S(2)}) collective-permute-start(f32[3,2,2,256]{3,2,1,0:T(2,128)} %here_ref.1), channel_id=1, source_target_pairs={{65,0},{66,1},{67,2},{68,3},{69,4},{70,5},{71,6},{72,7},{73,8},{74... | collective-permute-start | bytes 36872 | tf_op jit(solution)/shard_map/ppermute | solution.py:843
  3.3 8.5 %collective-permute-start.5 = (f32[3,2,2,256]{3,2,1,0:T(2,128)}, f32[3,2,2,256]{3,2,1,0:T(2,128)S(1)}, u32[]{:S(2)}, u32[]{:S(2)}) collective-permute-start(f32[3,2,2,256]{3,2,1,0:T(2,128)} %here_ref.1), channel_id=1, source_target_pairs={{1,0},{2,1},{3,2},{4,3},{5,4},{6,5},{7,6},{8,7},{9,8},{10,9},{11,1... | collective-permute-start | bytes 36872 | tf_op jit(solution)/shard_map/ppermute | solution.py:842
  10.4 0.7 copy-start.2
  10.4 0.7 copy-start.3
  10.4 0.7 copy-start.5
  10.5 0.7 copy-start.6
  10.5 13.3 %copy-start.9 = (bf16[1,6,512]{2,1,0:T(8,128)(2,1)S(1)}, bf16[1,6,512]{2,1,0:T(8,128)(2,1)}, u32[]{:S(2)}) copy-start(bf16[1,6,512]{2,1,0:T(8,128)(2,1)} %param.20) | copy-start | bytes 18436
  10.5 23.0 %copy-start.1 = (bf16[1,512,512]{2,1,0:T(8,128)(2,1)S(1)}, bf16[1,512,512]{2,1,0:T(8,128)(2,1)}, u32[]{:S(2)}) copy-start(bf16[1,512,512]{2,1,0:T(8,128)(2,1)} %param.19) | copy-start | bytes 1572868
  10.5 23.0 %copy-start = (bf16[1,512,512]{2,1,0:T(8,128)(2,1)S(1)}, bf16[1,512,512]{2,1,0:T(8,128)(2,1)}, u32[]{:S(2)}) copy-start(bf16[1,512,512]{2,1,0:T(8,128)(2,1)} %param.18) | copy-start | bytes 1572868
  13.6 19.9 %all-to-all-start.2 = ((f32[64,2,128]{2,1,0:T(2,128)}), f32[64,2,128]{2,1,0:T(2,128)S(1)}, u32[]{:S(2)}, u32[]{:S(2)}) async-start(f32[64,2,128]{2,1,0:T(2,128)} %dispatch.1), calls=%async_computation.2 | async-start | bytes 131072 | tf_op jit(solution)/shard_map/all_to_all | solution.py:810
  45.9 15.9 %copy-start.4 = (f32[3,2,2,256]{3,2,1,0:T(2,128)S(1)}, f32[3,2,2,256]{3,2,1,0:T(2,128)}, u32[]{:S(2)}) copy-start(f32[3,2,2,256]{3,2,1,0:T(2,128)} %load_ref.1) | copy-start | bytes 36868
  63.1 8.7 %collective-permute-start.9 = (f32[30,2,2,256]{3,2,1,0:T(2,128)S(1)}, f32[30,2,2,256]{3,2,1,0:T(2,128)S(1)}, u32[]{:S(2)}, u32[]{:S(2)}) collective-permute-start(f32[30,2,2,256]{3,2,1,0:T(2,128)S(1)} %pick.1), channel_id=1, source_target_pairs={{0,64},{64,128},{128,192},{192,0},{1,65},{65,129},{129,193},{193,1... | collective-permute-start | bytes 368648 | tf_op jit(solution)/shard_map/ppermute | solution.py:816
  66.1 9.2 %collective-permute-start.8 = (f32[30,2,2,256]{3,2,1,0:T(2,128)S(1)}, f32[30,2,2,256]{3,2,1,0:T(2,128)S(1)}, u32[]{:S(2)}, u32[]{:S(2)}) collective-permute-start(f32[30,2,2,256]{3,2,1,0:T(2,128)S(1)} %pick.1), channel_id=1, source_target_pairs={{0,128},{64,192},{128,0},{192,64},{1,129},{65,193},{129,1},{193,65... | collective-permute-start | bytes 368648 | tf_op jit(solution)/shard_map/ppermute | solution.py:816
  69.7 5.6 %collective-permute-start.7 = (f32[30,2,2,256]{3,2,1,0:T(2,128)S(1)}, f32[30,2,2,256]{3,2,1,0:T(2,128)S(1)}, u32[]{:S(2)}, u32[]{:S(2)}) collective-permute-start(f32[30,2,2,256]{3,2,1,0:T(2,128)S(1)} %pick.1), channel_id=1, source_target_pairs={{0,192},{64,0},{128,64},{192,128},{1,193},{65,1},{129,65},{193,129... | collective-permute-start | bytes 368648 | tf_op jit(solution)/shard_map/ppermute | solution.py:816
  76.2 11.9 %collective-permute-start.10 = (f32[30,2,8,256]{3,2,1,0:T(8,128)S(1)}, f32[30,2,8,256]{3,2,1,0:T(8,128)S(1)}, u32[]{:S(2)}, u32[]{:S(2)}) collective-permute-start(f32[30,2,8,256]{3,2,1,0:T(8,128)S(1)} %constant_dynamic-slice_fusion.1.own_ref), channel_id=1, source_target_pairs={{0,1},{1,2},{2,3},{3,4},{4,5},{5,6},{6,7},{7,8},{8,9},{9,10},{10,1... | collective-permute-start | bytes 1474568 | tf_op jit(solution)/shard_map/ppermute | solution.py:806
  80.6 7.5 %collective-permute-start.11 = (f32[30,1,8,256]{3,2,1,0:T(8,128)S(1)}, f32[30,1,8,256]{3,2,1,0:T(8,128)S(1)}, u32[]{:S(2)}, u32[]{:S(2)}) collective-permute-start(f32[30,1,8,256]{3,2,1,0:T(8,128)S(1)} %constant_dynamic-slice_fusion), channel_id=1, source_target_pairs={{1,0},{2,1},{3,2},{4,3},{5,4},{6,5},{7,6},{8,7},{9,8},{10,9},{11,1... | collective-permute-start | bytes 737288 | tf_op jit(solution)/shard_map/ppermute | solution.py:806
  89.0 5.6 %collective-permute-start.13 = (f32[3,2,8,256]{3,2,1,0:T(8,128)S(1)}, f32[3,2,8,256]{3,2,1,0:T(8,128)S(1)}, u32[]{:S(2)}, u32[]{:S(2)}) collective-permute-start(f32[3,2,8,256]{3,2,1,0:T(8,128)S(1)} %get-tuple-element.51.v1_ref), channel_id=1, source_target_pairs={{1,0},{2,1},{3,2},{4,3},{5,4},{6,5},{7,6},{8,7},{9,8},{10,9},{11,1... | collective-permute-start | bytes 147464 | tf_op jit(solution)/shard_map/ppermute | solution.py:806
  90.9 4.8 %collective-permute-start.12 = (f32[3,2,8,256]{3,2,1,0:T(8,128)S(1)}, f32[3,2,8,256]{3,2,1,0:T(8,128)S(1)}, u32[]{:S(2)}, u32[]{:S(2)}) collective-permute-start(f32[3,2,8,256]{3,2,1,0:T(8,128)S(1)} %get-tuple-element.51.v1_ref), channel_id=1, source_target_pairs={{0,1},{1,2},{2,3},{3,4},{4,5},{5,6},{6,7},{7,8},{8,9},{9,10},{10,1... | collective-permute-start | bytes 147464 | tf_op jit(solution)/shard_map/ppermute | solution.py:806
  97.0 6.2 %collective-permute-start.15 = (f32[3,2,8,256]{3,2,1,0:T(8,128)S(1)}, f32[3,2,8,256]{3,2,1,0:T(8,128)S(1)}, u32[]{:S(2)}, u32[]{:S(2)}) collective-permute-start(f32[3,2,8,256]{3,2,1,0:T(8,128)S(1)} %get-tuple-element.53.v3_ref), channel_id=1, source_target_pairs={{1,0},{2,1},{3,2},{4,3},{5,4},{6,5},{7,6},{8,7},{9,8},{10,9},{11,1... | collective-permute-start | bytes 147464 | tf_op jit(solution)/shard_map/ppermute | solution.py:806
  98.9 5.4 %collective-permute-start.14 = (f32[3,2,8,256]{3,2,1,0:T(8,128)S(1)}, f32[3,2,8,256]{3,2,1,0:T(8,128)S(1)}, u32[]{:S(2)}, u32[]{:S(2)}) collective-permute-start(f32[3,2,8,256]{3,2,1,0:T(8,128)S(1)} %get-tuple-element.53.v3_ref), channel_id=1, source_target_pairs={{0,1},{1,2},{2,3},{3,4},{4,5},{5,6},{6,7},{7,8},{8,9},{9,10},{10,1... | collective-permute-start | bytes 147464 | tf_op jit(solution)/shard_map/ppermute | solution.py:806
  106.2 23.6 %all-to-all-start.4 = ((f32[64,1,128]{2,1,0:T(1,128)}), f32[64,1,128]{2,1,0:T(1,128)S(1)}, u32[]{:S(2)}, u32[]{:S(2)}) async-start(f32[64,1,128]{2,1,0:T(1,128)} %get-tuple-element.54), calls=%async_computation.4 | async-start | bytes 65536 | tf_op jit(solution)/shard_map/all_to_all | solution.py:810

commit v5 on v4

--- a/solution.py
+++ b/solution.py
@@ -185,16 +185,18 @@
     products = products_ref[...]
     high = products.astype(BF16)
     low = (products - high.astype(F32)).astype(BF16)
+    both = jnp.concatenate([high, low], axis=0)
     cols = cols_ref[...]
     for h in range(halves):
         bent = jnp.tanh(modes[h])
         slope = 1.0 - bent * bent
         slope_high = slope.astype(BF16)
         slope_low = (slope - slope_high.astype(F32)).astype(BF16)
+        curved = jnp.dot(both, slope_high, preferred_element_type=F32)
         rows = (
             jnp.dot(couple, modes[h].astype(BF16), preferred_element_type=F32)
-            + jnp.dot(high, slope_high, preferred_element_type=F32)
-            + jnp.dot(low, slope_high, preferred_element_type=F32)
+            + curved[:32]
+            + curved[32:]
             + jnp.dot(high, slope_low, preferred_element_type=F32)
             + cols[:, 0:1]
         )
@@ -871,6 +873,7 @@
         above,
         corner,
     )
+    send, forcing, coupling = lax.optimization_barrier((send, forcing, coupling))
     back, marks = micro_solve(
         swapped(send),
         stiffness[0],

time: 133 us -> 132 us (level)
  transfers between devices with their start and end apart: 14 -> 14, of which waited for: 7 -> 7; matrix products, arithmetic and copies ran while one was open for 1% -> 0% of each run, Pallas kernels for 0% -> 0%
where the time goes in v5:
time: 132 us
  starting transfers between devices  58.2 us (44%)
  waiting for transfers between devices  31.2 us (24%)
  Pallas kernels  21.4 us (16%)
  blocking collectives  15.9 us (12%)
  between operations  3.02 us (2%)
  local copies, waits for them, and re-layouts  1.99 us (2%)
    all_to_all x2, starting transfers between devices, swapped(): return lax.all_to_all(block, MICRO, split_axis=0, concat_axis=0, tiled=True)  25.1 us
    all_to_all x2, waiting for transfers between devices, swapped(): return lax.all_to_all(block, MICRO, split_axis=0, concat_axis=0, tiled=True)  18.6 us
    all_to_all x1, blocking collectives, swapped(): return lax.all_to_all(block, MICRO, split_axis=0, concat_axis=0, tiled=True)  15.9 us
    ppermute x3, starting transfers between devices, up_and_down(): lax.ppermute(up, MICRO, forward)  12.2 us
    pallas_call x1, Pallas kernels, micro_solve(): pl.pallas_call(micro_kernel, grid=(2,), in_specs=[whole(owners, 2, 128),...  12 us
    pallas_call x7, Pallas kernels, local_call(): pl.pallas_call(kernel, in_specs=specs, out_specs=[pl.BlockSpec(memory_spa...  9.38 us
    ppermute x3, starting transfers between devices, gather_planes(): lax.ppermute(block, 'macro', [(k, (k - shift) % count) for k in range(cou...  7.47 us
    ppermute x3, starting transfers between devices, up_and_down(): lax.ppermute(down, MICRO, backward)  5.76 us
  transfers between devices with their start and end apart: 14, of which 7 were waited for; matrix products, arithmetic and copies ran while one was open for 0% of the time, Pallas kernels for 0%

profile of v5, /device:TPU:1, one launch (start us, length us, event | category | flops | bytes accessed | tf_op | source)
XLA Modules:
  0.0 131.8 jit_solution(17220722253565511221)
XLA Ops:
  0.7 1.3 collective-permute-start.4
  2.0 1.3 collective-permute-start.6
  3.3 5.1 %collective-permute-start.5 = (f32[3,2,2,256]{3,2,1,0:T(2,128)}, f32[3,2,2,256]{3,2,1,0:T(2,128)S(1)}, u32[]{:S(2)}, u32[]{:S(2)}) collective-permute-start(f32[3,2,2,256]{3,2,1,0:T(2,128)} %here_ref.1), channel_id=1, source_target_pairs={{1,0},{2,1},{3,2},{4,3},{5,4},{6,5},{7,6},{8,7},{9,8},{10,9},{11,1... | collective-permute-start | bytes 36872 | tf_op jit(solution)/shard_map/ppermute | solution.py:844
  9.8 0.7 copy-done.3
  10.5 0.6 rank.1
  11.1 1.9 %dispatch.1 = f32[64,2,128]{2,1,0:T(2,128)} custom-call(s32[8,1024]{1,0:T(8,128)S(1)} %get-tuple-element.48.place_ref, f32[1,1]{1,0:T(1,128)} %get-tuple-element.49.mark_ref, f32[3,2,2,256]{3,2,1,0:T(2,128)S(1)} %get-tuple-element.50.own_ref, f32[3,2,2,256]{3,2,1,0:T(2,128)S(1)} %collective-permute-done.4.right_ref, ...), custom_call_target="tpu_custom_call" | custom-call | tf_op jit(solution)/shard_map/dispatch/pallas_call | solution.py:793
  13.1 10.7 %all-to-all-start.2 = ((f32[64,2,128]{2,1,0:T(2,128)}), f32[64,2,128]{2,1,0:T(2,128)S(1)}, u32[]{:S(2)}, u32[]{:S(2)}) async-start(f32[64,2,128]{2,1,0:T(2,128)} %dispatch.1), calls=%async_computation.2 | async-start | bytes 131072 | tf_op jit(solution)/shard_map/all_to_all | solution.py:812
  24.2 9.4 %all-to-all-done.2.got_ref = f32[64,2,128]{2,1,0:T(2,128)S(1)} async-done(((f32[64,2,128]{2,1,0:T(2,128)}), f32[64,2,128]{2,1,0:T(2,128)S(1)}, u32[]{:S(2)}, u32[]{:S(2)}) %all-to-all-start.2) | async-done | bytes 65568 | tf_op jit(solution)/shard_map/all_to_all | solution.py:812
  33.6 12.0 %micro_solve.1 = (f32[64,8,128]{2,1,0:T(8,128)S(1)}, f32[1,128]{1,0:T(1,128)S(1)}) custom-call(f32[64,2,128]{2,1,0:T(2,128)S(1)} %all-to-all-done.2.got_ref, bf16[512,512]{1,0:T(8,128)(2,1)S(1)} %bitcast.25, bf16[512,512]{1,0:T(8,128)(2,1)S(1)} %bitcast.26, bf16[512,8]{1,0:T(8,128)(2,1)S(1)} %pad_bitcast_fusion.force_ref, ...), custom_call_target="tpu_custom_call" | custom-call | tf_op jit(solution)/shard_map/micro_solve/pallas_call | solution.py:235
  45.7 15.9 %all_to_all.25.back_ref = f32[64,8,128]{2,1,0:T(8,128)S(1)} all-to-all(f32[64,8,128]{2,1,0:T(8,128)S(1)} %get-tuple-element.55), channel_id=1, replica_groups=mesh['macro'=4,'micro_0'=4,'micro_1'=8,'micro_2'=2] {'micro_0','micro_1'..., dimensions={0} | all-to-all | bytes 524288 | tf_op jit(solution)/shard_map/all_to_all | solution.py:812
  61.5 1.3 pick.1
  62.8 2.8 %collective-permute-start.9 = (f32[30,2,2,256]{3,2,1,0:T(2,128)S(1)}, f32[30,2,2,256]{3,2,1,0:T(2,128)S(1)}, u32[]{:S(2)}, u32[]{:S(2)}) collective-permute-start(f32[30,2,2,256]{3,2,1,0:T(2,128)S(1)} %pick.1), channel_id=1, source_target_pairs={{0,64},{64,128},{128,192},{192,0},{1,65},{65,129},{129,193},{193,1... | collective-permute-start | bytes 368648 | tf_op jit(solution)/shard_map/ppermute | solution.py:818
  65.6 3.8 %collective-permute-start.8 = (f32[30,2,2,256]{3,2,1,0:T(2,128)S(1)}, f32[30,2,2,256]{3,2,1,0:T(2,128)S(1)}, u32[]{:S(2)}, u32[]{:S(2)}) collective-permute-start(f32[30,2,2,256]{3,2,1,0:T(2,128)S(1)} %pick.1), channel_id=1, source_target_pairs={{0,128},{64,192},{128,0},{192,64},{1,129},{65,193},{129,1},{193,65... | collective-permute-start | bytes 368648 | tf_op jit(solution)/shard_map/ppermute | solution.py:818
  69.4 0.9 collective-permute-start.7
  70.3 1.3 collective-permute-done.9
  71.6 3.5 %collective-permute-done.8 = f32[30,2,2,256]{3,2,1,0:T(2,128)S(1)} collective-permute-done((f32[30,2,2,256]{3,2,1,0:T(2,128)S(1)}, f32[30,2,2,256]{3,2,1,0:T(2,128)S(1)}, u32[]{:S(2)}, u32[]{:S(2)}) %collective-permute-start.8) | collective-permute-done | bytes 122912 | tf_op jit(solution)/shard_map/ppermute | solution.py:818
  75.1 0.8 concatenate.3
  76.0 4.3 %collective-permute-start.10 = (f32[30,2,8,256]{3,2,1,0:T(8,128)S(1)}, f32[30,2,8,256]{3,2,1,0:T(8,128)S(1)}, u32[]{:S(2)}, u32[]{:S(2)}) collective-permute-start(f32[30,2,8,256]{3,2,1,0:T(8,128)S(1)} %constant_dynamic-slice_fusion.1.own_ref), channel_id=1, source_target_pairs={{0,1},{1,2},{2,3},{3,4},{4,5},{5,6},{6,7},{7,8},{8,9},{9,10},{10,1... | collective-permute-start | bytes 1474568 | tf_op jit(solution)/shard_map/ppermute | solution.py:808
  80.3 1.9 %collective-permute-start.11 = (f32[30,1,8,256]{3,2,1,0:T(8,128)S(1)}, f32[30,1,8,256]{3,2,1,0:T(8,128)S(1)}, u32[]{:S(2)}, u32[]{:S(2)}) collective-permute-start(f32[30,1,8,256]{3,2,1,0:T(8,128)S(1)} %constant_dynamic-slice_fusion), channel_id=1, source_target_pairs={{1,0},{2,1},{3,2},{4,3},{5,4},{6,5},{7,6},{8,7},{9,8},{10,9},{11,1... | collective-permute-start | bytes 737288 | tf_op jit(solution)/shard_map/ppermute | solution.py:808
  82.3 5.5 %collective-permute-done.11.high_ref = f32[30,1,8,256]{3,2,1,0:T(8,128)S(1)} collective-permute-done((f32[30,1,8,256]{3,2,1,0:T(8,128)S(1)}, f32[30,1,8,256]{3,2,1,0:T(8,128)S(1)}, u32[]{:S(2)}, u32[]{:S(2)}) %collective-permute-start.11) | collective-permute-done | bytes 245792 | tf_op jit(solution)/shard_map/ppermute | solution.py:808
  87.8 0.9 first_rows.1
  88.7 1.9 %collective-permute-start.13 = (f32[3,2,8,256]{3,2,1,0:T(8,128)S(1)}, f32[3,2,8,256]{3,2,1,0:T(8,128)S(1)}, u32[]{:S(2)}, u32[]{:S(2)}) collective-permute-start(f32[3,2,8,256]{3,2,1,0:T(8,128)S(1)} %get-tuple-element.57.v1_ref), channel_id=1, source_target_pairs={{1,0},{2,1},{3,2},{4,3},{5,4},{6,5},{7,6},{8,7},{9,8},{10,9},{11,1... | collective-permute-start | bytes 147464 | tf_op jit(solution)/shard_map/ppermute | solution.py:808
  90.7 3.6 %collective-permute-start.12 = (f32[3,2,8,256]{3,2,1,0:T(8,128)S(1)}, f32[3,2,8,256]{3,2,1,0:T(8,128)S(1)}, u32[]{:S(2)}, u32[]{:S(2)}) collective-permute-start(f32[3,2,8,256]{3,2,1,0:T(8,128)S(1)} %get-tuple-element.57.v1_ref), channel_id=1, source_target_pairs={{0,1},{1,2},{2,3},{3,4},{4,5},{5,6},{6,7},{7,8},{8,9},{9,10},{10,1... | collective-permute-start | bytes 147464 | tf_op jit(solution)/shard_map/ppermute | solution.py:808
  94.3 1.1 collective-permute-done.12.v1_low_ref
  95.5 1.2 second_rows.1
  96.7 1.9 %collective-permute-start.15 = (f32[3,2,8,256]{3,2,1,0:T(8,128)S(1)}, f32[3,2,8,256]{3,2,1,0:T(8,128)S(1)}, u32[]{:S(2)}, u32[]{:S(2)}) collective-permute-start(f32[3,2,8,256]{3,2,1,0:T(8,128)S(1)} %get-tuple-element.59.v3_ref), channel_id=1, source_target_pairs={{1,0},{2,1},{3,2},{4,3},{5,4},{6,5},{7,6},{8,7},{9,8},{10,9},{11,1... | collective-permute-start | bytes 147464 | tf_op jit(solution)/shard_map/ppermute | solution.py:808
  98.6 4.2 %collective-permute-start.14 = (f32[3,2,8,256]{3,2,1,0:T(8,128)S(1)}, f32[3,2,8,256]{3,2,1,0:T(8,128)S(1)}, u32[]{:S(2)}, u32[]{:S(2)}) collective-permute-start(f32[3,2,8,256]{3,2,1,0:T(8,128)S(1)} %get-tuple-element.59.v3_ref), channel_id=1, source_target_pairs={{0,1},{1,2},{2,3},{3,4},{4,5},{5,6},{6,7},{7,8},{8,9},{9,10},{10,1... | collective-permute-start | bytes 147464 | tf_op jit(solution)/shard_map/ppermute | solution.py:808
  102.9 1.1 collective-permute-done.14.v3_low_ref
  104.0 1.9 %third_rows.1 = (f32[3,2,8,256]{3,2,1,0:T(8,128)S(1)}, f32[3,2,8,256]{3,2,1,0:T(8,128)S(1)}, f32[64,1,128]{2,1,0:T(1,128)}) custom-call(s32[2]{0:T(128)S(1)} %pad_add_fusion.flags_ref, f32[1,128]{1,0:T(1,128)S(1)} %get-tuple-element.54.marks_ref, f32[30,2,8,256]{3,2,1,0:T(8,128)S(1)} %collective-permute-done.10.low_ref, ...), custom_call_target="tpu_custom_call" | custom-call | tf_op jit(solution)/shard_map/third_rows/pallas_call | solution.py:793
  106.0 14.4 %all-to-all-start.4 = ((f32[64,1,128]{2,1,0:T(1,128)}), f32[64,1,128]{2,1,0:T(1,128)S(1)}, u32[]{:S(2)}, u32[]{:S(2)}) async-start(f32[64,1,128]{2,1,0:T(1,128)} %get-tuple-element.60), calls=%async_computation.4 | async-start | bytes 65536 | tf_op jit(solution)/shard_map/all_to_all | solution.py:812
  120.3 9.3 %all-to-all-done.4.sums_ref = f32[64,1,128]{2,1,0:T(1,128)S(1)} async-done(((f32[64,1,128]{2,1,0:T(1,128)}), f32[64,1,128]{2,1,0:T(1,128)S(1)}, u32[]{:S(2)}, u32[]{:S(2)}) %all-to-all-start.4) | async-done | bytes 32800 | tf_op jit(solution)/shard_map/all_to_all | solution.py:812
  129.6 1.5 %fourth_rows.1 = (f32[3,2,2,256]{3,2,1,0:T(2,128)}, f32[3,2,2,256]{3,2,1,0:T(2,128)}, s32[1,1]{1,0:T(1,128)}) custom-call(s32[2]{0:T(128)S(1)} %pad_add_fusion.flags_ref, f32[1,128]{1,0:T(1,128)S(1)} %get-tuple-element.54.marks_ref, f32[64,1,128]{2,1,0:T(1,128)S(1)} %all-to-all-done.4.sums_ref, f32[3,4,8,256]{3,2,1,0:T(8,128)S(1)} %get-tuple-element.56.v0_ref, ...), custom_call_target="tpu_custom_call" | custom-call | tf_op jit(solution)/shard_map/fourth_rows/pallas_call | solution.py:793
  (39 shorter events, 0.7 us)
Async XLA Ops:
  0.6 9.1 %copy-start.7 = (f32[32,8]{1,0:T(8,128)S(1)}, f32[32,8]{1,0:T(8,128)}, u32[]{:S(2)}) copy-start(f32[32,8]{1,0:T(8,128)} %constant.52.clone) | copy-start | bytes 3076
  0.6 9.1 %copy-start.8 = (f32[32,8]{1,0:T(8,128)S(1)}, f32[32,8]{1,0:T(8,128)}, u32[]{:S(2)}) copy-start(f32[32,8]{1,0:T(8,128)} %constant.51.clone) | copy-start | bytes 3076
  0.7 10.4 %collective-permute-start.4 = (f32[3,2,2,256]{3,2,1,0:T(2,128)}, f32[3,2,2,256]{3,2,1,0:T(2,128)S(1)}, u32[]{:S(2)}, u32[]{:S(2)}) collective-permute-start(f32[3,2,2,256]{3,2,1,0:T(2,128)} %here_ref.1), channel_id=1, source_target_pairs={{64,0},{128,64},{192,128},{65,1},{129,65},{193,129},{66,2},{130,66... | collective-permute-start | bytes 36872 | tf_op jit(solution)/shard_map/ppermute | solution.py:843
  2.0 9.1 %collective-permute-start.6 = (f32[3,2,2,256]{3,2,1,0:T(2,128)}, f32[3,2,2,256]{3,2,1,0:T(2,128)S(1)}, u32[]{:S(2)}, u32[]{:S(2)}) collective-permute-start(f32[3,2,2,256]{3,2,1,0:T(2,128)} %here_ref.1), channel_id=1, source_target_pairs={{65,0},{66,1},{67,2},{68,3},{69,4},{70,5},{71,6},{72,7},{73,8},{74... | collective-permute-start | bytes 36872 | tf_op jit(solution)/shard_map/ppermute | solution.py:845
  3.3 7.8 %collective-permute-start.5 = (f32[3,2,2,256]{3,2,1,0:T(2,128)}, f32[3,2,2,256]{3,2,1,0:T(2,128)S(1)}, u32[]{:S(2)}, u32[]{:S(2)}) collective-permute-start(f32[3,2,2,256]{3,2,1,0:T(2,128)} %here_ref.1), channel_id=1, source_target_pairs={{1,0},{2,1},{3,2},{4,3},{5,4},{6,5},{7,6},{8,7},{9,8},{10,9},{11,1... | collective-permute-start | bytes 36872 | tf_op jit(solution)/shard_map/ppermute | solution.py:844
  9.7 0.7 copy-start.3
  9.7 0.7 copy-start.5
  9.7 0.7 copy-start.6
  9.8 0.7 copy-start.2
  11.1 12.8 %copy-start.9 = (bf16[1,6,512]{2,1,0:T(8,128)(2,1)S(1)}, bf16[1,6,512]{2,1,0:T(8,128)(2,1)}, u32[]{:S(2)}) copy-start(bf16[1,6,512]{2,1,0:T(8,128)(2,1)} %param.20) | copy-start | bytes 18436
  11.1 22.5 %copy-start = (bf16[1,512,512]{2,1,0:T(8,128)(2,1)S(1)}, bf16[1,512,512]{2,1,0:T(8,128)(2,1)}, u32[]{:S(2)}) copy-start(bf16[1,512,512]{2,1,0:T(8,128)(2,1)} %param.18) | copy-start | bytes 1572868
  11.1 22.5 %copy-start.1 = (bf16[1,512,512]{2,1,0:T(8,128)(2,1)S(1)}, bf16[1,512,512]{2,1,0:T(8,128)(2,1)}, u32[]{:S(2)}) copy-start(bf16[1,512,512]{2,1,0:T(8,128)(2,1)} %param.19) | copy-start | bytes 1572868
  13.1 20.5 %all-to-all-start.2 = ((f32[64,2,128]{2,1,0:T(2,128)}), f32[64,2,128]{2,1,0:T(2,128)S(1)}, u32[]{:S(2)}, u32[]{:S(2)}) async-start(f32[64,2,128]{2,1,0:T(2,128)} %dispatch.1), calls=%async_computation.2 | async-start | bytes 131072 | tf_op jit(solution)/shard_map/all_to_all | solution.py:812
  45.7 15.9 %copy-start.4 = (f32[3,2,2,256]{3,2,1,0:T(2,128)S(1)}, f32[3,2,2,256]{3,2,1,0:T(2,128)}, u32[]{:S(2)}) copy-start(f32[3,2,2,256]{3,2,1,0:T(2,128)} %load_ref.1) | copy-start | bytes 36868
  62.8 8.7 %collective-permute-start.9 = (f32[30,2,2,256]{3,2,1,0:T(2,128)S(1)}, f32[30,2,2,256]{3,2,1,0:T(2,128)S(1)}, u32[]{:S(2)}, u32[]{:S(2)}) collective-permute-start(f32[30,2,2,256]{3,2,1,0:T(2,128)S(1)} %pick.1), channel_id=1, source_target_pairs={{0,64},{64,128},{128,192},{192,0},{1,65},{65,129},{129,193},{193,1... | collective-permute-start | bytes 368648 | tf_op jit(solution)/shard_map/ppermute | solution.py:818
  65.6 9.4 %collective-permute-start.8 = (f32[30,2,2,256]{3,2,1,0:T(2,128)S(1)}, f32[30,2,2,256]{3,2,1,0:T(2,128)S(1)}, u32[]{:S(2)}, u32[]{:S(2)}) collective-permute-start(f32[30,2,2,256]{3,2,1,0:T(2,128)S(1)} %pick.1), channel_id=1, source_target_pairs={{0,128},{64,192},{128,0},{192,64},{1,129},{65,193},{129,1},{193,65... | collective-permute-start | bytes 368648 | tf_op jit(solution)/shard_map/ppermute | solution.py:818
  69.4 5.6 %collective-permute-start.7 = (f32[30,2,2,256]{3,2,1,0:T(2,128)S(1)}, f32[30,2,2,256]{3,2,1,0:T(2,128)S(1)}, u32[]{:S(2)}, u32[]{:S(2)}) collective-permute-start(f32[30,2,2,256]{3,2,1,0:T(2,128)S(1)} %pick.1), channel_id=1, source_target_pairs={{0,192},{64,0},{128,64},{192,128},{1,193},{65,1},{129,65},{193,129... | collective-permute-start | bytes 368648 | tf_op jit(solution)/shard_map/ppermute | solution.py:818
  76.0 11.9 %collective-permute-start.10 = (f32[30,2,8,256]{3,2,1,0:T(8,128)S(1)}, f32[30,2,8,256]{3,2,1,0:T(8,128)S(1)}, u32[]{:S(2)}, u32[]{:S(2)}) collective-permute-start(f32[30,2,8,256]{3,2,1,0:T(8,128)S(1)} %constant_dynamic-slice_fusion.1.own_ref), channel_id=1, source_target_pairs={{0,1},{1,2},{2,3},{3,4},{4,5},{5,6},{6,7},{7,8},{8,9},{9,10},{10,1... | collective-permute-start | bytes 1474568 | tf_op jit(solution)/shard_map/ppermute | solution.py:808
  80.3 7.5 %collective-permute-start.11 = (f32[30,1,8,256]{3,2,1,0:T(8,128)S(1)}, f32[30,1,8,256]{3,2,1,0:T(8,128)S(1)}, u32[]{:S(2)}, u32[]{:S(2)}) collective-permute-start(f32[30,1,8,256]{3,2,1,0:T(8,128)S(1)} %constant_dynamic-slice_fusion), channel_id=1, source_target_pairs={{1,0},{2,1},{3,2},{4,3},{5,4},{6,5},{7,6},{8,7},{9,8},{10,9},{11,1... | collective-permute-start | bytes 737288 | tf_op jit(solution)/shard_map/ppermute | solution.py:808
  88.7 5.6 %collective-permute-start.13 = (f32[3,2,8,256]{3,2,1,0:T(8,128)S(1)}, f32[3,2,8,256]{3,2,1,0:T(8,128)S(1)}, u32[]{:S(2)}, u32[]{:S(2)}) collective-permute-start(f32[3,2,8,256]{3,2,1,0:T(8,128)S(1)} %get-tuple-element.57.v1_ref), channel_id=1, source_target_pairs={{1,0},{2,1},{3,2},{4,3},{5,4},{6,5},{7,6},{8,7},{9,8},{10,9},{11,1... | collective-permute-start | bytes 147464 | tf_op jit(solution)/shard_map/ppermute | solution.py:808
  90.7 4.8 %collective-permute-start.12 = (f32[3,2,8,256]{3,2,1,0:T(8,128)S(1)}, f32[3,2,8,256]{3,2,1,0:T(8,128)S(1)}, u32[]{:S(2)}, u32[]{:S(2)}) collective-permute-start(f32[3,2,8,256]{3,2,1,0:T(8,128)S(1)} %get-tuple-element.57.v1_ref), channel_id=1, source_target_pairs={{0,1},{1,2},{2,3},{3,4},{4,5},{5,6},{6,7},{7,8},{8,9},{9,10},{10,1... | collective-permute-start | bytes 147464 | tf_op jit(solution)/shard_map/ppermute | solution.py:808
  96.7 6.2 %collective-permute-start.15 = (f32[3,2,8,256]{3,2,1,0:T(8,128)S(1)}, f32[3,2,8,256]{3,2,1,0:T(8,128)S(1)}, u32[]{:S(2)}, u32[]{:S(2)}) collective-permute-start(f32[3,2,8,256]{3,2,1,0:T(8,128)S(1)} %get-tuple-element.59.v3_ref), channel_id=1, source_target_pairs={{1,0},{2,1},{3,2},{4,3},{5,4},{6,5},{7,6},{8,7},{9,8},{10,9},{11,1... | collective-permute-start | bytes 147464 | tf_op jit(solution)/shard_map/ppermute | solution.py:808
  98.6 5.4 %collective-permute-start.14 = (f32[3,2,8,256]{3,2,1,0:T(8,128)S(1)}, f32[3,2,8,256]{3,2,1,0:T(8,128)S(1)}, u32[]{:S(2)}, u32[]{:S(2)}) collective-permute-start(f32[3,2,8,256]{3,2,1,0:T(8,128)S(1)} %get-tuple-element.59.v3_ref), channel_id=1, source_target_pairs={{0,1},{1,2},{2,3},{3,4},{4,5},{5,6},{6,7},{7,8},{8,9},{9,10},{10,1... | collective-permute-start | bytes 147464 | tf_op jit(solution)/shard_map/ppermute | solution.py:808
  106.0 23.6 %all-to-all-start.4 = ((f32[64,1,128]{2,1,0:T(1,128)}), f32[64,1,128]{2,1,0:T(1,128)S(1)}, u32[]{:S(2)}, u32[]{:S(2)}) async-start(f32[64,1,128]{2,1,0:T(1,128)} %get-tuple-element.60), calls=%async_computation.4 | async-start | bytes 65536 | tf_op jit(solution)/shard_map/all_to_all | solution.py:812

commit v6 on v5

--- a/solution.py
+++ b/solution.py
@@ -812,16 +812,23 @@
     return lax.all_to_all(block, MICRO, split_axis=0, concat_axis=0, tiled=True)
 
 
-def gather_planes(block):
+def order_kernel(flags_ref, piece_0, piece_1, piece_2, piece_3, own_ref, edge_ref):
+    pieces = [ref[...] for ref in (piece_0, piece_1, piece_2, piece_3)]
+    for turn in range(4):
+
+        @pl.when(flags_ref[1] == 2 * turn)
+        def _():
+            whole = jnp.concatenate([pieces[(k - turn) % 4] for k in range(4)], axis=2)
+            own_ref[...] = whole
+            edge_ref[...] = whole[:, :1]
+
+
+def from_ring(block):
     count = lax.axis_size("macro")
-    pieces = [block] + [
+    return [block] + [
         lax.ppermute(block, "macro", [(k, (k - shift) % count) for k in range(count)])
         for shift in range(1, count)
     ]
-    planes = block.shape[2]
-    twice = jnp.concatenate(pieces + pieces[:-1], axis=2)
-    start = (count - lax.axis_index("macro")) % count * planes
-    return lax.dynamic_slice_in_dim(twice, start, count * planes, axis=2)
 
 
 def shards(
@@ -886,16 +893,22 @@
     (values,) = local_call(
         pick_kernel, ((FIELDS, width, planes, depth),), "pick", swapped(back), place, load
     )
-    own = gather_planes(values)
-    low, high = up_and_down(own, own[:, :1])
     flags = jnp.stack(
         [
             (lax.axis_index(MICRO) == owners - 1).astype(jnp.int32),
             (lax.axis_index("macro") * planes).astype(jnp.int32),
         ]
     )
+    whole = planes * rows_x
+    own, edge = local_call(
+        order_kernel,
+        ((FIELDS, width, whole, depth), (FIELDS, 1, whole, depth)),
+        "order",
+        *from_ring(values),
+        flags=flags,
+    )
+    low, high = up_and_down(own, edge)
     sets = (marks, low, own, high)
-    whole = own.shape[2]
     two = (3, 2, whole, depth)
     four = (3, 4, whole, depth)
     v0, v1 = local_call(first_kernel, (four, two), "first_rows", *sets, flags=flags)

time: 132 us -> 133 us (level)
    pallas_call x7 -> x8, Pallas kernels: 9.38 us -> 10.3 us  [local_call(): pl.pallas_call(kernel, in_specs=specs, out_specs=[pl.BlockSpec(memory_spa...]
  transfers between devices with their start and end apart: 14 -> 14, of which waited for: 7 -> 7; matrix products, arithmetic and copies ran while one was open for 0% -> 1% of each run, Pallas kernels for 0% -> 0%
where the time goes in v6:
time: 133 us; the launch traced here: 132 us
  starting transfers between devices  57.5 us (43%)
  waiting for transfers between devices  31.2 us (23%)
  Pallas kernels  22.4 us (17%)
  blocking collectives  15.9 us (12%)
  between operations  2.97 us (2%)
    all_to_all x2, starting transfers between devices, swapped(): return lax.all_to_all(block, MICRO, split_axis=0, concat_axis=0, tiled=True)  24.4 us
    all_to_all x2, waiting for transfers between devices, swapped(): return lax.all_to_all(block, MICRO, split_axis=0, concat_axis=0, tiled=True)  18.6 us
    all_to_all x1, blocking collectives, swapped(): return lax.all_to_all(block, MICRO, split_axis=0, concat_axis=0, tiled=True)  15.9 us
    ppermute x3, starting transfers between devices, up_and_down(): lax.ppermute(up, MICRO, forward)  12.2 us
    pallas_call x1, Pallas kernels, micro_solve(): pl.pallas_call(micro_kernel, grid=(2,), in_specs=[whole(owners, 2, 128),...  12 us
    pallas_call x8, Pallas kernels, local_call(): pl.pallas_call(kernel, in_specs=specs, out_specs=[pl.BlockSpec(memory_spa...  10.3 us
    ppermute x3, starting transfers between devices, from_ring(): lax.ppermute(block, 'macro', [(k, (k - shift) % count) for k in range(cou...  7.47 us
    ppermute x3, starting transfers between devices, up_and_down(): lax.ppermute(down, MICRO, backward)  5.76 us
  transfers between devices with their start and end apart: 14, of which 7 were waited for; matrix products, arithmetic and copies ran while one was open for 1% of the time, Pallas kernels for 0%

profile of v6, /device:TPU:1, one launch (start us, length us, event | category | flops | bytes accessed | tf_op | source)
XLA Modules:
  0.0 131.8 jit_solution(7004170763162542408)
XLA Ops:
  0.6 1.3 collective-permute-start.4
  1.9 1.3 collective-permute-start.6
  3.2 5.1 %collective-permute-start.5 = (f32[3,2,2,256]{3,2,1,0:T(2,128)}, f32[3,2,2,256]{3,2,1,0:T(2,128)S(1)}, u32[]{:S(2)}, u32[]{:S(2)}) collective-permute-start(f32[3,2,2,256]{3,2,1,0:T(2,128)} %here_ref.1), channel_id=1, source_target_pairs={{1,0},{2,1},{3,2},{4,3},{5,4},{6,5},{7,6},{8,7},{9,8},{10,9},{11,1... | collective-permute-start | bytes 36872 | tf_op jit(solution)/shard_map/ppermute | solution.py:851
  9.7 0.7 multiply_add_fusion.cols_ref
  10.5 0.7 copy-done.2
  11.8 1.9 %dispatch.1 = f32[64,2,128]{2,1,0:T(2,128)} custom-call(s32[8,1024]{1,0:T(8,128)S(1)} %get-tuple-element.50.place_ref, f32[1,1]{1,0:T(1,128)} %get-tuple-element.51.mark_ref, f32[3,2,2,256]{3,2,1,0:T(2,128)S(1)} %get-tuple-element.52.own_ref, f32[3,2,2,256]{3,2,1,0:T(2,128)S(1)} %collective-permute-done.4.right_ref, ...), custom_call_target="tpu_custom_call" | custom-call | tf_op jit(solution)/shard_map/dispatch/pallas_call | solution.py:793
  13.8 10.0 %all-to-all-start.2 = ((f32[64,2,128]{2,1,0:T(2,128)}), f32[64,2,128]{2,1,0:T(2,128)S(1)}, u32[]{:S(2)}, u32[]{:S(2)}) async-start(f32[64,2,128]{2,1,0:T(2,128)} %dispatch.1), calls=%async_computation.2 | async-start | bytes 131072 | tf_op jit(solution)/shard_map/all_to_all | solution.py:812
  24.2 9.4 %all-to-all-done.2.got_ref = f32[64,2,128]{2,1,0:T(2,128)S(1)} async-done(((f32[64,2,128]{2,1,0:T(2,128)}), f32[64,2,128]{2,1,0:T(2,128)S(1)}, u32[]{:S(2)}, u32[]{:S(2)}) %all-to-all-start.2) | async-done | bytes 65568 | tf_op jit(solution)/shard_map/all_to_all | solution.py:812
  33.6 12.0 %micro_solve.1 = (f32[64,8,128]{2,1,0:T(8,128)S(1)}, f32[1,128]{1,0:T(1,128)S(1)}) custom-call(f32[64,2,128]{2,1,0:T(2,128)S(1)} %all-to-all-done.2.got_ref, bf16[512,512]{1,0:T(8,128)(2,1)S(1)} %bitcast.25, bf16[512,512]{1,0:T(8,128)(2,1)S(1)} %bitcast.26, bf16[512,8]{1,0:T(8,128)(2,1)S(1)} %pad_bitcast_fusion.force_ref, ...), custom_call_target="tpu_custom_call" | custom-call | tf_op jit(solution)/shard_map/micro_solve/pallas_call | solution.py:235
  45.7 15.9 %all_to_all.25.back_ref = f32[64,8,128]{2,1,0:T(8,128)S(1)} all-to-all(f32[64,8,128]{2,1,0:T(8,128)S(1)} %get-tuple-element.57), channel_id=1, replica_groups=mesh['macro'=4,'micro_0'=4,'micro_1'=8,'micro_2'=2] {'micro_0','micro_1'..., dimensions={0} | all-to-all | bytes 524288 | tf_op jit(solution)/shard_map/all_to_all | solution.py:812
  61.5 1.3 pick.1.piece_0
  62.8 3.1 %collective-permute-start.9 = (f32[30,2,2,256]{3,2,1,0:T(2,128)S(1)}, f32[30,2,2,256]{3,2,1,0:T(2,128)S(1)}, u32[]{:S(2)}, u32[]{:S(2)}) collective-permute-start(f32[30,2,2,256]{3,2,1,0:T(2,128)S(1)} %pick.1.piece_0), channel_id=1, source_target_pairs={{0,64},{64,128},{128,192},{192,0},{1,65},{65,129},{129,193},{193,1... | collective-permute-start | bytes 368648 | tf_op jit(solution)/shard_map/ppermute | solution.py:829
  65.9 3.5 %collective-permute-start.8 = (f32[30,2,2,256]{3,2,1,0:T(2,128)S(1)}, f32[30,2,2,256]{3,2,1,0:T(2,128)S(1)}, u32[]{:S(2)}, u32[]{:S(2)}) collective-permute-start(f32[30,2,2,256]{3,2,1,0:T(2,128)S(1)} %pick.1.piece_0), channel_id=1, source_target_pairs={{0,128},{64,192},{128,0},{192,64},{1,129},{65,193},{129,1},{193,65... | collective-permute-start | bytes 368648 | tf_op jit(solution)/shard_map/ppermute | solution.py:829
  69.4 0.9 collective-permute-start.7
  70.4 1.2 collective-permute-done.9.piece_3
  71.6 3.5 %collective-permute-done.8.piece_2 = f32[30,2,2,256]{3,2,1,0:T(2,128)S(1)} collective-permute-done((f32[30,2,2,256]{3,2,1,0:T(2,128)S(1)}, f32[30,2,2,256]{3,2,1,0:T(2,128)S(1)}, u32[]{:S(2)}, u32[]{:S(2)}) %collective-permute-start.8) | collective-permute-done | bytes 122912 | tf_op jit(solution)/shard_map/ppermute | solution.py:829
  75.0 0.9 order.1
  76.0 4.3 %collective-permute-start.10 = (f32[30,2,8,256]{3,2,1,0:T(8,128)S(1)}, f32[30,2,8,256]{3,2,1,0:T(8,128)S(1)}, u32[]{:S(2)}, u32[]{:S(2)}) collective-permute-start(f32[30,2,8,256]{3,2,1,0:T(8,128)S(1)} %get-tuple-element.58.own_ref), channel_id=1, source_target_pairs={{0,1},{1,2},{2,3},{3,4},{4,5},{5,6},{6,7},{7,8},{8,9},{9,10},{10,1... | collective-permute-start | bytes 1474568 | tf_op jit(solution)/shard_map/ppermute | solution.py:808
  80.3 1.9 %collective-permute-start.11 = (f32[30,1,8,256]{3,2,1,0:T(8,128)S(1)}, f32[30,1,8,256]{3,2,1,0:T(8,128)S(1)}, u32[]{:S(2)}, u32[]{:S(2)}) collective-permute-start(f32[30,1,8,256]{3,2,1,0:T(8,128)S(1)} %get-tuple-element.59), channel_id=1, source_target_pairs={{1,0},{2,1},{3,2},{4,3},{5,4},{6,5},{7,6},{8,7},{9,8},{10,9},{11,1... | collective-permute-start | bytes 737288 | tf_op jit(solution)/shard_map/ppermute | solution.py:808
  82.2 5.6 %collective-permute-done.11.high_ref = f32[30,1,8,256]{3,2,1,0:T(8,128)S(1)} collective-permute-done((f32[30,1,8,256]{3,2,1,0:T(8,128)S(1)}, f32[30,1,8,256]{3,2,1,0:T(8,128)S(1)}, u32[]{:S(2)}, u32[]{:S(2)}) %collective-permute-start.11) | collective-permute-done | bytes 245792 | tf_op jit(solution)/shard_map/ppermute | solution.py:808
  87.8 0.9 first_rows.1
  88.7 1.9 %collective-permute-start.13 = (f32[3,2,8,256]{3,2,1,0:T(8,128)S(1)}, f32[3,2,8,256]{3,2,1,0:T(8,128)S(1)}, u32[]{:S(2)}, u32[]{:S(2)}) collective-permute-start(f32[3,2,8,256]{3,2,1,0:T(8,128)S(1)} %get-tuple-element.61.v1_ref), channel_id=1, source_target_pairs={{1,0},{2,1},{3,2},{4,3},{5,4},{6,5},{7,6},{8,7},{9,8},{10,9},{11,1... | collective-permute-start | bytes 147464 | tf_op jit(solution)/shard_map/ppermute | solution.py:808
  90.7 3.6 %collective-permute-start.12 = (f32[3,2,8,256]{3,2,1,0:T(8,128)S(1)}, f32[3,2,8,256]{3,2,1,0:T(8,128)S(1)}, u32[]{:S(2)}, u32[]{:S(2)}) collective-permute-start(f32[3,2,8,256]{3,2,1,0:T(8,128)S(1)} %get-tuple-element.61.v1_ref), channel_id=1, source_target_pairs={{0,1},{1,2},{2,3},{3,4},{4,5},{5,6},{6,7},{7,8},{8,9},{9,10},{10,1... | collective-permute-start | bytes 147464 | tf_op jit(solution)/shard_map/ppermute | solution.py:808
  94.3 1.1 collective-permute-done.12.v1_low_ref
  95.5 1.2 second_rows.1
  96.7 1.9 %collective-permute-start.15 = (f32[3,2,8,256]{3,2,1,0:T(8,128)S(1)}, f32[3,2,8,256]{3,2,1,0:T(8,128)S(1)}, u32[]{:S(2)}, u32[]{:S(2)}) collective-permute-start(f32[3,2,8,256]{3,2,1,0:T(8,128)S(1)} %get-tuple-element.63.v3_ref), channel_id=1, source_target_pairs={{1,0},{2,1},{3,2},{4,3},{5,4},{6,5},{7,6},{8,7},{9,8},{10,9},{11,1... | collective-permute-start | bytes 147464 | tf_op jit(solution)/shard_map/ppermute | solution.py:808
  98.6 4.2 %collective-permute-start.14 = (f32[3,2,8,256]{3,2,1,0:T(8,128)S(1)}, f32[3,2,8,256]{3,2,1,0:T(8,128)S(1)}, u32[]{:S(2)}, u32[]{:S(2)}) collective-permute-start(f32[3,2,8,256]{3,2,1,0:T(8,128)S(1)} %get-tuple-element.63.v3_ref), channel_id=1, source_target_pairs={{0,1},{1,2},{2,3},{3,4},{4,5},{5,6},{6,7},{7,8},{8,9},{9,10},{10,1... | collective-permute-start | bytes 147464 | tf_op jit(solution)/shard_map/ppermute | solution.py:808
  102.9 1.1 collective-permute-done.14.v3_low_ref
  104.0 1.9 %third_rows.1 = (f32[3,2,8,256]{3,2,1,0:T(8,128)S(1)}, f32[3,2,8,256]{3,2,1,0:T(8,128)S(1)}, f32[64,1,128]{2,1,0:T(1,128)}) custom-call(s32[2]{0:T(128)S(1)} %pad_add_fusion.flags_ref, f32[1,128]{1,0:T(1,128)S(1)} %get-tuple-element.56.marks_ref, f32[30,2,8,256]{3,2,1,0:T(8,128)S(1)} %collective-permute-done.10.low_ref, ...), custom_call_target="tpu_custom_call" | custom-call | tf_op jit(solution)/shard_map/third_rows/pallas_call | solution.py:793
  106.0 14.4 %all-to-all-start.4 = ((f32[64,1,128]{2,1,0:T(1,128)}), f32[64,1,128]{2,1,0:T(1,128)S(1)}, u32[]{:S(2)}, u32[]{:S(2)}) async-start(f32[64,1,128]{2,1,0:T(1,128)} %get-tuple-element.64), calls=%async_computation.4 | async-start | bytes 65536 | tf_op jit(solution)/shard_map/all_to_all | solution.py:812
  120.3 9.3 %all-to-all-done.4.sums_ref = f32[64,1,128]{2,1,0:T(1,128)S(1)} async-done(((f32[64,1,128]{2,1,0:T(1,128)}), f32[64,1,128]{2,1,0:T(1,128)S(1)}, u32[]{:S(2)}, u32[]{:S(2)}) %all-to-all-start.4) | async-done | bytes 32800 | tf_op jit(solution)/shard_map/all_to_all | solution.py:812
  129.6 1.5 %fourth_rows.1 = (f32[3,2,2,256]{3,2,1,0:T(2,128)}, f32[3,2,2,256]{3,2,1,0:T(2,128)}, s32[1,1]{1,0:T(1,128)}) custom-call(s32[2]{0:T(128)S(1)} %pad_add_fusion.flags_ref, f32[1,128]{1,0:T(1,128)S(1)} %get-tuple-element.56.marks_ref, f32[64,1,128]{2,1,0:T(1,128)S(1)} %all-to-all-done.4.sums_ref, f32[3,4,8,256]{3,2,1,0:T(8,128)S(1)} %get-tuple-element.60.v0_ref, ...), custom_call_target="tpu_custom_call" | custom-call | tf_op jit(solution)/shard_map/fourth_rows/pallas_call | solution.py:793
  (35 shorter events, 1.1 us)
Async XLA Ops:
  0.6 9.1 %copy-start.7 = (f32[32,8]{1,0:T(8,128)S(1)}, f32[32,8]{1,0:T(8,128)}, u32[]{:S(2)}) copy-start(f32[32,8]{1,0:T(8,128)} %constant.37.clone) | copy-start | bytes 3076
  0.6 11.1 %collective-permute-start.4 = (f32[3,2,2,256]{3,2,1,0:T(2,128)}, f32[3,2,2,256]{3,2,1,0:T(2,128)S(1)}, u32[]{:S(2)}, u32[]{:S(2)}) collective-permute-start(f32[3,2,2,256]{3,2,1,0:T(2,128)} %here_ref.1), channel_id=1, source_target_pairs={{64,0},{128,64},{192,128},{65,1},{129,65},{193,129},{66,2},{130,66... | collective-permute-start | bytes 36872 | tf_op jit(solution)/shard_map/ppermute | solution.py:850
  1.9 9.8 %collective-permute-start.6 = (f32[3,2,2,256]{3,2,1,0:T(2,128)}, f32[3,2,2,256]{3,2,1,0:T(2,128)S(1)}, u32[]{:S(2)}, u32[]{:S(2)}) collective-permute-start(f32[3,2,2,256]{3,2,1,0:T(2,128)} %here_ref.1), channel_id=1, source_target_pairs={{65,0},{66,1},{67,2},{68,3},{69,4},{70,5},{71,6},{72,7},{73,8},{74... | collective-permute-start | bytes 36872 | tf_op jit(solution)/shard_map/ppermute | solution.py:852
  3.2 8.5 %collective-permute-start.5 = (f32[3,2,2,256]{3,2,1,0:T(2,128)}, f32[3,2,2,256]{3,2,1,0:T(2,128)S(1)}, u32[]{:S(2)}, u32[]{:S(2)}) collective-permute-start(f32[3,2,2,256]{3,2,1,0:T(2,128)} %here_ref.1), channel_id=1, source_target_pairs={{1,0},{2,1},{3,2},{4,3},{5,4},{6,5},{7,6},{8,7},{9,8},{10,9},{11,1... | collective-permute-start | bytes 36872 | tf_op jit(solution)/shard_map/ppermute | solution.py:851
  9.7 0.8 copy-start.3
  9.7 0.8 copy-start.5
  9.7 0.8 copy-start.6
  10.5 0.7 copy-start.2
  11.8 12.1 %copy-start.8 = (bf16[1,6,512]{2,1,0:T(8,128)(2,1)S(1)}, bf16[1,6,512]{2,1,0:T(8,128)(2,1)}, u32[]{:S(2)}) copy-start(bf16[1,6,512]{2,1,0:T(8,128)(2,1)} %param.20) | copy-start | bytes 18436
  11.8 21.8 %copy-start = (bf16[1,512,512]{2,1,0:T(8,128)(2,1)S(1)}, bf16[1,512,512]{2,1,0:T(8,128)(2,1)}, u32[]{:S(2)}) copy-start(bf16[1,512,512]{2,1,0:T(8,128)(2,1)} %param.18) | copy-start | bytes 1572868
  11.8 21.8 %copy-start.1 = (bf16[1,512,512]{2,1,0:T(8,128)(2,1)S(1)}, bf16[1,512,512]{2,1,0:T(8,128)(2,1)}, u32[]{:S(2)}) copy-start(bf16[1,512,512]{2,1,0:T(8,128)(2,1)} %param.19) | copy-start | bytes 1572868
  13.8 19.8 %all-to-all-start.2 = ((f32[64,2,128]{2,1,0:T(2,128)}), f32[64,2,128]{2,1,0:T(2,128)S(1)}, u32[]{:S(2)}, u32[]{:S(2)}) async-start(f32[64,2,128]{2,1,0:T(2,128)} %dispatch.1), calls=%async_computation.2 | async-start | bytes 131072 | tf_op jit(solution)/shard_map/all_to_all | solution.py:812
  45.6 15.9 %copy-start.4 = (f32[3,2,2,256]{3,2,1,0:T(2,128)S(1)}, f32[3,2,2,256]{3,2,1,0:T(2,128)}, u32[]{:S(2)}) copy-start(f32[3,2,2,256]{3,2,1,0:T(2,128)} %load_ref.1) | copy-start | bytes 36868
  62.8 8.7 %collective-permute-start.9 = (f32[30,2,2,256]{3,2,1,0:T(2,128)S(1)}, f32[30,2,2,256]{3,2,1,0:T(2,128)S(1)}, u32[]{:S(2)}, u32[]{:S(2)}) collective-permute-start(f32[30,2,2,256]{3,2,1,0:T(2,128)S(1)} %pick.1.piece_0), channel_id=1, source_target_pairs={{0,64},{64,128},{128,192},{192,0},{1,65},{65,129},{129,193},{193,1... | collective-permute-start | bytes 368648 | tf_op jit(solution)/shard_map/ppermute | solution.py:829
  65.9 9.2 %collective-permute-start.8 = (f32[30,2,2,256]{3,2,1,0:T(2,128)S(1)}, f32[30,2,2,256]{3,2,1,0:T(2,128)S(1)}, u32[]{:S(2)}, u32[]{:S(2)}) collective-permute-start(f32[30,2,2,256]{3,2,1,0:T(2,128)S(1)} %pick.1.piece_0), channel_id=1, source_target_pairs={{0,128},{64,192},{128,0},{192,64},{1,129},{65,193},{129,1},{193,65... | collective-permute-start | bytes 368648 | tf_op jit(solution)/shard_map/ppermute | solution.py:829
  69.4 5.6 %collective-permute-start.7 = (f32[30,2,2,256]{3,2,1,0:T(2,128)S(1)}, f32[30,2,2,256]{3,2,1,0:T(2,128)S(1)}, u32[]{:S(2)}, u32[]{:S(2)}) collective-permute-start(f32[30,2,2,256]{3,2,1,0:T(2,128)S(1)} %pick.1.piece_0), channel_id=1, source_target_pairs={{0,192},{64,0},{128,64},{192,128},{1,193},{65,1},{129,65},{193,129... | collective-permute-start | bytes 368648 | tf_op jit(solution)/shard_map/ppermute | solution.py:829
  76.0 11.8 %collective-permute-start.10 = (f32[30,2,8,256]{3,2,1,0:T(8,128)S(1)}, f32[30,2,8,256]{3,2,1,0:T(8,128)S(1)}, u32[]{:S(2)}, u32[]{:S(2)}) collective-permute-start(f32[30,2,8,256]{3,2,1,0:T(8,128)S(1)} %get-tuple-element.58.own_ref), channel_id=1, source_target_pairs={{0,1},{1,2},{2,3},{3,4},{4,5},{5,6},{6,7},{7,8},{8,9},{9,10},{10,1... | collective-permute-start | bytes 1474568 | tf_op jit(solution)/shard_map/ppermute | solution.py:808
  80.3 7.5 %collective-permute-start.11 = (f32[30,1,8,256]{3,2,1,0:T(8,128)S(1)}, f32[30,1,8,256]{3,2,1,0:T(8,128)S(1)}, u32[]{:S(2)}, u32[]{:S(2)}) collective-permute-start(f32[30,1,8,256]{3,2,1,0:T(8,128)S(1)} %get-tuple-element.59), channel_id=1, source_target_pairs={{1,0},{2,1},{3,2},{4,3},{5,4},{6,5},{7,6},{8,7},{9,8},{10,9},{11,1... | collective-permute-start | bytes 737288 | tf_op jit(solution)/shard_map/ppermute | solution.py:808
  88.7 5.6 %collective-permute-start.13 = (f32[3,2,8,256]{3,2,1,0:T(8,128)S(1)}, f32[3,2,8,256]{3,2,1,0:T(8,128)S(1)}, u32[]{:S(2)}, u32[]{:S(2)}) collective-permute-start(f32[3,2,8,256]{3,2,1,0:T(8,128)S(1)} %get-tuple-element.61.v1_ref), channel_id=1, source_target_pairs={{1,0},{2,1},{3,2},{4,3},{5,4},{6,5},{7,6},{8,7},{9,8},{10,9},{11,1... | collective-permute-start | bytes 147464 | tf_op jit(solution)/shard_map/ppermute | solution.py:808
  90.7 4.8 %collective-permute-start.12 = (f32[3,2,8,256]{3,2,1,0:T(8,128)S(1)}, f32[3,2,8,256]{3,2,1,0:T(8,128)S(1)}, u32[]{:S(2)}, u32[]{:S(2)}) collective-permute-start(f32[3,2,8,256]{3,2,1,0:T(8,128)S(1)} %get-tuple-element.61.v1_ref), channel_id=1, source_target_pairs={{0,1},{1,2},{2,3},{3,4},{4,5},{5,6},{6,7},{7,8},{8,9},{9,10},{10,1... | collective-permute-start | bytes 147464 | tf_op jit(solution)/shard_map/ppermute | solution.py:808
  96.7 6.2 %collective-permute-start.15 = (f32[3,2,8,256]{3,2,1,0:T(8,128)S(1)}, f32[3,2,8,256]{3,2,1,0:T(8,128)S(1)}, u32[]{:S(2)}, u32[]{:S(2)}) collective-permute-start(f32[3,2,8,256]{3,2,1,0:T(8,128)S(1)} %get-tuple-element.63.v3_ref), channel_id=1, source_target_pairs={{1,0},{2,1},{3,2},{4,3},{5,4},{6,5},{7,6},{8,7},{9,8},{10,9},{11,1... | collective-permute-start | bytes 147464 | tf_op jit(solution)/shard_map/ppermute | solution.py:808
  98.6 5.4 %collective-permute-start.14 = (f32[3,2,8,256]{3,2,1,0:T(8,128)S(1)}, f32[3,2,8,256]{3,2,1,0:T(8,128)S(1)}, u32[]{:S(2)}, u32[]{:S(2)}) collective-permute-start(f32[3,2,8,256]{3,2,1,0:T(8,128)S(1)} %get-tuple-element.63.v3_ref), channel_id=1, source_target_pairs={{0,1},{1,2},{2,3},{3,4},{4,5},{5,6},{6,7},{7,8},{8,9},{9,10},{10,1... | collective-permute-start | bytes 147464 | tf_op jit(solution)/shard_map/ppermute | solution.py:808
  106.0 23.6 %all-to-all-start.4 = ((f32[64,1,128]{2,1,0:T(1,128)}), f32[64,1,128]{2,1,0:T(1,128)S(1)}, u32[]{:S(2)}, u32[]{:S(2)}) async-start(f32[64,1,128]{2,1,0:T(1,128)} %get-tuple-element.64), calls=%async_computation.4 | async-start | bytes 65536 | tf_op jit(solution)/shard_map/all_to_all | solution.py:812
